TPU v7x, 128 devices: a whole 4x4x4 slice. The times are simulated.
128 devices in a mesh: shot: 8 (over x, z_hi), dom: 16 (over z_lo, y, core).
Axes of the slice: x: 4, y: 4, z: 4 (z_hi: 2, z_lo: 2; z = z_hi * 2 + z_lo), core: 2. Of those that a mesh axis runs over, the one named last changes fastest.
Arguments:
- velocity: float32 [512, 32, 128], P('dom'), may hold values from 1.5 to 3
- noise_field: float32 [512, 32, 128], P('dom'), may hold values from -6 to 6
- step_size: float32 [1], replicated, may hold values from 0.05 to 0.5
- field_prev: float32 [16, 512, 32, 128], P('shot', 'dom'), may hold values from -6 to 6
- field_now: float32 [16, 512, 32, 128], P('shot', 'dom'), may hold values from -6 to 6
- adjoint_next: float32 [16, 512, 32, 128], P('shot', 'dom'), may hold values from -6 to 6
- adjoint_now: float32 [16, 512, 32, 128], P('shot', 'dom'), may hold values from -6 to 6
- wavelet: float32 [16, 4], P('shot'), may hold values from -8 to 8
- source_cells: int32 [16, 8], P('shot'), may hold values from 0 to 2097151
- source_signs: int32 [16, 8], P('shot'), may hold values from 0 to 1
- record_cells: int32 [16, 256], P('shot'), may hold values from 0 to 2097151
- observed: float32 [16, 4, 256], P('shot'), may hold values from -6 to 6
Outputs:
- new_velocity: float32 [512, 32, 128], P('dom', None, 'shot')
Inputs may be any that keep to these rules, and one draw needn't show every extreme that they name: `source_signs`: 0 stands for a negative sign, 1 for a positive one. `source_cells`: cells flattened as x 32 * 128 + z * 128 + y. `record_cells`: cells flattened as x 32 * 128 + z * 128 + y.
All inputs are finite; a program needn't handle non-finite values.
Results may differ from a plain program's by a relative error of at most 0.00009.
Values sent between devices are 32-bit elements; how exact they have to be, the bound alone decides.
No kernel may reach another device: no remote copies, remote signals or barrier semaphores. Data moves between devices by JAX's collectives and lax.ppermute only.
A program may use at most 128 MiB of HBM per device.

v0:
```python
import math

import jax
import jax.numpy as jnp
from jax import lax
from jax.sharding import PartitionSpec as P

STEPS = 4


COEFFS = (-205.0 / 72.0, 8.0 / 5.0, -1.0 / 5.0, 8.0 / 315.0, -1.0 / 560.0)
COURANT = 0.02


def extended(block, sides, width):
    for axis, dim in sides:
        count = lax.axis_size(axis)
        forward = [(i, i + 1) for i in range(count - 1)]
        backward = [(target, source) for source, target in forward]
        low = lax.ppermute(
            lax.slice_in_dim(block, block.shape[dim] - width, None, axis=dim), axis, forward
        )
        high = lax.ppermute(lax.slice_in_dim(block, 0, width, axis=dim), axis, backward)
        block = jnp.concatenate([low, block, high], axis=dim)
    return block


def stencil(padded):
    margin = 4
    rank = padded.ndim
    lengths = [padded.shape[rank - 3 + place] - 2 * margin for place in range(3)]

    def window(offsets):
        sliced = padded
        for place in range(3):
            begin = margin + offsets[place]
            sliced = lax.slice_in_dim(sliced, begin, begin + lengths[place], axis=rank - 3 + place)
        return sliced

    summed = 3.0 * COEFFS[0] * window((0, 0, 0))
    for distance in range(1, 5):
        beside_all = window((distance, 0, 0)) + window((-distance, 0, 0))
        beside_all = beside_all + window((0, distance, 0)) + window((0, -distance, 0))
        beside_all = beside_all + window((0, 0, distance)) + window((0, 0, -distance))
        summed = summed + COEFFS[distance] * beside_all
    return summed


def cosine_basis(length):
    wave_index = jnp.arange(length, dtype=jnp.int32)[:, None]
    position = jnp.arange(length, dtype=jnp.int32)[None, :]
    phase = wave_index * (2 * position + 1) % (4 * length)
    angle = math.pi / (2.0 * length) * phase.astype(jnp.float32)
    factor = jnp.where(wave_index == 0, math.sqrt(1.0 / length), math.sqrt(2.0 / length)).astype(
        jnp.float32
    )
    return factor * jnp.cos(angle)


def prior_gain(length, cutoff):
    scaled = jnp.arange(length, dtype=jnp.float32) / float(cutoff)
    return 1.0 / jnp.sqrt(1.0 + scaled)


def precondition(gradient, noise_cols, rate):
    length = gradient.shape[0]
    basis = cosine_basis(length)
    spectrum = prior_gain(length, length // 32)[:, None]
    highest = lax.Precision.HIGHEST
    grad_hat = jnp.dot(basis, gradient.reshape(length, -1), precision=highest)
    noise_hat = jnp.dot(basis, noise_cols.reshape(length, -1), precision=highest)
    weights = spectrum * (-0.5 * rate * spectrum * grad_hat + jnp.sqrt(rate) * noise_hat)
    update = lax.dot_general(basis, weights, (((0,), (0,)), ((), ())), precision=highest)
    return update.reshape(gradient.shape)


def widen(padded):
    return jnp.pad(padded, ((0, 0), (0, 0), (4, 4), (4, 4)))


def body(
    velocity,
    noise_field,
    step_size,
    field_prev,
    field_now,
    adjoint_next,
    adjoint_now,
    wavelet,
    source_cells,
    source_signs,
    record_cells,
    observed,
):
    speed_sq = COURANT * velocity * velocity
    shots_here = field_now.shape[0]
    slab_rows = velocity.shape[0]
    plane_cells = velocity.shape[1] * velocity.shape[2]
    slab_cells = slab_rows * plane_cells
    first_row = lax.axis_index("dom") * slab_rows
    offset = first_row * plane_cells
    row_ids = jnp.arange(shots_here, dtype=jnp.int32)[:, None]
    source_local = source_cells - offset
    source_inside = (source_local >= 0) & (source_local < slab_cells)
    source_target = jnp.where(source_inside, source_local, slab_cells)
    record_local = record_cells - offset
    record_inside = (record_local >= 0) & (record_local < slab_cells)
    record_target = jnp.where(record_inside, record_local, slab_cells)
    record_clip = jnp.clip(record_local, 0, slab_cells - 1)
    amplitude = (2 * source_signs - 1).astype(jnp.float32)

    def place(field, target, values):
        flat = field.reshape(shots_here, -1)
        rows_full = jnp.broadcast_to(row_ids, target.shape)
        return flat.at[rows_full, target].add(values, mode="drop").reshape(field.shape)

    summed = jnp.zeros(field_now.shape, jnp.float32)
    prior, current = (field_prev, field_now)
    laplacians = []
    samples = []
    for moment in range(STEPS):
        padded = extended(current, (("dom", 1),), 4)
        spread = stencil(widen(padded))
        laplacians.append(spread)
        advanced = 2.0 * current - prior + speed_sq * spread
        advanced = place(advanced, source_target, amplitude * wavelet[:, moment][:, None])
        samples.append(jnp.take_along_axis(advanced.reshape(shots_here, -1), record_clip, axis=1))
        prior, current = (current, advanced)
    adj_later, adj_current = (adjoint_next, adjoint_now)
    for moment in range(STEPS, 0, -1):
        misfit = samples[moment - 1] - observed[:, moment - 1, :]
        padded = extended(adj_current, (("dom", 1),), 4)
        spread = stencil(widen(padded))
        earlier = 2.0 * adj_current - adj_later + speed_sq * spread
        earlier = place(earlier, record_target, misfit)
        adj_later, adj_current = (adj_current, earlier)
        summed = summed + adj_current * laplacians[moment - 1]
    partial_value = 2.0 * COURANT * velocity * jnp.sum(summed, axis=0)
    rate = step_size[0]
    shot_rows = velocity.shape[2] // lax.axis_size("shot")
    start = lax.axis_index("shot") * shot_rows
    total = lax.psum(partial_value, "shot")
    grad_cols, noise_cols = (
        lax.all_to_all(total, "dom", split_axis=2, concat_axis=0, tiled=True),
        lax.all_to_all(noise_field, "dom", split_axis=2, concat_axis=0, tiled=True),
    )
    update = precondition(grad_cols, noise_cols, rate)
    returned = lax.all_to_all(update, "dom", split_axis=0, concat_axis=2, tiled=True)
    result = lax.dynamic_slice_in_dim(velocity + returned, start, shot_rows, 2)
    return result


def solution(mesh):
    placed = (
        P("dom", None, None),
        P("dom", None, None),
        P(),
        P("shot", "dom", None, None),
        P("shot", "dom", None, None),
        P("shot", "dom", None, None),
        P("shot", "dom", None, None),
        P("shot", None),
        P("shot", None),
        P("shot", None),
        P("shot", None),
        P("shot", None, None),
    )
    return jax.shard_map(
        body, mesh=mesh, in_specs=placed, out_specs=P("dom", None, "shot"), check_vma=False
    )
```

profile of v0, /device:TPU:1, one launch (start us, length us, event | category | flops | bytes accessed | tf_op | source)
XLA Modules:
  0.0 571.5 jit_solution(9023833268099805198)
XLA Ops:
  7.5 4.6 collective-permute-start.3
  15.7 3.6 collective-permute-start.1
  37.4 8.3 %multiply_add_fusion.3 = (f32[2,32,32,128]{3,2,1,0:T(8,128)}, f32[2,32,32,128]{3,2,1,0:T(8,128)}) fusion(f32[2,32,32,128]{3,2,1,0:T(8,128)} %param.17, f32[2,32,32,128]{3,2,1,0:T(8,128)} %param.18, f32[32,32,128]{2,1,0:T(8,128)} %multiply_multiply_fusion, f32[2,40,40,136]{3,2,1,0:T(8,128)S(1)} %select_maximum_fusion.12, f32[2,36,32,128]{3,2,1,0:T(8,128)} %copy-done.23, ...), kind=kLoop, calls=%fused_computation.293 | loop fusion | flops 8650752 | bytes 29884416 | tf_op jit(solution)/shard_map/add | solution.py:125
  49.7 3.9 collective-permute-start.5
  66.2 22.5 %multiply_add_fusion.2 = (f32[2,32,32,128]{3,2,1,0:T(8,128)}, f32[2,32,32,128]{3,2,1,0:T(8,128)}) fusion(f32[2,32,32,128]{3,2,1,0:T(8,128)} %param.18, f32[2,32,32,128]{3,2,1,0:T(8,128)} %bitcast.179, f32[32,32,128]{2,1,0:T(8,128)} %multiply_multiply_fusion, f32[2,40,40,136]{3,2,1,0:T(8,128)} %select_maximum_fusion.10, ...), kind=kLoop, calls=%fused_computation.292 | loop fusion | flops 8650752 | bytes 29884416 | tf_op jit(solution)/shard_map/add | solution.py:125
  100.9 7.9 %fusion.75 = f32[2,32,32,128]{3,2,1,0:T(8,128)} fusion(f32[2,40,40,136]{3,2,1,0:T(8,128)S(1)} %select_maximum_fusion.14, f32[2,36,32,128]{3,2,1,0:T(8,128)} %copy-done.22, f32[2,36,32,128]{3,2,1,0:T(8,128)} %constant_dynamic-update-slice_fusion, f32[2,32,32,128]{3,2,1,0:T(8,128)S(1)} %copy-done.18, f32[2,32,32,128]{3,2,1,0:T(8,128)} %param.19, ...), kind=kLoop, calls=%fused_computation.263 | loop fusion | flops 8650752 | bytes 28835840 | tf_op jit(solution)/shard_map/add | solution.py:134
  108.8 3.2 copy.112
  112.0 4.8 gather_fusion.3
  126.9 8.2 %multiply_add_fusion.1 = (f32[2,32,32,128]{3,2,1,0:T(8,128)}, f32[2,32,32,128]{3,2,1,0:T(8,128)}) fusion(f32[2,32,32,128]{3,2,1,0:T(8,128)} %bitcast.180, f32[2,32,32,128]{3,2,1,0:T(8,128)} %bitcast.183, f32[32,32,128]{2,1,0:T(8,128)} %multiply_multiply_fusion, f32[2,40,40,136]{3,2,1,0:T(8,128)S(1)} %select_maximum_fusion.8, ...), kind=kLoop, calls=%fused_computation.291 | loop fusion | flops 8650752 | bytes 29884416 | tf_op jit(solution)/shard_map/add | solution.py:125
  142.0 7.1 %gather_fusion.2 = f32[512]{0:T(512)} fusion(f32[2,131072]{1,0:T(2,128)S(1)} %copy-done.16, s32[512]{0:T(512)S(1)} %bitcast.156), kind=kCustom, calls=%fused_computation.2.clone | custom fusion | bytes 8192 | tf_op jit(solution)/shard_map/jit(take_along_axis)/gather | solution.py:127
  149.8 4.8 gather_fusion.1
  165.0 8.2 %multiply_add_fusion = (f32[2,32,32,128]{3,2,1,0:T(8,128)}, f32[2,32,32,128]{3,2,1,0:T(8,128)}) fusion(f32[2,32,32,128]{3,2,1,0:T(8,128)} %bitcast.184, f32[2,32,32,128]{3,2,1,0:T(8,128)} %bitcast.195, f32[32,32,128]{2,1,0:T(8,128)} %multiply_multiply_fusion, f32[2,40,40,136]{3,2,1,0:T(8,128)S(1)} %select_maximum_fusion.6, ...), kind=kLoop, calls=%fused_computation.290 | loop fusion | flops 8650752 | bytes 29884416 | tf_op jit(solution)/shard_map/add | solution.py:125
  176.7 4.8 gather_fusion
  181.7 24.8 %scatter_fusion.4 = f32[2,131072]{1,0:T(2,128)S(1)} fusion(f32[2,131072]{1,0:T(2,128)S(1)} %bitcast.196, s32[512]{0:T(512)S(1)} %bitcast.151, f32[512]{0:T(512)S(1)} %bitcast.224), kind=kCustom, calls=%fused_computation.8 | custom fusion | flops 512 | bytes 10240 | tf_op jit(solution)/shard_map/scatter-add | solution.py:115
  213.2 3.8 collective-permute-done.10
  219.1 7.8 %fusion.33 = f32[2,32,32,128]{3,2,1,0:T(8,128)} fusion(f32[2,40,40,136]{3,2,1,0:T(8,128)S(1)} %select_maximum_fusion.4, f32[2,36,32,128]{3,2,1,0:T(8,128)} %copy-done.26, f32[2,36,32,128]{3,2,1,0:T(8,128)} %constant_dynamic-update-slice_fusion.20, f32[2,32,32,128]{3,2,1,0:T(8,128)S(1)} %bitcast.162, f32[2,32,32,128]{3,2,1,0:T(8,128)} %param.20, ...), kind=kLoop, calls=%fused_computation.121 | loop fusion | flops 8650752 | bytes 28835840 | tf_op jit(solution)/shard_map/add | solution.py:134
  228.9 24.8 %scatter_fusion.5 = f32[2,131072]{1,0:T(2,128)S(1)} fusion(f32[2,131072]{1,0:T(2,128)S(1)} %bitcast.201, s32[512]{0:T(512)S(1)} %bitcast.152, f32[512]{0:T(512)S(1)} %bitcast.222), kind=kCustom, calls=%fused_computation.9 | custom fusion | flops 512 | bytes 10240 | tf_op jit(solution)/shard_map/scatter-add | solution.py:115
  260.9 7.1 %collective-permute-done.12 = f32[2,4,32,128]{3,2,1,0:T(8,128)S(1)} collective-permute-done((f32[2,4,32,128]{3,2,1,0:T(8,128)S(1)}, f32[2,4,32,128]{3,2,1,0:T(8,128)S(1)}, u32[]{:S(2)}, u32[]{:S(2)}) %collective-permute-start.12) | collective-permute-done | bytes 131104 | tf_op jit(solution)/shard_map/ppermute | solution.py:23
  270.2 7.8 %fusion.23 = f32[2,32,32,128]{3,2,1,0:T(8,128)} fusion(f32[2,40,40,136]{3,2,1,0:T(8,128)S(1)} %select_maximum_fusion.2, f32[2,36,32,128]{3,2,1,0:T(8,128)} %copy-done.27, f32[2,36,32,128]{3,2,1,0:T(8,128)} %constant_dynamic-update-slice_fusion.24, f32[2,32,32,128]{3,2,1,0:T(8,128)} %bitcast.168, f32[2,32,32,128]{3,2,1,0:T(8,128)S(1)} %bitcast.163, ...), kind=kLoop, calls=%fused_computation.91 | loop fusion | flops 8650752 | bytes 28835840 | tf_op jit(solution)/shard_map/add | solution.py:134
  280.0 24.8 %scatter_fusion.6 = f32[2,131072]{1,0:T(2,128)S(1)} fusion(f32[2,131072]{1,0:T(2,128)S(1)} %bitcast.203, s32[512]{0:T(512)S(1)} %bitcast.153, f32[512]{0:T(512)S(1)} %bitcast.223), kind=kCustom, calls=%fused_computation.10 | custom fusion | flops 512 | bytes 10240 | tf_op jit(solution)/shard_map/scatter-add | solution.py:115
  311.5 3.7 collective-permute-done.14
  317.4 7.9 %fusion.13 = f32[2,32,32,128]{3,2,1,0:T(8,128)} fusion(f32[2,40,40,136]{3,2,1,0:T(8,128)S(1)} %select_maximum_fusion, f32[2,36,32,128]{3,2,1,0:T(8,128)} %copy-done.28, f32[2,36,32,128]{3,2,1,0:T(8,128)} %constant_dynamic-update-slice_fusion.28, f32[2,32,32,128]{3,2,1,0:T(8,128)} %bitcast.174, f32[2,32,32,128]{3,2,1,0:T(8,128)S(1)} %bitcast.169, ...), kind=kLoop, calls=%fused_computation.61 | loop fusion | flops 8650752 | bytes 28835840 | tf_op jit(solution)/shard_map/add | solution.py:134
  328.3 66.7 %scatter_fusion.7 = f32[2,131072]{1,0:T(2,128)} fusion(f32[2,131072]{1,0:T(2,128)} %bitcast.199, s32[512]{0:T(512)S(1)} %bitcast.154, f32[512]{0:T(512)S(1)} %bitcast.221), kind=kCustom, calls=%fused_computation.11 | custom fusion | flops 512 | bytes 10240 | tf_op jit(solution)/shard_map/scatter-add | solution.py:115
  396.4 3.3 add_reduce_fusion
  405.2 11.2 %all-to-all-start.1 = ((f32[16,1,8192]{2,1,0:T(1,128)}), f32[16,1,8192]{2,1,0:T(1,128)S(1)}, u32[]{:S(2)}, u32[]{:S(2)}) async-start(f32[16,1,8192]{2,1,0:T(1,128)} %reshape.253), calls=%async_computation.1 | async-start | bytes 1048576 | tf_op jit(solution)/shard_map/all_to_all | solution.py:145
  416.5 78.1 %all-reduce.10.cloned.1.call-done = f32[32,32,128]{2,1,0:T(8,128)} async-done(((f32[32,32,128]{2,1,0:T(8,128)}), f32[32,32,128]{2,1,0:T(8,128)}) %all-reduce.10.cloned.1.call-update) | async-done | bytes 524304 | tf_op jit(solution)/shard_map/psum | solution.py:142
  499.2 10.7 %all-to-all-start = ((f32[16,1,8192]{2,1,0:T(1,128)}), f32[16,1,8192]{2,1,0:T(1,128)}, u32[]{:S(2)}, u32[]{:S(2)}) async-start(f32[16,1,8192]{2,1,0:T(1,128)} %reshape.255), calls=%async_computation | async-start | bytes 1048576 | tf_op jit(solution)/shard_map/all_to_all | solution.py:144
  518.7 4.8 convolution_multiply_fusion
  532.4 4.8 fusion.4
  537.3 5.1 convolution_bitcast_fusion
  544.9 6.0 %all-to-all-start.2 = ((f32[16,1,8192]{2,1,0:T(1,128)}), f32[16,1,8192]{2,1,0:T(1,128)S(1)}, u32[]{:S(2)}, u32[]{:S(2)}) async-start(f32[16,1,8192]{2,1,0:T(1,128)} %reshape.257), calls=%async_computation.2 | async-start | bytes 1048576 | tf_op jit(solution)/shard_map/all_to_all | solution.py:148
  551.3 9.5 %all-to-all-done.2 = f32[16,1,8192]{2,1,0:T(1,128)S(1)} async-done(((f32[16,1,8192]{2,1,0:T(1,128)}), f32[16,1,8192]{2,1,0:T(1,128)S(1)}, u32[]{:S(2)}, u32[]{:S(2)}) %all-to-all-start.2) | async-done | bytes 524320 | tf_op jit(solution)/shard_map/all_to_all | solution.py:148
  (218 shorter events, 151.3 us)
Async XLA Ops:
  6.5 488.0 %all-reduce.10.cloned.1.call-start = ((), (), s32[]{:S(2)}) async-start(), calls=%async_computation.3 | async-start | bytes 1048576 | tf_op jit(solution)/shard_map/psum | solution.py:142
  7.5 22.4 %collective-permute-start.3 = (f32[2,4,32,128]{3,2,1,0:T(8,128)S(1)}, f32[2,4,32,128]{3,2,1,0:T(8,128)S(1)}, u32[]{:S(2)}, u32[]{:S(2)}) collective-permute-start(f32[2,4,32,128]{3,2,1,0:T(8,128)S(1)} %get-tuple-element.46), channel_id=1, source_target_pairs={{0,1},{1,2},{2,3},{3,4},{4,5},{5,6},{6,7},{7,8},{8,9},{9,10},{10,1... | collective-permute-start | bytes 393224 | tf_op jit(solution)/shard_map/ppermute | solution.py:20
  12.1 21.3 %collective-permute-start.2 = (f32[2,4,32,128]{3,2,1,0:T(8,128)S(1)}, f32[2,4,32,128]{3,2,1,0:T(8,128)}, u32[]{:S(2)}, u32[]{:S(2)}) collective-permute-start(f32[2,4,32,128]{3,2,1,0:T(8,128)S(1)} %get-tuple-element.47), channel_id=1, source_target_pairs={{1,0},{2,1},{3,2},{4,3},{5,4},{6,5},{7,6},{8,7},{9,8},{10,9},{11,1... | collective-permute-start | bytes 393224 | tf_op jit(solution)/shard_map/ppermute | solution.py:23
  15.7 40.3 %collective-permute-start.1 = (f32[2,4,32,128]{3,2,1,0:T(8,128)}, f32[2,4,32,128]{3,2,1,0:T(8,128)S(1)}, u32[]{:S(2)}, u32[]{:S(2)}) collective-permute-start(f32[2,4,32,128]{3,2,1,0:T(8,128)} %get-tuple-element.50), channel_id=1, source_target_pairs={{0,1},{1,2},{2,3},{3,4},{4,5},{5,6},{6,7},{7,8},{8,9},{9,10},{10,1... | collective-permute-start | bytes 393224 | tf_op jit(solution)/shard_map/ppermute | solution.py:20
  19.4 36.7 %collective-permute-start = (f32[2,4,32,128]{3,2,1,0:T(8,128)}, f32[2,4,32,128]{3,2,1,0:T(8,128)S(1)}, u32[]{:S(2)}, u32[]{:S(2)}) collective-permute-start(f32[2,4,32,128]{3,2,1,0:T(8,128)} %get-tuple-element.51), channel_id=1, source_target_pairs={{1,0},{2,1},{3,2},{4,3},{5,4},{6,5},{7,6},{8,7},{9,8},{10,9},{11,1... | collective-permute-start | bytes 393224 | tf_op jit(solution)/shard_map/ppermute | solution.py:23
  49.7 13.3 %copy-start.11 = (f32[1,2,1024,128]{3,2,1,0:T(8,128)}, f32[1,2,1024,128]{3,2,1,0:T(8,128)S(1)}, u32[]{:S(2)}) copy-start(f32[1,2,1024,128]{3,2,1,0:T(8,128)S(1)} %copy.61) | copy-start | bytes 3145732
  49.7 10.9 %collective-permute-start.5 = (f32[2,4,32,128]{3,2,1,0:T(8,128)S(1)}, f32[2,4,32,128]{3,2,1,0:T(8,128)S(1)}, u32[]{:S(2)}, u32[]{:S(2)}) collective-permute-start(f32[2,4,32,128]{3,2,1,0:T(8,128)S(1)} %get-tuple-element.42), channel_id=1, source_target_pairs={{0,1},{1,2},{2,3},{3,4},{4,5},{5,6},{6,7},{7,8},{8,9},{9,10},{10,1... | collective-permute-start | bytes 393224 | tf_op jit(solution)/shard_map/ppermute | solution.py:20
  53.6 9.3 %collective-permute-start.4 = (f32[2,4,32,128]{3,2,1,0:T(8,128)S(1)}, f32[2,4,32,128]{3,2,1,0:T(8,128)S(1)}, u32[]{:S(2)}, u32[]{:S(2)}) collective-permute-start(f32[2,4,32,128]{3,2,1,0:T(8,128)S(1)} %get-tuple-element.43), channel_id=1, source_target_pairs={{1,0},{2,1},{3,2},{4,3},{5,4},{6,5},{7,6},{8,7},{9,8},{10,9},{11,1... | collective-permute-start | bytes 393224 | tf_op jit(solution)/shard_map/ppermute | solution.py:23
  97.7 21.8 %collective-permute-start.7 = (f32[2,4,32,128]{3,2,1,0:T(8,128)}, f32[2,4,32,128]{3,2,1,0:T(8,128)S(1)}, u32[]{:S(2)}, u32[]{:S(2)}) collective-permute-start(f32[2,4,32,128]{3,2,1,0:T(8,128)} %get-tuple-element.38), channel_id=1, source_target_pairs={{0,1},{1,2},{2,3},{3,4},{4,5},{5,6},{6,7},{7,8},{8,9},{9,10},{10,1... | collective-permute-start | bytes 393224 | tf_op jit(solution)/shard_map/ppermute | solution.py:20
  108.8 10.8 %copy-start.13 = (f32[1,2,1024,128]{3,2,1,0:T(8,128)S(1)}, f32[1,2,1024,128]{3,2,1,0:T(8,128)}, u32[]{:S(2)}) copy-start(f32[1,2,1024,128]{3,2,1,0:T(8,128)} %copy-done.12) | copy-start | bytes 3145732
  117.4 6.3 %collective-permute-start.6 = (f32[2,4,32,128]{3,2,1,0:T(8,128)S(1)}, f32[2,4,32,128]{3,2,1,0:T(8,128)S(1)}, u32[]{:S(2)}, u32[]{:S(2)}) collective-permute-start(f32[2,4,32,128]{3,2,1,0:T(8,128)S(1)} %get-tuple-element.39), channel_id=1, source_target_pairs={{1,0},{2,1},{3,2},{4,3},{5,4},{6,5},{7,6},{8,7},{9,8},{10,9},{11,1... | collective-permute-start | bytes 393224 | tf_op jit(solution)/shard_map/ppermute | solution.py:23
  138.7 20.3 %copy-start.20 = (f32[1,2,1024,128]{3,2,1,0:T(8,128)}, f32[1,2,1024,128]{3,2,1,0:T(8,128)S(1)}, u32[]{:S(2)}) copy-start(f32[1,2,1024,128]{3,2,1,0:T(8,128)S(1)} %copy.65) | copy-start | bytes 3145732
  138.7 19.1 %collective-permute-start.9 = (f32[2,4,32,128]{3,2,1,0:T(8,128)S(1)}, f32[2,4,32,128]{3,2,1,0:T(8,128)S(1)}, u32[]{:S(2)}, u32[]{:S(2)}) collective-permute-start(f32[2,4,32,128]{3,2,1,0:T(8,128)S(1)} %get-tuple-element.34), channel_id=1, source_target_pairs={{0,1},{1,2},{2,3},{3,4},{4,5},{5,6},{6,7},{7,8},{8,9},{9,10},{10,1... | collective-permute-start | bytes 393224 | tf_op jit(solution)/shard_map/ppermute | solution.py:20
  155.2 6.6 %collective-permute-start.8 = (f32[2,4,32,128]{3,2,1,0:T(8,128)S(1)}, f32[2,4,32,128]{3,2,1,0:T(8,128)S(1)}, u32[]{:S(2)}, u32[]{:S(2)}) collective-permute-start(f32[2,4,32,128]{3,2,1,0:T(8,128)S(1)} %get-tuple-element.35), channel_id=1, source_target_pairs={{1,0},{2,1},{3,2},{4,3},{5,4},{6,5},{7,6},{8,7},{9,8},{10,9},{11,1... | collective-permute-start | bytes 393224 | tf_op jit(solution)/shard_map/ppermute | solution.py:23
  206.5 12.5 %copy-start.3 = (f32[1,2,1024,128]{3,2,1,0:T(8,128)}, f32[1,2,1024,128]{3,2,1,0:T(8,128)S(1)}, u32[]{:S(2)}) copy-start(f32[1,2,1024,128]{3,2,1,0:T(8,128)S(1)} %copy.69) | copy-start | bytes 3145732
  206.6 4.4 collective-permute-start.11
  208.5 8.4 %collective-permute-start.10 = (f32[2,4,32,128]{3,2,1,0:T(8,128)S(1)}, f32[2,4,32,128]{3,2,1,0:T(8,128)S(1)}, u32[]{:S(2)}, u32[]{:S(2)}) collective-permute-start(f32[2,4,32,128]{3,2,1,0:T(8,128)S(1)} %get-tuple-element.31), channel_id=1, source_target_pairs={{1,0},{2,1},{3,2},{4,3},{5,4},{6,5},{7,6},{8,7},{9,8},{10,9},{11,1... | collective-permute-start | bytes 393224 | tf_op jit(solution)/shard_map/ppermute | solution.py:23
  253.8 15.7 %copy-start.6 = (f32[1,2,1024,128]{3,2,1,0:T(8,128)}, f32[1,2,1024,128]{3,2,1,0:T(8,128)S(1)}, u32[]{:S(2)}) copy-start(f32[1,2,1024,128]{3,2,1,0:T(8,128)S(1)} %copy.72) | copy-start | bytes 3145732
  253.8 4.8 collective-permute-start.13
  255.8 12.3 %collective-permute-start.12 = (f32[2,4,32,128]{3,2,1,0:T(8,128)S(1)}, f32[2,4,32,128]{3,2,1,0:T(8,128)S(1)}, u32[]{:S(2)}, u32[]{:S(2)}) collective-permute-start(f32[2,4,32,128]{3,2,1,0:T(8,128)S(1)} %get-tuple-element.27), channel_id=1, source_target_pairs={{1,0},{2,1},{3,2},{4,3},{5,4},{6,5},{7,6},{8,7},{9,8},{10,9},{11,1... | collective-permute-start | bytes 393224 | tf_op jit(solution)/shard_map/ppermute | solution.py:23
  258.7 11.5 %copy-start.1 = (f32[32,32,128]{2,1,0:T(8,128)S(1)}, f32[32,32,128]{2,1,0:T(8,128)}, u32[]{:S(2)}) copy-start(f32[32,32,128]{2,1,0:T(8,128)} %multiply_multiply_fusion) | copy-start | bytes 1572868
  258.7 11.5 %copy-start.4 = (f32[1,2,1024,128]{3,2,1,0:T(8,128)S(1)}, f32[1,2,1024,128]{3,2,1,0:T(8,128)}, u32[]{:S(2)}) copy-start(f32[1,2,1024,128]{3,2,1,0:T(8,128)} %copy-done.3) | copy-start | bytes 3145732
  280.0 26.9 %copy-start.33 = (f32[1,2,2,128]{3,2,1,0:T(2,128)S(1)}, f32[1,2,2,128]{3,2,1,0:T(2,128)}, u32[]{:S(2)}) copy-start(f32[1,2,2,128]{3,2,1,0:T(2,128)} %get-tuple-element.10) | copy-start | bytes 6148
  304.9 11.9 %copy-start.9 = (f32[1,2,1024,128]{3,2,1,0:T(8,128)}, f32[1,2,1024,128]{3,2,1,0:T(8,128)S(1)}, u32[]{:S(2)}) copy-start(f32[1,2,1024,128]{3,2,1,0:T(8,128)S(1)} %copy.75) | copy-start | bytes 3145732
  304.9 4.4 collective-permute-start.15
  307.0 8.3 %collective-permute-start.14 = (f32[2,4,32,128]{3,2,1,0:T(8,128)S(1)}, f32[2,4,32,128]{3,2,1,0:T(8,128)S(1)}, u32[]{:S(2)}, u32[]{:S(2)}) collective-permute-start(f32[2,4,32,128]{3,2,1,0:T(8,128)S(1)} %get-tuple-element.23), channel_id=1, source_target_pairs={{1,0},{2,1},{3,2},{4,3},{5,4},{6,5},{7,6},{8,7},{9,8},{10,9},{11,1... | collective-permute-start | bytes 393224 | tf_op jit(solution)/shard_map/ppermute | solution.py:23
  328.3 68.0 %copy-start.5 = (f32[1,2,1024,128]{3,2,1,0:T(8,128)S(1)}, f32[1,2,1024,128]{3,2,1,0:T(8,128)}, u32[]{:S(2)}) copy-start(f32[1,2,1024,128]{3,2,1,0:T(8,128)} %copy-done.3) | copy-start | bytes 3145732
  328.3 68.0 %copy-start.8 = (f32[1,2,1024,128]{3,2,1,0:T(8,128)S(1)}, f32[1,2,1024,128]{3,2,1,0:T(8,128)}, u32[]{:S(2)}) copy-start(f32[1,2,1024,128]{3,2,1,0:T(8,128)} %copy-done.6) | copy-start | bytes 3145732
  328.3 68.0 %copy-start.10 = (f32[1,2,1024,128]{3,2,1,0:T(8,128)S(1)}, f32[1,2,1024,128]{3,2,1,0:T(8,128)}, u32[]{:S(2)}) copy-start(f32[1,2,1024,128]{3,2,1,0:T(8,128)} %copy-done.9) | copy-start | bytes 3145732
  405.2 93.9 %all-to-all-start.1 = ((f32[16,1,8192]{2,1,0:T(1,128)}), f32[16,1,8192]{2,1,0:T(1,128)S(1)}, u32[]{:S(2)}, u32[]{:S(2)}) async-start(f32[16,1,8192]{2,1,0:T(1,128)} %reshape.253), calls=%async_computation.1 | async-start | bytes 1048576 | tf_op jit(solution)/shard_map/all_to_all | solution.py:145
  499.2 24.4 %all-to-all-start = ((f32[16,1,8192]{2,1,0:T(1,128)}), f32[16,1,8192]{2,1,0:T(1,128)}, u32[]{:S(2)}, u32[]{:S(2)}) async-start(f32[16,1,8192]{2,1,0:T(1,128)} %reshape.255), calls=%async_computation | async-start | bytes 1048576 | tf_op jit(solution)/shard_map/all_to_all | solution.py:144
  544.9 15.9 %all-to-all-start.2 = ((f32[16,1,8192]{2,1,0:T(1,128)}), f32[16,1,8192]{2,1,0:T(1,128)S(1)}, u32[]{:S(2)}, u32[]{:S(2)}) async-start(f32[16,1,8192]{2,1,0:T(1,128)} %reshape.257), calls=%async_computation.2 | async-start | bytes 1048576 | tf_op jit(solution)/shard_map/all_to_all | solution.py:148
  (29 other events, 168.0 us)
Sparse Core Ops, SparseCore 0:
  400.8 93.7 all-reduce.9
where the time goes:
time: 579 us; the launch traced here: 571 us
  other arithmetic  261 us (45%)
  waiting for transfers between devices  106 us (18%)
  local copies, waits for them, and re-layouts  105 us (18%)
  starting transfers between devices  69.5 us (12%)
  between operations  15.4 us (3%)
  matrix products  14.7 us (3%)
    scatter-add x8, other arithmetic, place(): flat.at[rows_full, target].add(values, mode='drop').reshape(field.shape)  149 us
    psum x1, waiting for transfers between devices, body(): total = lax.psum(partial_value, 'shot')  78.1 us
    unnamed x127, local copies, waits for them, and re-layouts  52 us
    add x4, other arithmetic, body(): advanced = 2.0 * current - prior + speed_sq * spread  47.2 us
    add x4, other arithmetic, body(): earlier = 2.0 * adj_current - adj_later + speed_sq * spread  31.4 us
    gather x8, local copies, waits for them, and re-layouts, body(): jnp.take_along_axis(advanced.reshape(shots_here, -1), record_clip, axis=1)  23.5 us
    ppermute x8, starting transfers between devices, extended(): lax.ppermute(lax.slice_in_dim(block, block.shape[dim] - width, None, axis...  23 us
    ppermute x8, starting transfers between devices, extended(): lax.ppermute(lax.slice_in_dim(block, 0, width, axis=dim), axis, backward)  18.6 us
  transfers between devices with their start and end apart: 20, of which 7 were waited for; matrix products, arithmetic and copies ran while one was open for 17% of the time, Pallas kernels for 0%

commit v1 on v0

v1 whole, which is shorter than its diff:
```python
import math

import jax
import jax.numpy as jnp
import ml_dtypes
import numpy as np
from jax import lax
from jax.experimental import pallas as pl
from jax.experimental.pallas import tpu as pltpu
from jax.sharding import PartitionSpec as P

STEPS = 4
COEFFS = (-205.0 / 72.0, 8.0 / 5.0, -1.0 / 5.0, 8.0 / 315.0, -1.0 / 560.0)
COURANT = 0.02
CUTOFF = 16

NX, NZ, NY = 512, 32, 128
SLAB = 32
DEEP = 16
SHALLOW = 12
ROWS = SLAB + 2 * DEEP
PAD = 8
DEPTH = NZ + 2 * PAD
SHOTS_HERE = 2
NREC = 256
LIST = NREC + 8
CHUNK = 8
VMEM_LIMIT = 56 * 1024 * 1024

ANY = pl.BlockSpec(memory_space=pl.ANY)
VMEM = pl.BlockSpec(memory_space=pltpu.VMEM)
SMEM = pl.BlockSpec(memory_space=pltpu.SMEM)


def split_host(matrix):
    high = matrix.astype(ml_dtypes.bfloat16)
    low = (matrix - high.astype(np.float64)).astype(ml_dtypes.bfloat16)
    return high, low


def lane_operator():
    band = np.zeros((NY, NY))
    np.fill_diagonal(band, 3.0 * COEFFS[0])
    for distance in range(1, 5):
        band += COEFFS[distance] * (np.eye(NY, k=distance) + np.eye(NY, k=-distance))
    high, low = split_host(band)
    zero = np.zeros_like(low)
    return np.block([[high, low], [high, zero]])


def prior_operators():
    wave = np.arange(NX)[:, None]
    position = np.arange(NX)[None, :]
    factor = np.where(wave == 0, math.sqrt(1.0 / NX), math.sqrt(2.0 / NX))
    basis = factor * np.cos(math.pi / (2.0 * NX) * (wave * (2 * position + 1) % (4 * NX)))
    gain = 1.0 / np.sqrt(1.0 + np.arange(NX) / CUTOFF)
    squared = basis.T @ (gain[:, None] ** 2 * basis)
    single = basis.T @ (gain[:, None] * basis)
    return np.stack([*split_host(squared), *split_host(single)])


def split(values):
    high = values.astype(jnp.bfloat16)
    low = (values - high.astype(jnp.float32)).astype(jnp.bfloat16)
    return high, low


def dot(left, right):
    return jnp.dot(left, right, preferred_element_type=jnp.float32)


def prepare_kernel(rec, row_out, lane_out, index_out, count_out):
    base = (lax.axis_index("dom") * SLAB - DEEP) * (NZ * NY)
    first = (DEEP - SHALLOW) * NZ * NY
    last = (DEEP + SLAB + SHALLOW) * NZ * NY
    for shot in range(SHOTS_HERE):

        def gather(item, count, shot=shot):
            cell = rec[shot, item] - base
            inside = (cell >= first) & (cell < last)
            row_out[shot, count] = cell >> 7
            lane_out[shot, count] = cell & 127
            index_out[shot, count] = item
            return count + inside.astype(jnp.int32)

        count = lax.fori_loop(0, NREC, gather, jnp.int32(0), unroll=8)
        for extra in range(4):
            row_out[shot, count + extra] = DEEP * NZ
            lane_out[shot, count + extra] = -1
            index_out[shot, count + extra] = 0
        count_out[shot] = (count + 3) >> 2


def clear_pads(fields, number):
    zeros = jnp.zeros((ROWS, PAD, NY), jnp.float32)
    for field in range(1, number):
        for shot in range(SHOTS_HERE):
            fields[field, shot, :, 0:PAD, :] = zeros
            fields[field, shot, :, PAD + NZ : DEPTH, :] = zeros


def load_field(fields, field, own, low, high, offset, width, sems, base):
    copies = []
    begin = DEEP - width
    for shot in range(SHOTS_HERE):
        planes = pl.ds(offset + shot * width, width)
        view = fields.at[field, shot]
        for number, (source, target) in enumerate(
            (
                (low.at[planes], view.at[pl.ds(begin, width), pl.ds(PAD, NZ), :]),
                (own.at[shot], view.at[pl.ds(DEEP, SLAB), pl.ds(PAD, NZ), :]),
                (high.at[planes], view.at[pl.ds(DEEP + SLAB, width), pl.ds(PAD, NZ), :]),
            )
        ):
            copies.append(pltpu.make_async_copy(source, target, sems.at[base + shot * 3 + number]))
    return copies


def load_speed(speed, own, low, high, offset, sems, base):
    planes = pl.ds(offset, SHALLOW)
    return [
        pltpu.make_async_copy(low.at[planes], speed.at[pl.ds(DEEP - SHALLOW, SHALLOW)], sems.at[base]),
        pltpu.make_async_copy(own, speed.at[pl.ds(DEEP, SLAB)], sems.at[base + 1]),
        pltpu.make_async_copy(high.at[planes], speed.at[pl.ds(DEEP + SLAB, SHALLOW)], sems.at[base + 2]),
    ]


def square_speed(speed):
    @pl.loop(0, (SLAB + 2 * SHALLOW) // 8)
    def _(part):
        rows = pl.ds(DEEP - SHALLOW + part * 8, 8)
        value = speed[rows]
        speed[rows] = COURANT * value * value


def leap(fields, speed, lanes, source, margin, laplacians=None, slot=None):
    first = DEEP - margin
    chunks = (SLAB + 2 * margin) // CHUNK

    @pl.loop(0, SHOTS_HERE * chunks)
    def _(item):
        shot = item // chunks
        begin = first + (item % chunks) * CHUNK
        block = fields[source, shot, pl.ds(begin, CHUNK), PAD : PAD + NZ, :].reshape(CHUNK * NZ, NY)
        along = dot(jnp.concatenate(split(block), axis=1), lanes[...])
        for plane in range(CHUNK):
            here = begin + plane
            part = along[plane * NZ : (plane + 1) * NZ]
            spread = part[:, :NY] + part[:, NY:]
            for distance in range(1, 5):
                beside = (
                    fields[source, shot, here + distance, PAD : PAD + NZ, :]
                    + fields[source, shot, here - distance, PAD : PAD + NZ, :]
                ) + (
                    fields[source, shot, here, PAD + distance : PAD + NZ + distance, :]
                    + fields[source, shot, here, PAD - distance : PAD + NZ - distance, :]
                )
                spread = spread + COEFFS[distance] * beside
            centre = fields[source, shot, here, PAD : PAD + NZ, :]
            before = fields[source - 1, shot, here, PAD : PAD + NZ, :]
            fields[source + 1, shot, here, PAD : PAD + NZ, :] = (
                2.0 * centre - before + speed[here] * spread
            )
            if laplacians is not None:
                laplacians[slot, shot, here] = spread


def lane_ids():
    return lax.broadcasted_iota(jnp.int32, (1, NY), 1)


def forward_kernel(
    rows, lanes_of, index, counts, src, signs, wave,
    now, prev, vel, low, high, lanes,
    lap_out, samples,
    fields, laps, speed, sems, out_sems,
):
    copies = load_field(fields, 1, now, low, high, 0, DEEP, sems, 0)
    copies += load_field(fields, 0, prev, low, high, 2 * DEEP, SHALLOW, sems, 6)
    copies += load_speed(speed, vel, low, high, 2 * DEEP + 2 * SHALLOW, sems, 12)
    for copy in copies:
        copy.start()
    clear_pads(fields, 5)
    for copy in copies:
        copy.wait()
    square_speed(speed)
    base = (lax.axis_index("dom") * SLAB - DEEP) * (NZ * NY)
    ids = lane_ids()
    outs = []
    for moment in range(STEPS):
        margin = 4 * (STEPS - 1 - moment)
        leap(fields, speed, lanes, moment + 1, margin, laps, moment)
        out = pltpu.make_async_copy(laps.at[moment, :, pl.ds(DEEP, SLAB)], lap_out.at[moment], out_sems.at[moment])
        out.start()
        outs.append(out)
        first = (DEEP - margin) * NZ * NY
        last = (DEEP + SLAB + margin) * NZ * NY
        for shot in range(SHOTS_HERE):

            @pl.loop(0, src.shape[1])
            def _(item, shot=shot):
                cell = src[shot, item] - base

                @pl.when((cell >= first) & (cell < last))
                def _():
                    amplitude = (2 * signs[shot, item] - 1).astype(jnp.float32) * wave[shot, moment]
                    plane = cell >> 12
                    depth = PAD + ((cell >> 7) & (NZ - 1))
                    view = fields.at[moment + 2, shot, plane, pl.ds(depth, 1), :]
                    view[...] = view[...] + jnp.where(ids == (cell & 127), amplitude, 0.0)

    for shot in range(SHOTS_HERE):

        def sample(group, state, shot=shot):
            state = list(state)
            for member in range(4):
                item = group * 4 + member
                row, lane, which = rows[shot, item], lanes_of[shot, item], index[shot, item]
                plane = row >> 5
                depth = PAD + (row & (NZ - 1))
                own = (lane >= 0) & (plane >= DEEP) & (plane < DEEP + SLAB)
                shift = (which - lane) & 127
                for half in range(2):
                    hit = ids == jnp.where(own, which - half * NY, -1)
                    for moment in range(STEPS):
                        line = fields[moment + 2, shot, plane, pl.ds(depth, 1), :]
                        line = pltpu.roll(line, shift, 1)
                        state[moment * 2 + half] = jnp.where(hit, line, state[moment * 2 + half])
            return tuple(state)

        zero = jnp.zeros((1, NY), jnp.float32)
        state = lax.fori_loop(0, counts[shot], sample, (zero,) * (2 * STEPS))
        for moment in range(STEPS):
            for half in range(2):
                line = shot * STEPS + moment
                samples[line : line + 1, half * NY : (half + 1) * NY] = state[moment * 2 + half]
    for out in outs:
        out.wait()


def adjoint_kernel(
    rows, lanes_of, index, counts, misfit,
    now, after, vel, low, high, vel_low, vel_high, laps_in, lanes,
    tiles,
    fields, laps, speed, plain, grad, sems,
):
    copies = load_field(fields, 1, now, low, high, 0, DEEP, sems, 0)
    copies += load_field(fields, 0, after, low, high, 2 * DEEP, SHALLOW, sems, 6)
    copies += load_speed(speed, vel, vel_low, vel_high, 2 * DEEP + 2 * SHALLOW, sems, 12)
    late = [
        pltpu.make_async_copy(laps_in, laps, sems.at[15]),
        pltpu.make_async_copy(vel, plain, sems.at[16]),
    ]
    for copy in copies + late:
        copy.start()
    clear_pads(fields, 5)
    for copy in copies:
        copy.wait()
    square_speed(speed)
    ids = lane_ids()
    for step in range(STEPS):
        moment = STEPS - step
        leap(fields, speed, lanes, step + 1, 4 * (STEPS - 1 - step))
        for shot in range(SHOTS_HERE):

            @pl.loop(0, counts[shot])
            def _(group, shot=shot):
                for member in range(4):
                    item = group * 4 + member
                    row = rows[shot, item]
                    value = misfit[shot * STEPS + moment - 1, index[shot, item]]
                    depth = PAD + (row & (NZ - 1))
                    view = fields.at[step + 2, shot, row >> 5, pl.ds(depth, 1), :]
                    view[...] = view[...] + jnp.where(ids == lanes_of[shot, item], value, 0.0)

    for copy in late:
        copy.wait()

    @pl.loop(0, SLAB)
    def _(plane):
        total = jnp.zeros((NZ, NY), jnp.float32)
        for shot in range(SHOTS_HERE):
            for step in range(STEPS):
                total = total + (
                    fields[step + 2, shot, DEEP + plane, PAD : PAD + NZ, :]
                    * laps[STEPS - 1 - step, shot, plane]
                )
        grad[pl.ds(plane * NZ, NZ), :] = (2.0 * COURANT) * plain[plane] * total

    pack(grad, tiles)


def pack(source, tiles):
    for group in range(NZ // 4):
        block = jnp.concatenate(
            [source[pl.ds(group * 4 + place, SLAB, stride=NZ), :] for place in range(4)], axis=0
        )
        tiles[:, group] = block.T.reshape(tiles.shape[0], 2, 8, NY)


def noise_kernel(noise, tiles, scratch):
    shot = lax.axis_index("shot")
    for group in range(NZ // 4):
        block = jnp.concatenate(
            [noise[pl.ds(group * 4 + place, SLAB, stride=NZ), :] for place in range(4)], axis=0
        )
        scratch[...] = block.T
        tiles[group] = scratch[pl.ds(pl.multiple_of(shot * 16, 16), 16), :].reshape(2, 8, NY)


def swap_blocks(tiles):
    lane = lax.broadcasted_iota(jnp.int32, (8, NY), 1) // SLAB
    swapped = []
    for b in range(4):
        value = tiles[b]
        for a in range(4):
            if a != b:
                value = jnp.where(lane == a, pltpu.roll(tiles[a], (SLAB * (a - b)) % NY, 1), value)
        swapped.append(value)
    return swapped


def gathered(tiles):
    parts = [swap_blocks(tiles[4 * part : 4 * part + 4]) for part in range(4)]
    return jnp.concatenate(
        [jnp.concatenate([parts[part][z] for part in range(4)], axis=1) for z in range(4)], axis=0
    )


def precise(values, high, low):
    first, second = split(values)
    count = values.shape[0]
    both = dot(jnp.concatenate([first, second], axis=0), high)
    return both[:count] + both[count:] + dot(first, low)


def prior_kernel(scales, received, noise, operators, tiles):
    count = received.shape[0] // 16
    sums = []
    for block in range(16):
        total = received[block]
        for shot in range(1, count):
            total = total + received[shot * 16 + block]
        sums.append(total)
    update = scales[0] * precise(gathered(sums), operators[0], operators[1])
    noises = gathered([noise[block] for block in range(16)])
    update = update + scales[1] * precise(noises, operators[2], operators[3])
    for part in range(4):
        lanes = slice(part * NY, (part + 1) * NY)
        swapped = swap_blocks([update[8 * z : 8 * z + 8, lanes] for z in range(4)])
        for place in range(4):
            tiles[4 * part + place] = swapped[place]


def finish_kernel(returned, velocity, out):
    shift = (NY - lax.axis_index("shot") * 16) & (NY - 1)
    for group in range(NZ // 4):
        block = jnp.concatenate([returned[2 * group], returned[2 * group + 1]], axis=0)
        turned = jnp.concatenate([block, jnp.zeros((NY - 16, NY), jnp.float32)], axis=0).T
        for place in range(4):
            where = pl.ds(group * 4 + place, SLAB, stride=NZ)
            base = pltpu.roll(velocity[where, :], shift, 1)
            value = base + turned[place * SLAB : (place + 1) * SLAB]
            out[where, :] = value[:, :16]


def shape(*dims, dtype=jnp.float32):
    return jax.ShapeDtypeStruct(dims, dtype)


def params():
    return pltpu.CompilerParams(vmem_limit_bytes=VMEM_LIMIT)


def neighbours(axis):
    count = lax.axis_size(axis)
    up = [(i, i + 1) for i in range(count - 1)]
    return up, [(b, a) for a, b in up]


def exchange(axis, to_high, to_low):
    up, down = neighbours(axis)
    return lax.ppermute(to_high, axis, up), lax.ppermute(to_low, axis, down)


def edge(deep, shallow, velocity=None):
    both = []
    for begin_deep, begin_shallow in ((SLAB - DEEP, SLAB - SHALLOW), (0, 0)):
        pieces = [deep[s, begin_deep : begin_deep + DEEP] for s in range(SHOTS_HERE)]
        pieces += [shallow[s, begin_shallow : begin_shallow + SHALLOW] for s in range(SHOTS_HERE)]
        if velocity is not None:
            pieces.append(velocity[begin_shallow : begin_shallow + SHALLOW])
        both.append(jnp.concatenate(pieces, axis=0))
    return both


def body(
    velocity,
    noise_field,
    step_size,
    field_prev,
    field_now,
    adjoint_next,
    adjoint_now,
    wavelet,
    source_cells,
    source_signs,
    record_cells,
    observed,
):
    lanes = jnp.asarray(lane_operator())
    operators = jnp.asarray(prior_operators())
    low, high = exchange("dom", *edge(field_now, field_prev, velocity))
    adj_low, adj_high = exchange("dom", *edge(adjoint_now, adjoint_next))

    noise_tiles = pl.pallas_call(
        noise_kernel,
        out_shape=shape(8, 2, 8, NY),
        in_specs=[VMEM],
        out_specs=VMEM,
        scratch_shapes=[pltpu.VMEM((NY, NY), jnp.float32)],
        name="noise_pack",
    )(noise_field.reshape(SLAB * NZ, NY))
    noise_cols = lax.all_to_all(noise_tiles.reshape(16, 8, NY), "dom", 0, 0, tiled=True)

    lists = pl.pallas_call(
        prepare_kernel,
        out_shape=(
            shape(SHOTS_HERE, LIST, dtype=jnp.int32),
            shape(SHOTS_HERE, LIST, dtype=jnp.int32),
            shape(SHOTS_HERE, LIST, dtype=jnp.int32),
            shape(SHOTS_HERE, dtype=jnp.int32),
        ),
        in_specs=[SMEM],
        out_specs=(SMEM,) * 4,
        name="record_lists",
    )(record_cells)

    fields = pltpu.VMEM((STEPS + 2, SHOTS_HERE, ROWS, DEPTH, NY), jnp.float32)
    laplacians, samples = pl.pallas_call(
        forward_kernel,
        out_shape=(shape(STEPS, SHOTS_HERE, SLAB, NZ, NY), shape(SHOTS_HERE * STEPS, NREC)),
        in_specs=[SMEM] * 7 + [ANY] * 5 + [VMEM],
        out_specs=(ANY, VMEM),
        scratch_shapes=[
            fields,
            pltpu.VMEM((STEPS, SHOTS_HERE, ROWS, NZ, NY), jnp.float32),
            pltpu.VMEM((ROWS, NZ, NY), jnp.float32),
            pltpu.SemaphoreType.DMA((15,)),
            pltpu.SemaphoreType.DMA((STEPS,)),
        ],
        compiler_params=params(),
        name="forward_steps",
    )(*lists, source_cells, source_signs, wavelet, field_now, field_prev, velocity, low, high, lanes)

    from_low, from_high = exchange("dom", samples, samples)
    misfit = samples + from_low + from_high - observed.reshape(SHOTS_HERE * STEPS, NREC)

    tiles = pl.pallas_call(
        adjoint_kernel,
        out_shape=shape(8, 8, 2, 8, NY),
        in_specs=[SMEM] * 5 + [ANY] * 8 + [VMEM],
        out_specs=VMEM,
        scratch_shapes=[
            fields,
            pltpu.VMEM((STEPS, SHOTS_HERE, SLAB, NZ, NY), jnp.float32),
            pltpu.VMEM((ROWS, NZ, NY), jnp.float32),
            pltpu.VMEM((SLAB, NZ, NY), jnp.float32),
            pltpu.VMEM((SLAB * NZ, NY), jnp.float32),
            pltpu.SemaphoreType.DMA((17,)),
        ],
        compiler_params=params(),
        name="adjoint_steps",
    )(*lists, misfit, adjoint_now, adjoint_next, velocity, adj_low, adj_high, low, high, laplacians, lanes)

    received = lax.all_to_all(tiles.reshape(128, 8, NY), ("shot", "dom"), 0, 0, tiled=True)
    scales = jnp.concatenate([-0.5 * step_size, jnp.sqrt(step_size)])
    update = pl.pallas_call(
        prior_kernel,
        out_shape=shape(16, 8, NY),
        in_specs=[SMEM, VMEM, VMEM, VMEM],
        out_specs=VMEM,
        compiler_params=params(),
        name="prior",
    )(scales, received, noise_cols, operators)
    returned = lax.all_to_all(update, "dom", 0, 0, tiled=True)
    out = pl.pallas_call(
        finish_kernel,
        out_shape=shape(SLAB * NZ, 16),
        in_specs=[VMEM, VMEM],
        out_specs=VMEM,
        name="finish",
    )(returned, velocity.reshape(SLAB * NZ, NY))
    return out.reshape(SLAB, NZ, 16)


def solution(mesh):
    placed = (
        P("dom", None, None),
        P("dom", None, None),
        P(),
        P("shot", "dom", None, None),
        P("shot", "dom", None, None),
        P("shot", "dom", None, None),
        P("shot", "dom", None, None),
        P("shot", None),
        P("shot", None),
        P("shot", None),
        P("shot", None),
        P("shot", None, None),
    )
    return jax.shard_map(
        body, mesh=mesh, in_specs=placed, out_specs=P("dom", None, "shot"), check_vma=False
    )
```

time: 579 us -> 123 us (0.21); the launches traced: 571 us -> 122 us
  other arithmetic: 261 us -> 4.08 us
  local copies, waits for them, and re-layouts: 105 us -> 10.1 us
  waiting for transfers between devices: 106 us -> 13 us
  Pallas kernels: 0 us -> 46.7 us
  starting transfers between devices: 69.5 us -> 36.5 us
  matrix products: 14.7 us -> 0 us
  between operations: 15.4 us -> 0.88 us
  blocking collectives: 0 us -> 11 us
    scatter-add x8 -> x0, other arithmetic: 149 us -> none  [place(): flat.at[rows_full, target].add(values, mode='drop').reshape(field.shape)]
    add x10 -> x0, other arithmetic: 79.3 us -> none  [the longest x4 47.2 us: body(): advanced = 2.0 * current - prior + speed_sq * spread]
    psum x1 -> x0, waiting for transfers between devices: 78.1 us -> none  [body(): total = lax.psum(partial_value, 'shot')]
    pallas_call x0 -> x6, Pallas kernels: none -> 46.7 us  [the longest x1 17.1 us: body(): pl.pallas_call(adjoint_kernel, out_shape=shape(8, 8, 2, 8, NY), in_specs=...]
    unnamed x127 -> x26, local copies, waits for them, and re-layouts: 52 us -> 7.27 us
    ppermute x16 -> x6, starting transfers between devices: 41.6 us -> 17.1 us  [exchange(): return (lax.ppermute(to_high, axis, up), lax.ppermute(to_low, axis, down))]
    gather x8 -> x0, local copies, waits for them, and re-layouts: 23.5 us -> none  [body(): jnp.take_along_axis(advanced.reshape(shots_here, -1), record_clip, axis=1)]
    ppermute x16 -> x6, waiting for transfers between devices: 18.3 us -> 0.77 us  [exchange(): return (lax.ppermute(to_high, axis, up), lax.ppermute(to_low, axis, down))]
  transfers between devices with their start and end apart: 20 -> 8, of which waited for: 7 -> 2; matrix products, arithmetic and copies ran while one was open for 17% -> 3% of each run, Pallas kernels for 0% -> 34%
where the time goes in v1:
time: 123 us; the launch traced here: 122 us
  Pallas kernels  46.7 us (38%)
  starting transfers between devices  36.5 us (30%)
  waiting for transfers between devices  13 us (11%)
  blocking collectives  11 us (9%)
  local copies, waits for them, and re-layouts  10.1 us (8%)
  other arithmetic  4.08 us (3%)
    ppermute x6, starting transfers between devices, exchange(): return (lax.ppermute(to_high, axis, up), lax.ppermute(to_low, axis, down))  17.1 us
    pallas_call x1, Pallas kernels, body(): pl.pallas_call(adjoint_kernel, out_shape=shape(8, 8, 2, 8, NY), in_specs=...  17.1 us
    pallas_call x1, Pallas kernels, body(): pl.pallas_call(forward_kernel, out_shape=(shape(STEPS, SHOTS_HERE, SLAB,...  16.6 us
    all_to_all x1, waiting for transfers between devices, body(): lax.all_to_all(tiles.reshape(128, 8, NY), ('shot', 'dom'), 0, 0, tiled=True)  12.2 us
    all_to_all x1, blocking collectives, body(): returned = lax.all_to_all(update, 'dom', 0, 0, tiled=True)  11 us
    all_to_all x1, starting transfers between devices, body(): lax.all_to_all(tiles.reshape(128, 8, NY), ('shot', 'dom'), 0, 0, tiled=True)  10.5 us
    all_to_all x1, starting transfers between devices, body(): lax.all_to_all(noise_tiles.reshape(16, 8, NY), 'dom', 0, 0, tiled=True)  8.89 us
    unnamed x26, local copies, waits for them, and re-layouts  7.27 us
  transfers between devices with their start and end apart: 8, of which 2 were waited for; matrix products, arithmetic and copies ran while one was open for 3% of the time, Pallas kernels for 34%

profile of v1, /device:TPU:1, one launch (start us, length us, event | category | flops | bytes accessed | tf_op | source)
XLA Modules:
  0.0 122.2 jit_solution(15097734573661802084)
XLA Ops:
  0.0 2.0 %bitcast_dynamic-update-slice_fusion.1 = (f32[68,32,128]{2,1,0:T(8,128)}, f32[68,32,128]{2,1,0:T(8,128)}) fusion(f32[2,32,32,128]{3,2,1,0:T(8,128)} %now.2), kind=kLoop, calls=%fused_computation.3 | loop fusion | bytes 1048576
  2.0 0.8 bitcast_dynamic-update-slice_fusion
  2.9 0.8 bitcast_dynamic-update-slice_fusion.5
  3.6 0.8 bitcast_dynamic-update-slice_fusion.4
  4.4 0.8 slice_dynamic-update-slice_fusion
  5.2 3.4 %collective-permute-start.1 = (f32[68,32,128]{2,1,0:T(8,128)}, f32[68,32,128]{2,1,0:T(8,128)S(1)}, u32[]{:S(2)}, u32[]{:S(2)}) collective-permute-start(f32[68,32,128]{2,1,0:T(8,128)} %get-tuple-element.33), channel_id=1, source_target_pairs={{1,0},{2,1},{3,2},{4,3},{5,4},{6,5},{7,6},{8,7},{9,8},{10,9},{11,1... | collective-permute-start | bytes 3342344 | tf_op jit(solution)/shard_map/ppermute | solution.py:383
  8.7 3.2 %collective-permute-start = (f32[68,32,128]{2,1,0:T(8,128)}, f32[68,32,128]{2,1,0:T(8,128)S(1)}, u32[]{:S(2)}, u32[]{:S(2)}) collective-permute-start(f32[68,32,128]{2,1,0:T(8,128)} %get-tuple-element.34), channel_id=1, source_target_pairs={{0,1},{1,2},{2,3},{3,4},{4,5},{5,6},{6,7},{7,8},{8,9},{9,10},{10,1... | collective-permute-start | bytes 3342344 | tf_op jit(solution)/shard_map/ppermute | solution.py:383
  11.9 0.1 slice_bitcast_fusion.1
  12.0 1.1 pad_maximum_fusion
  13.1 2.4 %collective-permute-start.4 = (f32[56,32,128]{2,1,0:T(8,128)}, f32[56,32,128]{2,1,0:T(8,128)S(1)}, u32[]{:S(2)}, u32[]{:S(2)}) collective-permute-start(f32[56,32,128]{2,1,0:T(8,128)} %pad_maximum_fusion), channel_id=1, source_target_pairs={{0,1},{1,2},{2,3},{3,4},{4,5},{5,6},{6,7},{7,8},{8,9},{9,10},{10,1... | collective-permute-start | bytes 2752520 | tf_op jit(solution)/shard_map/ppermute | solution.py:383
  15.5 1.1 pad_maximum_fusion.1
  16.6 2.0 %collective-permute-start.5 = (f32[56,32,128]{2,1,0:T(8,128)}, f32[56,32,128]{2,1,0:T(8,128)}, u32[]{:S(2)}, u32[]{:S(2)}) collective-permute-start(f32[56,32,128]{2,1,0:T(8,128)} %pad_maximum_fusion.1), channel_id=1, source_target_pairs={{1,0},{2,1},{3,2},{4,3},{5,4},{6,5},{7,6},{8,7},{9,8},{10,9},{11,1... | collective-permute-start | bytes 2752520 | tf_op jit(solution)/shard_map/ppermute | solution.py:383
  18.6 5.2 %record_lists.1 = (s32[2,264]{1,0:T(2,128)}, s32[2,264]{1,0:T(2,128)}, s32[2,264]{1,0:T(2,128)}, s32[2]{0:T(128)}) custom-call(s32[2,256]{1,0:T(2,128)} %rec.1), custom_call_target="tpu_custom_call" | custom-call | tf_op jit(solution)/shard_map/record_lists/pallas_call | solution.py:426
  23.8 0.8 collective-permute-done.low.vel_low
  24.6 0.3 copy-done.1
  24.9 0.7 copy-done.2
  25.6 16.6 %forward_steps.1 = (f32[4,2,32,32,128]{4,3,2,1,0:T(8,128)}, f32[8,256]{1,0:T(8,128)}) custom-call(s32[2,264]{1,0:T(2,128)} %get-tuple-element.11.rows, s32[2,264]{1,0:T(2,128)} %get-tuple-element.12.lanes_of, s32[2,264]{1,0:T(2,128)} %get-tuple-element.13.index, s32[2]{0:T(128)} %get-tuple-element.14.counts, s32[2,8]{1,0:T(2,128)} %src.1, s32[2,8]{1,0:T(2,128)} %signs.1, ...), custom_call_target="tpu_custom_call" | custom-call | tf_op jit(solution)/shard_map/forward_steps/pallas_call | solution.py:440
  42.3 1.9 %collective-permute-start.3 = (f32[8,256]{1,0:T(8,128)}, f32[8,256]{1,0:T(8,128)S(1)}, u32[]{:S(2)}, u32[]{:S(2)}) collective-permute-start(f32[8,256]{1,0:T(8,128)} %get-tuple-element.15), channel_id=1, source_target_pairs={{1,0},{2,1},{3,2},{4,3},{5,4},{6,5},{7,6},{8,7},{9,8},{10,9},{11,1... | collective-permute-start | bytes 24584 | tf_op jit(solution)/shard_map/ppermute | solution.py:383
  44.2 4.2 %collective-permute-start.2 = (f32[8,256]{1,0:T(8,128)}, f32[8,256]{1,0:T(8,128)S(1)}, u32[]{:S(2)}, u32[]{:S(2)}) collective-permute-start(f32[8,256]{1,0:T(8,128)} %get-tuple-element.15), channel_id=1, source_target_pairs={{0,1},{1,2},{2,3},{3,4},{4,5},{5,6},{6,7},{7,8},{8,9},{9,10},{10,1... | collective-permute-start | bytes 24584 | tf_op jit(solution)/shard_map/ppermute | solution.py:383
  48.4 2.0 %noise_pack.1 = f32[8,2,8,128]{3,2,1,0:T(8,128)} custom-call(f32[1024,128]{1,0:T(8,128)} %bitcast.40), custom_call_target="tpu_custom_call" | custom-call | tf_op jit(solution)/shard_map/noise_pack/pallas_call | solution.py:416
  50.4 8.9 %all-to-all-start.1 = ((f32[16,8,128]{2,1,0:T(8,128)}), f32[16,8,128]{2,1,0:T(8,128)S(1)}, u32[]{:S(2)}, u32[]{:S(2)}) async-start(f32[16,8,128]{2,1,0:T(8,128)} %bitcast.41), calls=%async_computation.1 | async-start | bytes 131072 | tf_op jit(solution)/shard_map/all_to_all | solution.py:424
  59.4 1.3 %add_subtract_fusion.misfit = f32[8,256]{1,0:T(8,128)} fusion(f32[8,256]{1,0:T(8,128)S(1)} %reshape.18, f32[8,256]{1,0:T(8,128)S(1)} %collective-permute-done.3, f32[8,256]{1,0:T(8,128)} %get-tuple-element.15, f32[8,256]{1,0:T(8,128)S(1)} %collective-permute-done.2), kind=kLoop, calls=%fused_computation.20 | loop fusion | flops 6144 | bytes 40960 | tf_op jit(solution)/shard_map/sub | solution.py:457
  60.7 1.0 copy-done.8
  61.7 17.1 %adjoint_steps.1 = f32[8,8,2,8,128]{4,3,2,1,0:T(8,128)} custom-call(s32[2,264]{1,0:T(2,128)} %get-tuple-element.11.rows, s32[2,264]{1,0:T(2,128)} %get-tuple-element.12.lanes_of, s32[2,264]{1,0:T(2,128)} %get-tuple-element.13.index, s32[2]{0:T(128)} %get-tuple-element.14.counts, f32[8,256]{1,0:T(8,128)} %add_subtract_fusion.misfit, f32[2,32,32,128]{3,2,1,0:T(8,128)} %now.3, ...), custom_call_target="tpu_custom_call" | custom-call | tf_op jit(solution)/shard_map/adjoint_steps/pallas_call | solution.py:459
  78.8 10.5 %all-to-all-start = ((f32[128,8,128]{2,1,0:T(8,128)}), f32[128,8,128]{2,1,0:T(8,128)S(1)}, u32[]{:S(2)}, u32[]{:S(2)}) async-start(f32[128,8,128]{2,1,0:T(8,128)} %bitcast.38), calls=%async_computation | async-start | bytes 1048576 | tf_op jit(solution)/shard_map/all_to_all | solution.py:476
  90.0 0.6 pad_maximum_fusion.2.scales
  90.6 12.2 %all-to-all-done.received = f32[128,8,128]{2,1,0:T(8,128)S(1)} async-done(((f32[128,8,128]{2,1,0:T(8,128)}), f32[128,8,128]{2,1,0:T(8,128)S(1)}, u32[]{:S(2)}, u32[]{:S(2)}) %all-to-all-start) | async-done | bytes 524320 | tf_op jit(solution)/shard_map/all_to_all | solution.py:476
  102.9 0.8 copy-done.7
  103.7 3.1 %prior.1 = f32[16,8,128]{2,1,0:T(8,128)} custom-call(f32[2]{0:T(128)} %pad_maximum_fusion.2.scales, f32[128,8,128]{2,1,0:T(8,128)} %copy-done.7, f32[16,8,128]{2,1,0:T(8,128)} %copy-done.9, bf16[4,512,512]{2,1,0:T(8,128)(2,1)} %constant.7.clone.operators), custom_call_target="tpu_custom_call" | custom-call | tf_op jit(solution)/shard_map/prior/pallas_call | solution.py:478
  106.7 11.0 %all_to_all.15.returned = f32[16,8,128]{2,1,0:T(8,128)} all-to-all(f32[16,8,128]{2,1,0:T(8,128)} %prior.1), channel_id=1, replica_groups=mesh['shot'=8,'dom'=16] {'dom'}, dimensions={0} | all-to-all | bytes 131072 | tf_op jit(solution)/shard_map/all_to_all | solution.py:486
  117.7 2.6 %finish.1 = f32[1024,16]{1,0:T(8,128)} custom-call(f32[16,8,128]{2,1,0:T(8,128)} %all_to_all.15.returned, f32[1024,128]{1,0:T(8,128)} %bitcast.37), custom_call_target="tpu_custom_call" | custom-call | tf_op jit(solution)/shard_map/finish/pallas_call | solution.py:487
  120.3 1.9 %copy.15 = f32[32,32,16]{1,2,0:T(8,128)} copy(f32[32,32,16]{2,1,0:T(8,128)} %bitcast.39) | data formatting | bytes 131072 | tf_op jit(solution)/shard_map/reshape | solution.py:494
  (26 shorter events, 0.1 us)
Async XLA Ops:
  0.0 2.0 %copy-start.4 = (f32[2,32,32,128]{3,2,1,0:T(8,128)S(1)}, f32[2,32,32,128]{3,2,1,0:T(8,128)}, u32[]{:S(2)}) copy-start(f32[2,32,32,128]{3,2,1,0:T(8,128)} %now.2) | copy-start | bytes 3145732
  0.0 2.8 %copy-start.6 = (f32[2,32,32,128]{3,2,1,0:T(8,128)S(1)}, f32[2,32,32,128]{3,2,1,0:T(8,128)}, u32[]{:S(2)}) copy-start(f32[2,32,32,128]{3,2,1,0:T(8,128)} %prev.1) | copy-start | bytes 3145732
  2.0 2.4 %copy-start = (f32[32,32,128]{2,1,0:T(8,128)S(1)}, f32[32,32,128]{2,1,0:T(8,128)}, u32[]{:S(2)}) copy-start(f32[32,32,128]{2,1,0:T(8,128)} %vel.3) | copy-start | bytes 1572868
  2.9 9.0 %copy-start.3 = (f32[2,32,32,128]{3,2,1,0:T(8,128)S(1)}, f32[2,32,32,128]{3,2,1,0:T(8,128)}, u32[]{:S(2)}) copy-start(f32[2,32,32,128]{3,2,1,0:T(8,128)} %now.3) | copy-start | bytes 3145732
  5.2 6.7 %copy-start.5 = (f32[2,32,32,128]{3,2,1,0:T(8,128)S(1)}, f32[2,32,32,128]{3,2,1,0:T(8,128)}, u32[]{:S(2)}) copy-start(f32[2,32,32,128]{3,2,1,0:T(8,128)} %after.1) | copy-start | bytes 3145732
  5.2 18.6 %collective-permute-start.1 = (f32[68,32,128]{2,1,0:T(8,128)}, f32[68,32,128]{2,1,0:T(8,128)S(1)}, u32[]{:S(2)}, u32[]{:S(2)}) collective-permute-start(f32[68,32,128]{2,1,0:T(8,128)} %get-tuple-element.33), channel_id=1, source_target_pairs={{1,0},{2,1},{3,2},{4,3},{5,4},{6,5},{7,6},{8,7},{9,8},{10,9},{11,1... | collective-permute-start | bytes 3342344 | tf_op jit(solution)/shard_map/ppermute | solution.py:383
  8.7 15.9 %collective-permute-start = (f32[68,32,128]{2,1,0:T(8,128)}, f32[68,32,128]{2,1,0:T(8,128)S(1)}, u32[]{:S(2)}, u32[]{:S(2)}) collective-permute-start(f32[68,32,128]{2,1,0:T(8,128)} %get-tuple-element.34), channel_id=1, source_target_pairs={{0,1},{1,2},{2,3},{3,4},{4,5},{5,6},{6,7},{7,8},{8,9},{9,10},{10,1... | collective-permute-start | bytes 3342344 | tf_op jit(solution)/shard_map/ppermute | solution.py:383
  13.1 47.6 %collective-permute-start.4 = (f32[56,32,128]{2,1,0:T(8,128)}, f32[56,32,128]{2,1,0:T(8,128)S(1)}, u32[]{:S(2)}, u32[]{:S(2)}) collective-permute-start(f32[56,32,128]{2,1,0:T(8,128)} %pad_maximum_fusion), channel_id=1, source_target_pairs={{0,1},{1,2},{2,3},{3,4},{4,5},{5,6},{6,7},{7,8},{8,9},{9,10},{10,1... | collective-permute-start | bytes 2752520 | tf_op jit(solution)/shard_map/ppermute | solution.py:383
  16.6 44.1 %collective-permute-start.5 = (f32[56,32,128]{2,1,0:T(8,128)}, f32[56,32,128]{2,1,0:T(8,128)}, u32[]{:S(2)}, u32[]{:S(2)}) collective-permute-start(f32[56,32,128]{2,1,0:T(8,128)} %pad_maximum_fusion.1), channel_id=1, source_target_pairs={{1,0},{2,1},{3,2},{4,3},{5,4},{6,5},{7,6},{8,7},{9,8},{10,9},{11,1... | collective-permute-start | bytes 2752520 | tf_op jit(solution)/shard_map/ppermute | solution.py:383
  23.8 1.0 copy-start.1
  24.6 1.0 copy-start.2
  25.6 33.7 %copy-start.10 = (f32[2,4,256]{2,1,0:T(4,128)S(1)}, f32[2,4,256]{2,1,0:T(4,128)}, u32[]{:S(2)}) copy-start(f32[2,4,256]{2,1,0:T(4,128)} %param.25) | copy-start | bytes 24580
  42.3 17.1 %collective-permute-start.3 = (f32[8,256]{1,0:T(8,128)}, f32[8,256]{1,0:T(8,128)S(1)}, u32[]{:S(2)}, u32[]{:S(2)}) collective-permute-start(f32[8,256]{1,0:T(8,128)} %get-tuple-element.15), channel_id=1, source_target_pairs={{1,0},{2,1},{3,2},{4,3},{5,4},{6,5},{7,6},{8,7},{9,8},{10,9},{11,1... | collective-permute-start | bytes 24584 | tf_op jit(solution)/shard_map/ppermute | solution.py:383
  44.2 15.2 %collective-permute-start.2 = (f32[8,256]{1,0:T(8,128)}, f32[8,256]{1,0:T(8,128)S(1)}, u32[]{:S(2)}, u32[]{:S(2)}) collective-permute-start(f32[8,256]{1,0:T(8,128)} %get-tuple-element.15), channel_id=1, source_target_pairs={{0,1},{1,2},{2,3},{3,4},{4,5},{5,6},{6,7},{7,8},{8,9},{9,10},{10,1... | collective-permute-start | bytes 24584 | tf_op jit(solution)/shard_map/ppermute | solution.py:383
  50.4 28.4 %all-to-all-start.1 = ((f32[16,8,128]{2,1,0:T(8,128)}), f32[16,8,128]{2,1,0:T(8,128)S(1)}, u32[]{:S(2)}, u32[]{:S(2)}) async-start(f32[16,8,128]{2,1,0:T(8,128)} %bitcast.41), calls=%async_computation.1 | async-start | bytes 131072 | tf_op jit(solution)/shard_map/all_to_all | solution.py:424
  60.7 1.0 copy-start.8
  78.8 24.0 %copy-start.9 = (f32[16,8,128]{2,1,0:T(8,128)}, f32[16,8,128]{2,1,0:T(8,128)S(1)}, u32[]{:S(2)}) copy-start(f32[16,8,128]{2,1,0:T(8,128)S(1)} %all-to-all-done.1.noise) | copy-start | bytes 196612
  78.8 24.0 %all-to-all-start = ((f32[128,8,128]{2,1,0:T(8,128)}), f32[128,8,128]{2,1,0:T(8,128)S(1)}, u32[]{:S(2)}, u32[]{:S(2)}) async-start(f32[128,8,128]{2,1,0:T(8,128)} %bitcast.38), calls=%async_computation | async-start | bytes 1048576 | tf_op jit(solution)/shard_map/all_to_all | solution.py:476
  102.9 0.8 copy-start.7

commit v2 on v1

v2 whole, which is shorter than its diff:
```python
import math

import jax
import jax.numpy as jnp
import ml_dtypes
import numpy as np
from jax import lax
from jax.experimental import pallas as pl
from jax.experimental.pallas import tpu as pltpu
from jax.sharding import PartitionSpec as P

STEPS = 4
COEFFS = (-205.0 / 72.0, 8.0 / 5.0, -1.0 / 5.0, 8.0 / 315.0, -1.0 / 560.0)
COURANT = 0.02
CUTOFF = 16

NX, NZ, NY = 512, 32, 128
SLAB = 32
DEEP = 16
SHALLOW = 12
ROWS = SLAB + 2 * DEEP
PAD = 8
DEPTH = NZ + 2 * PAD
SHOTS_HERE = 2
NREC = 256
LIST = NREC + 8
CHUNK = 4
VMEM_LIMIT = 56 * 1024 * 1024

ANY = pl.BlockSpec(memory_space=pl.ANY)
VMEM = pl.BlockSpec(memory_space=pltpu.VMEM)
SMEM = pl.BlockSpec(memory_space=pltpu.SMEM)


def split_host(matrix):
    high = matrix.astype(ml_dtypes.bfloat16)
    low = (matrix - high.astype(np.float64)).astype(ml_dtypes.bfloat16)
    return high, low


def lane_operator():
    band = np.zeros((NY, NY))
    np.fill_diagonal(band, 3.0 * COEFFS[0])
    for distance in range(1, 5):
        band += COEFFS[distance] * (np.eye(NY, k=distance) + np.eye(NY, k=-distance))
    high, low = split_host(band)
    zero = np.zeros_like(low)
    return np.block([[high, low], [high, zero]])


def prior_operators():
    wave = np.arange(NX)[:, None]
    position = np.arange(NX)[None, :]
    factor = np.where(wave == 0, math.sqrt(1.0 / NX), math.sqrt(2.0 / NX))
    basis = factor * np.cos(math.pi / (2.0 * NX) * (wave * (2 * position + 1) % (4 * NX)))
    gain = 1.0 / np.sqrt(1.0 + np.arange(NX) / CUTOFF)
    order = np.arange(NX).reshape(NX // 4, 4).T.reshape(-1)
    both = []
    for weight in (gain**2, gain):
        operator = basis.T @ (weight[:, None] * basis)
        both.append(np.stack(split_host(operator[order][:, order])))
    return both


def split(values):
    high = values.astype(jnp.bfloat16)
    low = (values - high.astype(jnp.float32)).astype(jnp.bfloat16)
    return high, low


def dot(left, right):
    return jnp.dot(left, right, preferred_element_type=jnp.float32)


def edge_pairs(deep, shallow, velocity, up, down):
    pairs = []
    for target, deep_at, shallow_at in ((up, SLAB - DEEP, SLAB - SHALLOW), (down, 0, 0)):
        for shot in range(SHOTS_HERE):
            pairs.append((deep.at[shot, pl.ds(deep_at, DEEP)], target.at[pl.ds(shot * DEEP, DEEP)]))
            begin = SHOTS_HERE * DEEP + shot * SHALLOW
            pairs.append((shallow.at[shot, pl.ds(shallow_at, SHALLOW)], target.at[pl.ds(begin, SHALLOW)]))
        if velocity is not None:
            begin = SHOTS_HERE * (DEEP + SHALLOW)
            pairs.append((velocity.at[pl.ds(shallow_at, SHALLOW)], target.at[pl.ds(begin, SHALLOW)]))
    return pairs


def started(pairs, sems):
    copies = [pltpu.make_async_copy(source, target, sems.at[n]) for n, (source, target) in enumerate(pairs)]
    for copy in copies:
        copy.start()
    return copies


def edge_kernel(deep, shallow, velocity, up, down, sems):
    for copy in started(edge_pairs(deep, shallow, velocity, up, down), sems):
        copy.wait()


def prepare_kernel(
    rec, src, deep, shallow, noise, velocity,
    up, down, noise_out, velocity_out, entries, counts, src_entries, src_counts,
    turned, sems,
):
    copies = started(edge_pairs(deep, shallow, None, up, down), sems)
    list_cells(rec, entries, counts)
    list_cells(src, src_entries, src_counts)
    column_slices(noise, noise_out, turned)
    column_slices(velocity, velocity_out, turned)
    for copy in copies:
        copy.wait()


def list_cells(cells, entries, count_out):
    base = (lax.axis_index("dom") * SLAB - SHALLOW) * (NZ * NY)
    span = (SLAB + 2 * SHALLOW) * NZ * NY

    def gather(item, counts):
        following = []
        for shot in range(SHOTS_HERE):
            cell = cells[shot, item] - base
            entries[shot, counts[shot]] = (cell << 8) | item
            inside = (cell >= 0) & (cell < span)
            following.append(counts[shot] + inside.astype(jnp.int32))
        return tuple(following)

    counts = lax.fori_loop(0, cells.shape[1], gather, (jnp.int32(0),) * SHOTS_HERE, unroll=8)
    for shot in range(SHOTS_HERE):
        for extra in range(4):
            entries[shot, counts[shot] + extra] = -1
        count_out[shot] = counts[shot]


def unpack_entry(entry):
    filler = entry < 0
    cell = jnp.where(filler, 0, entry >> 8)
    plane = (cell >> 12) + (DEEP - SHALLOW)
    depth = PAD + ((cell >> 7) & (NZ - 1))
    lane = jnp.where(filler, -1, cell & (NY - 1))
    return plane, depth, lane, jnp.where(filler, 0, entry & (NREC - 1))


def clear_pads(fields):
    zeros = jnp.zeros((ROWS, PAD, NY), jnp.float32)
    for field in fields:
        for shot in range(SHOTS_HERE):
            field[shot, :, 0:PAD, :] = zeros
            field[shot, :, PAD + NZ : DEPTH, :] = zeros


def load_field(field, own, low, high, offset, width, sems, base):
    copies = []
    begin = DEEP - width
    for shot in range(SHOTS_HERE):
        planes = pl.ds(offset + shot * width, width)
        view = field.at[shot]
        for number, (source, target) in enumerate(
            (
                (low.at[planes], view.at[pl.ds(begin, width), pl.ds(PAD, NZ), :]),
                (own.at[shot], view.at[pl.ds(DEEP, SLAB), pl.ds(PAD, NZ), :]),
                (high.at[planes], view.at[pl.ds(DEEP + SLAB, width), pl.ds(PAD, NZ), :]),
            )
        ):
            copies.append(pltpu.make_async_copy(source, target, sems.at[base + shot * 3 + number]))
    return copies


def load_speed(speed, own, low, high, offset, sems, base):
    planes = pl.ds(offset, SHALLOW)
    return [
        pltpu.make_async_copy(low.at[planes], speed.at[pl.ds(DEEP - SHALLOW, SHALLOW)], sems.at[base]),
        pltpu.make_async_copy(own, speed.at[pl.ds(DEEP, SLAB)], sems.at[base + 1]),
        pltpu.make_async_copy(high.at[planes], speed.at[pl.ds(DEEP + SLAB, SHALLOW)], sems.at[base + 2]),
    ]


def square_speed(speed):
    @pl.loop(0, (SLAB + 2 * SHALLOW) // 8)
    def _(part):
        rows = pl.ds(DEEP - SHALLOW + part * 8, 8)
        value = speed[rows]
        speed[rows] = COURANT * value * value


def along_lanes(field, lanes, along, margin):
    first, count = DEEP - margin, SLAB + 2 * margin
    part = count // 2
    for shot in range(SHOTS_HERE):
        for half in range(2):
            begin = first + half * part
            block = field[shot, begin : begin + part, PAD : PAD + NZ, :].reshape(part * NZ, NY)
            both = dot(jnp.concatenate(split(block), axis=1), lanes[...])
            along[shot, begin : begin + part] = (both[:, :NY] + both[:, NY:]).reshape(part, NZ, NY)


def leap(field, before, after, speed, along, margin, laplacians=None, slot=None):
    first = DEEP - margin

    @pl.loop(0, (SLAB + 2 * margin) // CHUNK)
    def _(chunk):
        for plane in range(CHUNK):
            here = first + chunk * CHUNK + plane
            for shot in range(SHOTS_HERE):
                spread = along[shot, here]
                for distance in range(1, 5):
                    beside = (
                        field[shot, here + distance, PAD : PAD + NZ, :]
                        + field[shot, here - distance, PAD : PAD + NZ, :]
                    ) + (
                        field[shot, here, PAD + distance : PAD + NZ + distance, :]
                        + field[shot, here, PAD - distance : PAD + NZ - distance, :]
                    )
                    spread = spread + COEFFS[distance] * beside
                centre = field[shot, here, PAD : PAD + NZ, :]
                after[shot, here, PAD : PAD + NZ, :] = (
                    2.0 * centre - before[shot, here, PAD : PAD + NZ, :] + speed[here] * spread
                )
                if laplacians is not None:
                    laplacians[slot, shot, here] = spread


def lane_ids():
    return lax.broadcasted_iota(jnp.int32, (1, NY), 1)


def forward_kernel(
    entries, counts, src, src_counts, signs, wave,
    now, prev, vel, low, high, lanes, noise,
    lap_out, outgoing,
    *scratch,
):
    fields = scratch[: STEPS + 2]
    laps, speed, along, samples, sems, out_sems = scratch[STEPS + 2 :]
    first_copies = load_field(fields[1], now, low, high, 0, DEEP, sems, 0)
    copies = load_field(fields[0], prev, low, high, 2 * DEEP, SHALLOW, sems, 6)
    copies += load_speed(speed, vel, low, high, 2 * DEEP + 2 * SHALLOW, sems, 12)
    for copy in first_copies + copies:
        copy.start()
    clear_pads(fields[1 : STEPS + 1])
    for copy in first_copies:
        copy.wait()
    ids = lane_ids()
    outs = []
    for moment in range(STEPS):
        margin = 4 * (STEPS - 1 - moment)
        along_lanes(fields[moment + 1], lanes, along, margin)
        if moment == 0:
            for copy in copies:
                copy.wait()
            square_speed(speed)
        leap(fields[moment + 1], fields[moment], fields[moment + 2], speed, along, margin, laps, moment)
        out = pltpu.make_async_copy(laps.at[moment, :, pl.ds(DEEP, SLAB)], lap_out.at[moment], out_sems.at[moment])
        out.start()
        outs.append(out)
        for shot in range(SHOTS_HERE):

            @pl.loop(0, src_counts[shot])
            def _(item, shot=shot):
                plane, depth, lane, which = unpack_entry(src[shot, item])
                amplitude = (2 * signs[shot, which] - 1).astype(jnp.float32) * wave[shot, moment]
                view = fields[moment + 2].at[shot, plane, pl.ds(depth, 1), :]
                view[...] = view[...] + jnp.where(ids == lane, amplitude, 0.0)

    for shot in range(SHOTS_HERE):

        def sample(group, state, shot=shot):
            state = list(state)
            for member in range(4):
                plane, depth, lane, which = unpack_entry(entries[shot, group * 4 + member])
                own = (lane >= 0) & (plane >= DEEP) & (plane < DEEP + SLAB)
                shift = (which - lane) & (NY - 1)
                hits = [ids == jnp.where(own, which - half * NY, -1) for half in range(2)]
                for moment in range(STEPS):
                    line = fields[moment + 2][shot, plane, pl.ds(depth, 1), :]
                    line = pltpu.roll(line, shift, 1)
                    for half in range(2):
                        at = moment * 2 + half
                        state[at] = jnp.where(hits[half], line, state[at])
            return tuple(state)

        zero = jnp.zeros((1, NY), jnp.float32)
        state = lax.fori_loop(0, (counts[shot] + 3) >> 2, sample, (zero,) * (2 * STEPS))
        for moment in range(STEPS):
            for half in range(2):
                line = half * 8 + shot * STEPS + moment
                samples[line : line + 1, :] = state[moment * 2 + half]
    block = samples[...]
    for target in range(16):
        outgoing[target * 24 : target * 24 + 8, :] = noise[target * 8 : target * 8 + 8, :]
        outgoing[target * 24 + 8 : target * 24 + 24, :] = block
    for out in outs:
        out.wait()


def adjoint_kernel(
    entries, counts,
    now, after, vel, low, high, vel_low, vel_high, laps_in, lanes, incoming, observed,
    tiles,
    *scratch,
):
    fields = scratch[: STEPS + 2]
    laps, speed, along, plain, differences, misfit, sems = scratch[STEPS + 2 :]
    first_copies = load_field(fields[1], now, low, high, 0, DEEP, sems, 0)
    copies = load_field(fields[0], after, low, high, 2 * DEEP, SHALLOW, sems, 6)
    copies += load_speed(speed, vel, vel_low, vel_high, 2 * DEEP + 2 * SHALLOW, sems, 12)
    late = [
        pltpu.make_async_copy(laps_in, laps, sems.at[15]),
        pltpu.make_async_copy(vel, plain, sems.at[16]),
    ]
    for copy in first_copies + copies + late:
        copy.start()
    total = incoming[8:24, :]
    for block in range(1, 16):
        total = total + incoming[block * 24 + 8 : block * 24 + 24, :]
    for shot in range(SHOTS_HERE):
        rows = slice(shot * STEPS, (shot + 1) * STEPS)
        for half in range(2):
            columns = slice(half * NY, (half + 1) * NY)
            differences[rows, columns] = (
                total[half * 8 + shot * STEPS : half * 8 + (shot + 1) * STEPS] - observed[shot, :, columns]
            )
    to_scalars = pltpu.make_async_copy(differences, misfit, sems.at[17])
    to_scalars.start()
    clear_pads(fields[1 : STEPS + 1])
    for copy in first_copies:
        copy.wait()
    ids = lane_ids()
    for step in range(STEPS):
        moment = STEPS - step
        margin = 4 * (STEPS - 1 - step)
        along_lanes(fields[step + 1], lanes, along, margin)
        if step == 0:
            for copy in copies:
                copy.wait()
            square_speed(speed)
        leap(fields[step + 1], fields[step], fields[step + 2], speed, along, margin)
        if step == 0:
            to_scalars.wait()
        for shot in range(SHOTS_HERE):

            @pl.loop(0, (counts[shot] + 3) >> 2)
            def _(group, shot=shot):
                for member in range(4):
                    plane, depth, lane, which = unpack_entry(entries[shot, group * 4 + member])
                    value = misfit[shot * STEPS + moment - 1, which]
                    view = fields[step + 2].at[shot, plane, pl.ds(depth, 1), :]
                    view[...] = view[...] + jnp.where(ids == lane, value, 0.0)

    for copy in late:
        copy.wait()
    for group in range(SLAB // 4):
        planes = []
        for plane in range(group * 4, group * 4 + 4):
            total = jnp.zeros((NZ, NY), jnp.float32)
            for shot in range(SHOTS_HERE):
                for step in range(STEPS):
                    total = total + (
                        fields[step + 2][shot, DEEP + plane, PAD : PAD + NZ, :]
                        * laps[STEPS - 1 - step, shot, plane]
                    )
            planes.append((2.0 * COURANT) * plain[plane] * total)
        tiles[pl.ds(group, NY, stride=SLAB // 4), :] = jnp.concatenate(planes, axis=0).T


def column_slices(source, target, turned):
    begin = pl.multiple_of(lax.axis_index("shot") * 16, 16)
    for group in range(SLAB // 4):
        turned[...] = source[group * NY : (group + 1) * NY, :].T
        target[pl.ds(group, 16, stride=SLAB // 4), :] = turned[pl.ds(begin, 16), :]


def apply_prior(columns, operators):
    lane = lax.broadcasted_iota(jnp.int32, (NY, NY), 1)
    blocks = []
    for place in range(4):
        turned = columns if place == 0 else pltpu.roll(columns, NY - 32 * place, 1)
        high = turned.astype(jnp.bfloat16).astype(jnp.float32)
        low = pltpu.roll(turned - high, 32, 1)
        blocks.append(jnp.where(lane < 32, high, low).astype(jnp.bfloat16))
    right = jnp.concatenate(blocks, axis=0)
    upper = dot(operators[0], right)
    lower = dot(operators[1], right)
    result = jnp.zeros((NY, NY), jnp.float32)
    for place in range(4):
        rows = slice(place * NY, (place + 1) * NY)
        value = (upper[rows] + lower[rows]) + pltpu.roll(upper[rows], NY - 32, 1)
        value = pltpu.roll(value, 32 * place, 1) if place else value
        result = jnp.where(lane // 32 == place, value, result)
    return result


def noise_kernel(step_size, incoming, operators, out):
    columns = jnp.concatenate([incoming[block * 24 : block * 24 + 8, :] for block in range(16)], axis=0)
    scale = jnp.sqrt(jnp.full((8, NY), step_size[0], jnp.float32))[0:1]
    out[...] = scale * apply_prior(columns, operators)


def prior_kernel(step_size, received, noise, operators_in, out, parts, operators, sems):
    count = parts.shape[0]
    pairs = [(received.at[pl.ds(part * NY, NY)], parts.at[part]) for part in range(count)]
    copies = started([*pairs, (operators_in, operators)], sems)
    total = None
    for part in range(count):
        copies[part].wait()
        total = parts[part] if part == 0 else total + parts[part]
    copies[count].wait()
    out[...] = (-0.5 * step_size[0]) * apply_prior(total, operators) + noise[...]


def finish_kernel(returned, velocity, out):
    for group in range(SLAB // 4):
        rows = pl.ds(group, 16, stride=SLAB // 4)
        value = returned[rows, :] + velocity[rows, :]
        for place in range(4):
            turned = value if place == 0 else pltpu.roll(value, NY - 32 * place, 1)
            out[group * 4 + place] = turned[:, :NZ]


def shape(*dims, dtype=jnp.float32):
    return jax.ShapeDtypeStruct(dims, dtype)


def params():
    return pltpu.CompilerParams(vmem_limit_bytes=VMEM_LIMIT)


def neighbours(axis):
    count = lax.axis_size(axis)
    up = [(i, i + 1) for i in range(count - 1)]
    return up, [(b, a) for a, b in up]


def exchange(axis, to_high, to_low):
    up, down = neighbours(axis)
    return lax.ppermute(to_high, axis, up), lax.ppermute(to_low, axis, down)


def body(
    velocity,
    noise_field,
    step_size,
    field_prev,
    field_now,
    adjoint_next,
    adjoint_now,
    wavelet,
    source_cells,
    source_signs,
    record_cells,
    observed,
):
    lanes = jnp.asarray(lane_operator())
    squared, single = (jnp.asarray(operator) for operator in prior_operators())
    planes = SHOTS_HERE * (DEEP + SHALLOW)
    up, down = pl.pallas_call(
        edge_kernel,
        out_shape=(shape(planes + SHALLOW, NZ, NY),) * 2,
        in_specs=[ANY] * 3,
        out_specs=(VMEM,) * 2,
        scratch_shapes=[pltpu.SemaphoreType.DMA((10,))],
        name="edges",
    )(field_now, field_prev, velocity)
    low, high = exchange("dom", up, down)
    adjoint_edge, up, down = lax.optimization_barrier((adjoint_now, up, down))

    adj_up, adj_down, noise_tiles, velocity_tiles, *lists = pl.pallas_call(
        prepare_kernel,
        out_shape=(
            *(shape(planes, NZ, NY),) * 2,
            *(shape(NY, NY),) * 2,
            shape(SHOTS_HERE, LIST, dtype=jnp.int32),
            shape(SHOTS_HERE, dtype=jnp.int32),
            shape(SHOTS_HERE, 16, dtype=jnp.int32),
            shape(SHOTS_HERE, dtype=jnp.int32),
        ),
        in_specs=[SMEM] * 2 + [ANY] * 2 + [VMEM] * 2,
        out_specs=(VMEM,) * 4 + (SMEM,) * 4,
        scratch_shapes=[pltpu.VMEM((NY, NY), jnp.float32), pltpu.SemaphoreType.DMA((8,))],
        name="prepare",
    )(
        record_cells, source_cells, adjoint_edge, adjoint_next,
        noise_field.reshape(SLAB * NZ, NY), velocity.reshape(SLAB * NZ, NY),
    )
    adj_low, adj_high = exchange("dom", adj_up, adj_down)

    fields = [pltpu.VMEM((SHOTS_HERE, ROWS, DEPTH, NY), jnp.float32)] * (STEPS + 2)
    speed = pltpu.VMEM((ROWS, NZ, NY), jnp.float32)
    along = pltpu.VMEM((SHOTS_HERE, ROWS, NZ, NY), jnp.float32)
    laplacians, outgoing = pl.pallas_call(
        forward_kernel,
        out_shape=(shape(STEPS, SHOTS_HERE, SLAB, NZ, NY), shape(16 * 24, NY)),
        in_specs=[SMEM] * 6 + [ANY] * 5 + [VMEM] * 2,
        out_specs=(ANY, VMEM),
        scratch_shapes=[
            *fields,
            pltpu.VMEM((STEPS, SHOTS_HERE, ROWS, NZ, NY), jnp.float32),
            speed,
            along,
            pltpu.VMEM((16, NY), jnp.float32),
            pltpu.SemaphoreType.DMA((15,)),
            pltpu.SemaphoreType.DMA((STEPS,)),
        ],
        compiler_params=params(),
        name="forward_steps",
    )(*lists, source_signs, wavelet, field_now, field_prev, velocity, low, high, lanes, noise_tiles)

    incoming = lax.all_to_all(outgoing.reshape(16, 24, NY), "dom", 0, 0, tiled=True).reshape(16 * 24, NY)

    tiles = pl.pallas_call(
        adjoint_kernel,
        out_shape=shape(SLAB * NZ, NY),
        in_specs=[SMEM] * 2 + [ANY] * 8 + [VMEM] * 3,
        out_specs=VMEM,
        scratch_shapes=[
            *fields,
            pltpu.VMEM((STEPS, SHOTS_HERE, SLAB, NZ, NY), jnp.float32),
            speed,
            along,
            pltpu.VMEM((SLAB, NZ, NY), jnp.float32),
            pltpu.VMEM((SHOTS_HERE * STEPS, NREC), jnp.float32),
            pltpu.SMEM((SHOTS_HERE * STEPS, NREC), jnp.float32),
            pltpu.SemaphoreType.DMA((18,)),
        ],
        compiler_params=params(),
        name="adjoint_steps",
    )(
        *lists[:2], adjoint_now, adjoint_next, velocity, adj_low, adj_high, low, high, laplacians,
        lanes, incoming, observed,
    )

    noise_update = pl.pallas_call(
        noise_kernel,
        out_shape=shape(NY, NY),
        in_specs=[SMEM, VMEM, VMEM],
        out_specs=VMEM,
        name="noise_prior",
    )(step_size, incoming, single)

    received = lax.all_to_all(tiles.reshape(128, 8, NY), ("shot", "dom"), 0, 0, tiled=True)
    update = pl.pallas_call(
        prior_kernel,
        out_shape=shape(NY, NY),
        in_specs=[SMEM, ANY, VMEM, ANY],
        out_specs=VMEM,
        scratch_shapes=[
            pltpu.VMEM((8, NY, NY), jnp.float32),
            pltpu.VMEM(squared.shape, jnp.bfloat16),
            pltpu.SemaphoreType.DMA((9,)),
        ],
        name="prior",
    )(step_size, received.reshape(128 * 8, NY), noise_update, squared)
    returned = lax.all_to_all(update.reshape(16, 8, NY), "dom", 0, 0, tiled=True)
    out = pl.pallas_call(
        finish_kernel,
        out_shape=shape(SLAB, 16, NZ),
        in_specs=[VMEM, VMEM],
        out_specs=VMEM,
        name="finish",
    )(returned.reshape(NY, NY), velocity_tiles)
    return out.transpose(0, 2, 1)


def solution(mesh):
    placed = (
        P("dom", None, None),
        P("dom", None, None),
        P(),
        P("shot", "dom", None, None),
        P("shot", "dom", None, None),
        P("shot", "dom", None, None),
        P("shot", "dom", None, None),
        P("shot", None),
        P("shot", None),
        P("shot", None),
        P("shot", None),
        P("shot", None, None),
    )
    return jax.shard_map(
        body, mesh=mesh, in_specs=placed, out_specs=P("dom", None, "shot"), check_vma=False
    )
```

time: 123 us -> 106 us (0.86)
  starting transfers between devices: 36.5 us -> 27.1 us
  local copies, waits for them, and re-layouts: 10.1 us -> 2.49 us
  waiting for transfers between devices: 13 us -> 20.5 us
  other arithmetic: 4.08 us -> 0 us
  Pallas kernels: 46.7 us -> 43.3 us
    all_to_all x1, waiting for transfers between devices: 0.01 us -> 6.63 us  [body(): lax.all_to_all(outgoing.reshape(16, 24, NY), 'dom', 0, 0, tiled=True)]
    ppermute x6 -> x4, starting transfers between devices: 17.1 us -> 12.1 us  [exchange(): return (lax.ppermute(to_high, axis, up), lax.ppermute(to_low, axis, down))]
    unnamed x26 -> x10, local copies, waits for them, and re-layouts: 7.27 us -> 2.49 us
    pallas_call x1, Pallas kernels: 16.6 us -> 12.7 us  [body(): pl.pallas_call(forward_kernel, out_shape=(shape(STEPS, SHOTS_HERE, SLAB,...]
    ppermute x6 -> x4, waiting for transfers between devices: 0.77 us -> 3.64 us  [exchange(): return (lax.ppermute(to_high, axis, up), lax.ppermute(to_low, axis, down))]
    concatenate x3 -> x0, other arithmetic: 2.78 us -> none  [the longest x2 2.17 us: edge(): both.append(jnp.concatenate(pieces, axis=0))]
    all_to_all x1, starting transfers between devices: 8.89 us -> 6.56 us  [body(): lax.all_to_all(outgoing.reshape(16, 24, NY), 'dom', 0, 0, tiled=True)]
    all_to_all x1, waiting for transfers between devices: 12.2 us -> 10.2 us  [body(): lax.all_to_all(tiles.reshape(128, 8, NY), ('shot', 'dom'), 0, 0, tiled=True)]
  transfers between devices with their start and end apart: 8 -> 6, of which waited for: 2 -> 3; matrix products, arithmetic and copies ran while one was open for 3% -> 0% of each run, Pallas kernels for 34% -> 20%
where the time goes in v2:
time: 106 us; the launch traced here: 105 us
  Pallas kernels  43.3 us (41%)
  starting transfers between devices  27.1 us (26%)
  waiting for transfers between devices  20.5 us (19%)
  blocking collectives  11 us (10%)
  local copies, waits for them, and re-layouts  2.49 us (2%)
    pallas_call x1, Pallas kernels, body(): pl.pallas_call(adjoint_kernel, out_shape=shape(SLAB * NZ, NY), in_specs=[...  13.6 us
    pallas_call x1, Pallas kernels, body(): pl.pallas_call(forward_kernel, out_shape=(shape(STEPS, SHOTS_HERE, SLAB,...  12.7 us
    ppermute x4, starting transfers between devices, exchange(): return (lax.ppermute(to_high, axis, up), lax.ppermute(to_low, axis, down))  12.1 us
    all_to_all x1, blocking collectives, body(): lax.all_to_all(update.reshape(16, 8, NY), 'dom', 0, 0, tiled=True)  11 us
    all_to_all x1, waiting for transfers between devices, body(): lax.all_to_all(tiles.reshape(128, 8, NY), ('shot', 'dom'), 0, 0, tiled=True)  10.2 us
    all_to_all x1, starting transfers between devices, body(): lax.all_to_all(tiles.reshape(128, 8, NY), ('shot', 'dom'), 0, 0, tiled=True)  8.49 us
    all_to_all x1, waiting for transfers between devices, body(): lax.all_to_all(outgoing.reshape(16, 24, NY), 'dom', 0, 0, tiled=True)  6.63 us
    all_to_all x1, starting transfers between devices, body(): lax.all_to_all(outgoing.reshape(16, 24, NY), 'dom', 0, 0, tiled=True)  6.56 us
  transfers between devices with their start and end apart: 6, of which 3 were waited for; matrix products, arithmetic and copies ran while one was open for 0% of the time, Pallas kernels for 20%

profile of v2, /device:TPU:1, one launch (start us, length us, event | category | flops | bytes accessed | tf_op | source)
XLA Modules:
  0.0 105.1 jit_solution(11135776771890290845)
XLA Ops:
  0.0 3.0 %edges.1 = (f32[68,32,128]{2,1,0:T(8,128)}, f32[68,32,128]{2,1,0:T(8,128)}) custom-call(f32[2,32,32,128]{3,2,1,0:T(8,128)} %now.2, f32[2,32,32,128]{3,2,1,0:T(8,128)} %prev.1, f32[32,32,128]{2,1,0:T(8,128)} %vel.3), custom_call_target="tpu_custom_call" | custom-call | tf_op jit(solution)/shard_map/edges/pallas_call | solution.py:455
  3.0 4.6 %collective-permute-start.2 = (f32[68,32,128]{2,1,0:T(8,128)}, f32[68,32,128]{2,1,0:T(8,128)S(1)}, u32[]{:S(2)}, u32[]{:S(2)}) collective-permute-start(f32[68,32,128]{2,1,0:T(8,128)} %get-tuple-element.18), channel_id=1, source_target_pairs={{0,1},{1,2},{2,3},{3,4},{4,5},{5,6},{6,7},{7,8},{8,9},{9,10},{10,1... | collective-permute-start | bytes 3342344 | tf_op jit(solution)/shard_map/ppermute | solution.py:435
  7.6 1.9 %collective-permute-start.3 = (f32[68,32,128]{2,1,0:T(8,128)}, f32[68,32,128]{2,1,0:T(8,128)S(1)}, u32[]{:S(2)}, u32[]{:S(2)}) collective-permute-start(f32[68,32,128]{2,1,0:T(8,128)} %get-tuple-element.19), channel_id=1, source_target_pairs={{1,0},{2,1},{3,2},{4,3},{5,4},{6,5},{7,6},{8,7},{9,8},{10,9},{11,1... | collective-permute-start | bytes 3342344 | tf_op jit(solution)/shard_map/ppermute | solution.py:435
  9.6 5.9 %prepare.1 = (f32[56,32,128]{2,1,0:T(8,128)}, f32[56,32,128]{2,1,0:T(8,128)}, f32[128,128]{1,0:T(8,128)}, f32[128,128]{1,0:T(8,128)}, s32[2,264]{1,0:T(2,128)}, ...) custom-call(s32[2,256]{1,0:T(2,128)} %rec.1, s32[2,8]{1,0:T(2,128)} %src.1, f32[2,32,32,128]{3,2,1,0:T(8,128)} %now.3, ...), custom_call_target="tpu_custom_call" | custom-call | tf_op jit(solution)/shard_map/prepare/pallas_call | solution.py:466
  15.4 3.6 %collective-permute-start = (f32[56,32,128]{2,1,0:T(8,128)}, f32[56,32,128]{2,1,0:T(8,128)S(1)}, u32[]{:S(2)}, u32[]{:S(2)}) collective-permute-start(f32[56,32,128]{2,1,0:T(8,128)} %get-tuple-element.23), channel_id=1, source_target_pairs={{0,1},{1,2},{2,3},{3,4},{4,5},{5,6},{6,7},{7,8},{8,9},{9,10},{10,1... | collective-permute-start | bytes 2752520 | tf_op jit(solution)/shard_map/ppermute | solution.py:435
  19.1 1.9 %collective-permute-start.1 = (f32[56,32,128]{2,1,0:T(8,128)}, f32[56,32,128]{2,1,0:T(8,128)}, u32[]{:S(2)}, u32[]{:S(2)}) collective-permute-start(f32[56,32,128]{2,1,0:T(8,128)} %get-tuple-element.24), channel_id=1, source_target_pairs={{1,0},{2,1},{3,2},{4,3},{5,4},{6,5},{7,6},{8,7},{9,8},{10,9},{11,1... | collective-permute-start | bytes 2752520 | tf_op jit(solution)/shard_map/ppermute | solution.py:435
  21.0 0.0 collective-permute-done.2.low.vel_low
  21.0 0.0 copy-start
  21.0 3.6 %collective-permute-done.3.high.vel_high = f32[68,32,128]{2,1,0:T(8,128)S(1)} collective-permute-done((f32[68,32,128]{2,1,0:T(8,128)}, f32[68,32,128]{2,1,0:T(8,128)S(1)}, u32[]{:S(2)}, u32[]{:S(2)}) %collective-permute-start.3) | collective-permute-done | bytes 1114144 | tf_op jit(solution)/shard_map/ppermute | solution.py:435
  24.7 0.0 copy-start.1
  24.7 0.0 copy-done
  24.7 1.0 copy-done.1
  25.7 12.7 %forward_steps.1 = (f32[4,2,32,32,128]{4,3,2,1,0:T(8,128)}, f32[384,128]{1,0:T(8,128)}) custom-call(s32[2,264]{1,0:T(2,128)} %get-tuple-element.21.entries, s32[2]{0:T(128)} %get-tuple-element.22.counts, s32[2,16]{1,0:T(2,128)} %get-tuple-element.25.src, s32[2]{0:T(128)} %get-tuple-element.26.src_counts, s32[2,8]{1,0:T(2,128)} %signs.1, f32[2,4]{1,0:T(2,128)} %wave.1, ...), custom_call_target="tpu_custom_call" | custom-call | tf_op jit(solution)/shard_map/forward_steps/pallas_call | solution.py:489
  38.4 6.6 %all-to-all-start = ((f32[16,24,128]{2,1,0:T(8,128)}), f32[16,24,128]{2,1,0:T(8,128)S(1)}, u32[]{:S(2)}, u32[]{:S(2)}) async-start(f32[16,24,128]{2,1,0:T(8,128)} %bitcast.17), calls=%async_computation | async-start | bytes 393216 | tf_op jit(solution)/shard_map/all_to_all | solution.py:507
  44.9 0.0 collective-permute-done.low
  44.9 0.0 copy-start.4
  44.9 0.0 collective-permute-done.1.high
  45.0 6.6 %all-to-all-done = f32[16,24,128]{2,1,0:T(8,128)S(1)} async-done(((f32[16,24,128]{2,1,0:T(8,128)}), f32[16,24,128]{2,1,0:T(8,128)S(1)}, u32[]{:S(2)}, u32[]{:S(2)}) %all-to-all-start) | async-done | bytes 196640 | tf_op jit(solution)/shard_map/all_to_all | solution.py:507
  51.6 0.0 copy-start.3
  51.6 0.0 copy-done.4
  51.6 0.7 copy-done.3
  52.3 13.6 %adjoint_steps.1 = f32[1024,128]{1,0:T(8,128)} custom-call(s32[2,264]{1,0:T(2,128)} %get-tuple-element.21.entries, s32[2]{0:T(128)} %get-tuple-element.22.counts, f32[2,32,32,128]{3,2,1,0:T(8,128)} %now.3, f32[2,32,32,128]{3,2,1,0:T(8,128)} %after.1, f32[32,32,128]{2,1,0:T(8,128)} %vel.3, f32[56,32,128]{2,1,0:T(8,128)} %copy-done.4, ...), custom_call_target="tpu_custom_call" | custom-call | tf_op jit(solution)/shard_map/adjoint_steps/pallas_call | solution.py:509
  65.9 8.5 %all-to-all-start.1 = ((f32[128,8,128]{2,1,0:T(8,128)}), f32[128,8,128]{2,1,0:T(8,128)S(1)}, u32[]{:S(2)}, u32[]{:S(2)}) async-start(f32[128,8,128]{2,1,0:T(8,128)} %bitcast.10), calls=%async_computation.1 | async-start | bytes 1048576 | tf_op jit(solution)/shard_map/all_to_all | solution.py:539
  75.0 2.7 %noise_prior.1.noise = f32[128,128]{1,0:T(8,128)} custom-call(f32[1]{0:T(128)S(6)} %copy.16.step_size, f32[384,128]{1,0:T(8,128)} %bitcast.13, bf16[2,512,512]{2,1,0:T(8,128)(2,1)} %constant.8.clone.operators), custom_call_target="tpu_custom_call" | custom-call | tf_op jit(solution)/shard_map/noise_prior/pallas_call | solution.py:531
  77.7 10.2 %all-to-all-done.1 = f32[128,8,128]{2,1,0:T(8,128)S(1)} async-done(((f32[128,8,128]{2,1,0:T(8,128)}), f32[128,8,128]{2,1,0:T(8,128)S(1)}, u32[]{:S(2)}, u32[]{:S(2)}) %all-to-all-start.1) | async-done | bytes 524320 | tf_op jit(solution)/shard_map/all_to_all | solution.py:539
  87.9 0.0 copy-start.2
  87.9 0.8 copy-done.2
  88.7 3.7 %prior.1 = f32[128,128]{1,0:T(8,128)} custom-call(f32[1]{0:T(128)S(6)} %copy.16.step_size, f32[1024,128]{1,0:T(8,128)} %bitcast.11, f32[128,128]{1,0:T(8,128)} %noise_prior.1.noise, bf16[2,512,512]{2,1,0:T(8,128)(2,1)} %constant.7.clone.operators_in), custom_call_target="tpu_custom_call" | custom-call | tf_op jit(solution)/shard_map/prior/pallas_call | solution.py:540
  92.4 11.0 %all_to_all.15 = f32[16,8,128]{2,1,0:T(8,128)} all-to-all(f32[16,8,128]{2,1,0:T(8,128)} %bitcast.15), channel_id=1, replica_groups=mesh['shot'=8,'dom'=16] {'dom'}, dimensions={0} | all-to-all | bytes 131072 | tf_op jit(solution)/shard_map/all_to_all | solution.py:552
  103.4 1.7 %finish.1 = f32[32,16,32]{2,1,0:T(8,128)} custom-call(f32[128,128]{1,0:T(8,128)} %bitcast.16, f32[128,128]{1,0:T(8,128)} %get-tuple-element.30.velocity), custom_call_target="tpu_custom_call" | custom-call | tf_op jit(solution)/shard_map/finish/pallas_call | solution.py:553
Async XLA Ops:
  3.0 18.0 %collective-permute-start.2 = (f32[68,32,128]{2,1,0:T(8,128)}, f32[68,32,128]{2,1,0:T(8,128)S(1)}, u32[]{:S(2)}, u32[]{:S(2)}) collective-permute-start(f32[68,32,128]{2,1,0:T(8,128)} %get-tuple-element.18), channel_id=1, source_target_pairs={{0,1},{1,2},{2,3},{3,4},{4,5},{5,6},{6,7},{7,8},{8,9},{9,10},{10,1... | collective-permute-start | bytes 3342344 | tf_op jit(solution)/shard_map/ppermute | solution.py:435
  7.6 17.0 %collective-permute-start.3 = (f32[68,32,128]{2,1,0:T(8,128)}, f32[68,32,128]{2,1,0:T(8,128)S(1)}, u32[]{:S(2)}, u32[]{:S(2)}) collective-permute-start(f32[68,32,128]{2,1,0:T(8,128)} %get-tuple-element.19), channel_id=1, source_target_pairs={{1,0},{2,1},{3,2},{4,3},{5,4},{6,5},{7,6},{8,7},{9,8},{10,9},{11,1... | collective-permute-start | bytes 3342344 | tf_op jit(solution)/shard_map/ppermute | solution.py:435
  15.4 29.5 %collective-permute-start = (f32[56,32,128]{2,1,0:T(8,128)}, f32[56,32,128]{2,1,0:T(8,128)S(1)}, u32[]{:S(2)}, u32[]{:S(2)}) collective-permute-start(f32[56,32,128]{2,1,0:T(8,128)} %get-tuple-element.23), channel_id=1, source_target_pairs={{0,1},{1,2},{2,3},{3,4},{4,5},{5,6},{6,7},{7,8},{8,9},{9,10},{10,1... | collective-permute-start | bytes 2752520 | tf_op jit(solution)/shard_map/ppermute | solution.py:435
  19.1 25.9 %collective-permute-start.1 = (f32[56,32,128]{2,1,0:T(8,128)}, f32[56,32,128]{2,1,0:T(8,128)}, u32[]{:S(2)}, u32[]{:S(2)}) collective-permute-start(f32[56,32,128]{2,1,0:T(8,128)} %get-tuple-element.24), channel_id=1, source_target_pairs={{1,0},{2,1},{3,2},{4,3},{5,4},{6,5},{7,6},{8,7},{9,8},{10,9},{11,1... | collective-permute-start | bytes 2752520 | tf_op jit(solution)/shard_map/ppermute | solution.py:435
  21.0 3.6 %copy-start = (f32[68,32,128]{2,1,0:T(8,128)}, f32[68,32,128]{2,1,0:T(8,128)S(1)}, u32[]{:S(2)}) copy-start(f32[68,32,128]{2,1,0:T(8,128)S(1)} %collective-permute-done.2.low.vel_low) | copy-start | bytes 3342340
  24.7 1.0 copy-start.1
  38.4 13.2 %all-to-all-start = ((f32[16,24,128]{2,1,0:T(8,128)}), f32[16,24,128]{2,1,0:T(8,128)S(1)}, u32[]{:S(2)}, u32[]{:S(2)}) async-start(f32[16,24,128]{2,1,0:T(8,128)} %bitcast.17), calls=%async_computation | async-start | bytes 393216 | tf_op jit(solution)/shard_map/all_to_all | solution.py:507
  44.9 6.7 %copy-start.4 = (f32[56,32,128]{2,1,0:T(8,128)}, f32[56,32,128]{2,1,0:T(8,128)S(1)}, u32[]{:S(2)}) copy-start(f32[56,32,128]{2,1,0:T(8,128)S(1)} %collective-permute-done.low) | copy-start | bytes 2752516
  51.6 0.7 copy-start.3
  65.9 22.0 %all-to-all-start.1 = ((f32[128,8,128]{2,1,0:T(8,128)}), f32[128,8,128]{2,1,0:T(8,128)S(1)}, u32[]{:S(2)}, u32[]{:S(2)}) async-start(f32[128,8,128]{2,1,0:T(8,128)} %bitcast.10), calls=%async_computation.1 | async-start | bytes 1048576 | tf_op jit(solution)/shard_map/all_to_all | solution.py:539
  87.9 0.8 copy-start.2

commit v3 on v2

--- a/solution.py
+++ b/solution.py
@@ -25,6 +25,7 @@
 NREC = 256
 LIST = NREC + 8
 CHUNK = 4
+HALVES = 2
 VMEM_LIMIT = 56 * 1024 * 1024
 
 ANY = pl.BlockSpec(memory_space=pl.ANY)
@@ -98,15 +99,14 @@
 
 
 def prepare_kernel(
-    rec, src, deep, shallow, noise, velocity,
-    up, down, noise_out, velocity_out, entries, counts, src_entries, src_counts,
+    rec, src, deep, shallow, noise,
+    up, down, noise_out, entries, counts, src_entries, src_counts,
     turned, sems,
 ):
     copies = started(edge_pairs(deep, shallow, None, up, down), sems)
     list_cells(rec, entries, counts)
     list_cells(src, src_entries, src_counts)
     column_slices(noise, noise_out, turned)
-    column_slices(velocity, velocity_out, turned)
     for copy in copies:
         copy.wait()
 
@@ -148,45 +148,39 @@
             field[shot, :, PAD + NZ : DEPTH, :] = zeros
 
 
-def load_field(field, own, low, high, offset, width, sems, base):
-    copies = []
-    begin = DEEP - width
+def own_pairs(field, own):
+    return [
+        (own.at[shot], field.at[shot, pl.ds(DEEP, SLAB), pl.ds(PAD, NZ), :]) for shot in range(SHOTS_HERE)
+    ]
+
+
+def halo_pairs(field, low, high, offset, width):
+    pairs = []
     for shot in range(SHOTS_HERE):
         planes = pl.ds(offset + shot * width, width)
-        view = field.at[shot]
-        for number, (source, target) in enumerate(
-            (
-                (low.at[planes], view.at[pl.ds(begin, width), pl.ds(PAD, NZ), :]),
-                (own.at[shot], view.at[pl.ds(DEEP, SLAB), pl.ds(PAD, NZ), :]),
-                (high.at[planes], view.at[pl.ds(DEEP + SLAB, width), pl.ds(PAD, NZ), :]),
-            )
-        ):
-            copies.append(pltpu.make_async_copy(source, target, sems.at[base + shot * 3 + number]))
-    return copies
-
-
-def load_speed(speed, own, low, high, offset, sems, base):
-    planes = pl.ds(offset, SHALLOW)
-    return [
-        pltpu.make_async_copy(low.at[planes], speed.at[pl.ds(DEEP - SHALLOW, SHALLOW)], sems.at[base]),
-        pltpu.make_async_copy(own, speed.at[pl.ds(DEEP, SLAB)], sems.at[base + 1]),
-        pltpu.make_async_copy(high.at[planes], speed.at[pl.ds(DEEP + SLAB, SHALLOW)], sems.at[base + 2]),
-    ]
-
-
-def square_speed(speed):
-    @pl.loop(0, (SLAB + 2 * SHALLOW) // 8)
-    def _(part):
-        rows = pl.ds(DEEP - SHALLOW + part * 8, 8)
-        value = speed[rows]
-        speed[rows] = COURANT * value * value
+        for source, begin in ((low, DEEP - width), (high, DEEP + SLAB)):
+            pairs.append((source.at[planes], field.at[shot, pl.ds(begin, width), pl.ds(PAD, NZ), :]))
+    return pairs
+
+
+def place_halo(field, low, high, offset, width):
+    for shot in range(SHOTS_HERE):
+        begin = offset + shot * width
+        field[shot, DEEP - width : DEEP, PAD : PAD + NZ, :] = low[begin : begin + width]
+        field[shot, DEEP + SLAB : DEEP + SLAB + width, PAD : PAD + NZ, :] = high[begin : begin + width]
+
+
+def square_rows(source, start, target, begin, count):
+    for row in range(0, count, 4):
+        value = source[start + row : start + row + 4]
+        target[begin + row : begin + row + 4] = COURANT * value * value
 
 
 def along_lanes(field, lanes, along, margin):
     first, count = DEEP - margin, SLAB + 2 * margin
-    part = count // 2
+    part = count // HALVES
     for shot in range(SHOTS_HERE):
-        for half in range(2):
+        for half in range(HALVES):
             begin = first + half * part
             block = field[shot, begin : begin + part, PAD : PAD + NZ, :].reshape(part * NZ, NY)
             both = dot(jnp.concatenate(split(block), axis=1), lanes[...])
@@ -226,18 +220,26 @@
 def forward_kernel(
     entries, counts, src, src_counts, signs, wave,
     now, prev, vel, low, high, lanes, noise,
-    lap_out, outgoing,
+    lap_out, outgoing, speed_out,
     *scratch,
 ):
     fields = scratch[: STEPS + 2]
     laps, speed, along, samples, sems, out_sems = scratch[STEPS + 2 :]
-    first_copies = load_field(fields[1], now, low, high, 0, DEEP, sems, 0)
-    copies = load_field(fields[0], prev, low, high, 2 * DEEP, SHALLOW, sems, 6)
-    copies += load_speed(speed, vel, low, high, 2 * DEEP + 2 * SHALLOW, sems, 12)
-    for copy in first_copies + copies:
-        copy.start()
+    copies = started(
+        [
+            *own_pairs(fields[1], now),
+            (vel, speed.at[pl.ds(DEEP, SLAB)]),
+            *own_pairs(fields[0], prev),
+        ],
+        sems,
+    )
+    place_halo(fields[1], low, high, 0, DEEP)
+    place_halo(fields[0], low, high, SHOTS_HERE * DEEP, SHALLOW)
+    begin = SHOTS_HERE * (DEEP + SHALLOW)
+    square_rows(low, begin, speed, DEEP - SHALLOW, SHALLOW)
+    square_rows(high, begin, speed, DEEP + SLAB, SHALLOW)
     clear_pads(fields[1 : STEPS + 1])
-    for copy in first_copies:
+    for copy in copies[:2]:
         copy.wait()
     ids = lane_ids()
     outs = []
@@ -245,9 +247,11 @@
         margin = 4 * (STEPS - 1 - moment)
         along_lanes(fields[moment + 1], lanes, along, margin)
         if moment == 0:
-            for copy in copies:
+            for copy in copies[2:]:
                 copy.wait()
-            square_speed(speed)
+            square_rows(speed, DEEP, speed, DEEP, SLAB)
+            outs.append(pltpu.make_async_copy(speed, speed_out, out_sems.at[STEPS]))
+            outs[0].start()
         leap(fields[moment + 1], fields[moment], fields[moment + 2], speed, along, margin, laps, moment)
         out = pltpu.make_async_copy(laps.at[moment, :, pl.ds(DEEP, SLAB)], lap_out.at[moment], out_sems.at[moment])
         out.start()
@@ -292,23 +296,62 @@
         out.wait()
 
 
+def halo_rows(field):
+    pairs = []
+    for shot in range(SHOTS_HERE):
+        for begin in (DEEP - 8, DEEP + SLAB):
+            pairs.append(field.at[shot, pl.ds(begin, 8), pl.ds(PAD, NZ), :])
+    return pairs
+
+
+def adjoint_start_kernel(
+    now, after, speed_in, low, high, lanes, earlier_out, halo_out, field, later, earlier, speed, along, sems
+):
+    copies = started(
+        [
+            *own_pairs(field, now),
+            *halo_pairs(field, low, high, 0, DEEP),
+            *own_pairs(later, after),
+            *halo_pairs(later, low, high, SHOTS_HERE * DEEP, SHALLOW),
+            (speed_in, speed),
+        ],
+        sems,
+    )
+    clear_pads([field])
+    for copy in copies[:6]:
+        copy.wait()
+    margin = 4 * (STEPS - 1)
+    along_lanes(field, lanes, along, margin)
+    for copy in copies[6:]:
+        copy.wait()
+    outs = started([(rows, halo_out.at[place]) for place, rows in enumerate(halo_rows(field))], sems)
+    leap(field, later, earlier, speed, along, margin)
+    out = pltpu.make_async_copy(earlier.at[:, :, pl.ds(PAD, NZ), :], earlier_out, sems.at[4])
+    out.start()
+    for copy in outs:
+        copy.wait()
+    out.wait()
+
+
 def adjoint_kernel(
     entries, counts,
-    now, after, vel, low, high, vel_low, vel_high, laps_in, lanes, incoming, observed,
+    earlier, now, halo, speed_in, vel, laps_in, lanes, incoming, observed,
     tiles,
     *scratch,
 ):
-    fields = scratch[: STEPS + 2]
-    laps, speed, along, plain, differences, misfit, sems = scratch[STEPS + 2 :]
-    first_copies = load_field(fields[1], now, low, high, 0, DEEP, sems, 0)
-    copies = load_field(fields[0], after, low, high, 2 * DEEP, SHALLOW, sems, 6)
-    copies += load_speed(speed, vel, vel_low, vel_high, 2 * DEEP + 2 * SHALLOW, sems, 12)
-    late = [
-        pltpu.make_async_copy(laps_in, laps, sems.at[15]),
-        pltpu.make_async_copy(vel, plain, sems.at[16]),
-    ]
-    for copy in first_copies + copies + late:
-        copy.start()
+    fields = [None, *scratch[: STEPS + 1]]
+    laps, speed, along, plain, differences, misfit, sems = scratch[STEPS + 1 :]
+    copies = started(
+        [
+            (earlier, fields[2].at[:, :, pl.ds(PAD, NZ), :]),
+            *own_pairs(fields[1], now),
+            *[(halo.at[place], rows) for place, rows in enumerate(halo_rows(fields[1]))],
+            (speed_in, speed),
+            (laps_in, laps),
+            (vel, plain),
+        ],
+        sems,
+    )
     total = incoming[8:24, :]
     for block in range(1, 16):
         total = total + incoming[block * 24 + 8 : block * 24 + 24, :]
@@ -319,23 +362,22 @@
             differences[rows, columns] = (
                 total[half * 8 + shot * STEPS : half * 8 + (shot + 1) * STEPS] - observed[shot, :, columns]
             )
-    to_scalars = pltpu.make_async_copy(differences, misfit, sems.at[17])
+    to_scalars = pltpu.make_async_copy(differences, misfit, sems.at[10])
     to_scalars.start()
-    clear_pads(fields[1 : STEPS + 1])
-    for copy in first_copies:
-        copy.wait()
+    clear_pads(fields[2 : STEPS + 1])
     ids = lane_ids()
     for step in range(STEPS):
         moment = STEPS - step
-        margin = 4 * (STEPS - 1 - step)
-        along_lanes(fields[step + 1], lanes, along, margin)
         if step == 0:
-            for copy in copies:
-                copy.wait()
-            square_speed(speed)
-        leap(fields[step + 1], fields[step], fields[step + 2], speed, along, margin)
-        if step == 0:
+            copies[0].wait()
             to_scalars.wait()
+        else:
+            margin = 4 * (STEPS - 1 - step)
+            along_lanes(fields[step + 1], lanes, along, margin)
+            if step == 1:
+                for copy in copies[1:8]:
+                    copy.wait()
+            leap(fields[step + 1], fields[step], fields[step + 2], speed, along, margin)
         for shot in range(SHOTS_HERE):
 
             @pl.loop(0, (counts[shot] + 3) >> 2)
@@ -346,7 +388,7 @@
                     view = fields[step + 2].at[shot, plane, pl.ds(depth, 1), :]
                     view[...] = view[...] + jnp.where(ids == lane, value, 0.0)
 
-    for copy in late:
+    for copy in copies[8:]:
         copy.wait()
     for group in range(SLAB // 4):
         planes = []
@@ -389,21 +431,17 @@
     return result
 
 
-def noise_kernel(step_size, incoming, operators, out):
+def noise_kernel(step_size, incoming, operators, velocity, out, velocity_out, turned):
+    column_slices(velocity, velocity_out, turned)
     columns = jnp.concatenate([incoming[block * 24 : block * 24 + 8, :] for block in range(16)], axis=0)
     scale = jnp.sqrt(jnp.full((8, NY), step_size[0], jnp.float32))[0:1]
     out[...] = scale * apply_prior(columns, operators)
 
 
-def prior_kernel(step_size, received, noise, operators_in, out, parts, operators, sems):
-    count = parts.shape[0]
-    pairs = [(received.at[pl.ds(part * NY, NY)], parts.at[part]) for part in range(count)]
-    copies = started([*pairs, (operators_in, operators)], sems)
-    total = None
-    for part in range(count):
-        copies[part].wait()
-        total = parts[part] if part == 0 else total + parts[part]
-    copies[count].wait()
+def prior_kernel(step_size, received, noise, operators, out):
+    total = received[0:NY, :]
+    for part in range(1, 8):
+        total = total + received[part * NY : (part + 1) * NY, :]
     out[...] = (-0.5 * step_size[0]) * apply_prior(total, operators) + noise[...]
 
 
@@ -418,6 +456,14 @@
 
 def shape(*dims, dtype=jnp.float32):
     return jax.ShapeDtypeStruct(dims, dtype)
+
+
+def pin(values):
+    return pltpu.with_memory_space_constraint(values, pltpu.VMEM)
+
+
+def leave(*values):
+    return [pltpu.with_memory_space_constraint(value, pltpu.HBM) for value in values]
 
 
 def params():
@@ -463,92 +509,103 @@
     low, high = exchange("dom", up, down)
     adjoint_edge, up, down = lax.optimization_barrier((adjoint_now, up, down))
 
-    adj_up, adj_down, noise_tiles, velocity_tiles, *lists = pl.pallas_call(
+    adj_up, adj_down, noise_tiles, *lists = pl.pallas_call(
         prepare_kernel,
         out_shape=(
             *(shape(planes, NZ, NY),) * 2,
-            *(shape(NY, NY),) * 2,
+            shape(NY, NY),
             shape(SHOTS_HERE, LIST, dtype=jnp.int32),
             shape(SHOTS_HERE, dtype=jnp.int32),
             shape(SHOTS_HERE, 16, dtype=jnp.int32),
             shape(SHOTS_HERE, dtype=jnp.int32),
         ),
-        in_specs=[SMEM] * 2 + [ANY] * 2 + [VMEM] * 2,
-        out_specs=(VMEM,) * 4 + (SMEM,) * 4,
+        in_specs=[SMEM] * 2 + [ANY] * 2 + [VMEM],
+        out_specs=(VMEM,) * 3 + (SMEM,) * 4,
         scratch_shapes=[pltpu.VMEM((NY, NY), jnp.float32), pltpu.SemaphoreType.DMA((8,))],
         name="prepare",
     )(
         record_cells, source_cells, adjoint_edge, adjoint_next,
-        noise_field.reshape(SLAB * NZ, NY), velocity.reshape(SLAB * NZ, NY),
+        noise_field.reshape(SLAB * NZ, NY),
     )
     adj_low, adj_high = exchange("dom", adj_up, adj_down)
 
     fields = [pltpu.VMEM((SHOTS_HERE, ROWS, DEPTH, NY), jnp.float32)] * (STEPS + 2)
     speed = pltpu.VMEM((ROWS, NZ, NY), jnp.float32)
     along = pltpu.VMEM((SHOTS_HERE, ROWS, NZ, NY), jnp.float32)
-    laplacians, outgoing = pl.pallas_call(
+    laplacians, outgoing, speed_sq = pl.pallas_call(
         forward_kernel,
-        out_shape=(shape(STEPS, SHOTS_HERE, SLAB, NZ, NY), shape(16 * 24, NY)),
-        in_specs=[SMEM] * 6 + [ANY] * 5 + [VMEM] * 2,
-        out_specs=(ANY, VMEM),
+        out_shape=(
+            shape(STEPS, SHOTS_HERE, SLAB, NZ, NY), shape(16 * 24, NY), shape(ROWS, NZ, NY),
+        ),
+        in_specs=[SMEM] * 6 + [ANY] * 3 + [VMEM] * 4,
+        out_specs=(ANY, VMEM, ANY),
         scratch_shapes=[
             *fields,
             pltpu.VMEM((STEPS, SHOTS_HERE, ROWS, NZ, NY), jnp.float32),
             speed,
             along,
             pltpu.VMEM((16, NY), jnp.float32),
-            pltpu.SemaphoreType.DMA((15,)),
-            pltpu.SemaphoreType.DMA((STEPS,)),
+            pltpu.SemaphoreType.DMA((5,)),
+            pltpu.SemaphoreType.DMA((STEPS + 1,)),
         ],
         compiler_params=params(),
         name="forward_steps",
-    )(*lists, source_signs, wavelet, field_now, field_prev, velocity, low, high, lanes, noise_tiles)
+    )(
+        *leave(*lists, source_signs, wavelet, field_now, field_prev, velocity),
+        pin(low), pin(high), *leave(lanes, noise_tiles),
+    )
 
     incoming = lax.all_to_all(outgoing.reshape(16, 24, NY), "dom", 0, 0, tiled=True).reshape(16 * 24, NY)
 
+    field = fields[0]
+    earlier, halo = pl.pallas_call(
+        adjoint_start_kernel,
+        out_shape=(shape(SHOTS_HERE, ROWS, NZ, NY), shape(SHOTS_HERE * 2, 8, NZ, NY)),
+        in_specs=[ANY] * 5 + [VMEM],
+        out_specs=(ANY,) * 2,
+        scratch_shapes=[field, field, field, speed, along, pltpu.SemaphoreType.DMA((13,))],
+        compiler_params=params(),
+        name="adjoint_start",
+    )(*leave(adjoint_now, adjoint_next, speed_sq), pin(adj_low), pin(adj_high), *leave(lanes))
     tiles = pl.pallas_call(
         adjoint_kernel,
         out_shape=shape(SLAB * NZ, NY),
-        in_specs=[SMEM] * 2 + [ANY] * 8 + [VMEM] * 3,
+        in_specs=[SMEM] * 2 + [ANY] * 6 + [VMEM] * 3,
         out_specs=VMEM,
         scratch_shapes=[
-            *fields,
+            *[field] * (STEPS + 1),
             pltpu.VMEM((STEPS, SHOTS_HERE, SLAB, NZ, NY), jnp.float32),
             speed,
             along,
             pltpu.VMEM((SLAB, NZ, NY), jnp.float32),
             pltpu.VMEM((SHOTS_HERE * STEPS, NREC), jnp.float32),
             pltpu.SMEM((SHOTS_HERE * STEPS, NREC), jnp.float32),
-            pltpu.SemaphoreType.DMA((18,)),
+            pltpu.SemaphoreType.DMA((11,)),
         ],
         compiler_params=params(),
         name="adjoint_steps",
     )(
-        *lists[:2], adjoint_now, adjoint_next, velocity, adj_low, adj_high, low, high, laplacians,
-        lanes, incoming, observed,
-    )
-
-    noise_update = pl.pallas_call(
+        *leave(*lists[:2], earlier, adjoint_now, halo, speed_sq, velocity, laplacians, lanes),
+        pin(incoming), *leave(observed),
+    )
+
+    noise_update, velocity_tiles = pl.pallas_call(
         noise_kernel,
-        out_shape=shape(NY, NY),
-        in_specs=[SMEM, VMEM, VMEM],
-        out_specs=VMEM,
+        out_shape=(shape(NY, NY),) * 2,
+        in_specs=[SMEM] + [VMEM] * 3,
+        out_specs=(VMEM,) * 2,
+        scratch_shapes=[pltpu.VMEM((NY, NY), jnp.float32)],
         name="noise_prior",
-    )(step_size, incoming, single)
+    )(step_size, pin(incoming), single, velocity.reshape(SLAB * NZ, NY))
 
     received = lax.all_to_all(tiles.reshape(128, 8, NY), ("shot", "dom"), 0, 0, tiled=True)
     update = pl.pallas_call(
         prior_kernel,
         out_shape=shape(NY, NY),
-        in_specs=[SMEM, ANY, VMEM, ANY],
+        in_specs=[SMEM, VMEM, VMEM, VMEM],
         out_specs=VMEM,
-        scratch_shapes=[
-            pltpu.VMEM((8, NY, NY), jnp.float32),
-            pltpu.VMEM(squared.shape, jnp.bfloat16),
-            pltpu.SemaphoreType.DMA((9,)),
-        ],
         name="prior",
-    )(step_size, received.reshape(128 * 8, NY), noise_update, squared)
+    )(step_size, pin(received.reshape(128 * 8, NY)), *leave(noise_update), pin(squared))
     returned = lax.all_to_all(update.reshape(16, 8, NY), "dom", 0, 0, tiled=True)
     out = pl.pallas_call(
         finish_kernel,

time: 106 us -> 100 us (0.943)
  waiting for transfers between devices: 20.5 us -> 14.5 us
  local copies, waits for them, and re-layouts: 2.49 us -> 0.01 us
  starting transfers between devices: 27.1 us -> 28.8 us
    all_to_all x1, waiting for transfers between devices: 6.63 us -> 0.38 us  [body(): lax.all_to_all(outgoing.reshape(16, 24, NY), 'dom', 0, 0, tiled=True)]
    pallas_call x2 -> x3, Pallas kernels: 6.4 us -> 11.1 us  [the longest x1 6.25 us: body(): pl.pallas_call(adjoint_start_kernel, out_shape=(shape(SHOTS_HERE, ROWS, N...]
    pallas_call x1, Pallas kernels: 13.6 us -> 10.9 us  [body(): pl.pallas_call(adjoint_kernel, out_shape=shape(SLAB * NZ, NY), in_specs=[...]
    unnamed x10 -> x2, local copies, waits for them, and re-layouts: 2.49 us -> 0.01 us
  transfers between devices with their start and end apart: 6 -> 6, of which waited for: 3 -> 3; matrix products, arithmetic and copies ran while one was open for 0% -> 0% of each run, Pallas kernels for 20% -> 27%
where the time goes in v3:
time: 100 us; the launch traced here: 99.4 us
  Pallas kernels  44.2 us (44%)
  starting transfers between devices  28.8 us (29%)
  waiting for transfers between devices  14.5 us (14%)
  blocking collectives  10.9 us (11%)
    ppermute x4, starting transfers between devices, exchange(): return (lax.ppermute(to_high, axis, up), lax.ppermute(to_low, axis, down))  12.1 us
    pallas_call x1, Pallas kernels, body(): pl.pallas_call(forward_kernel, out_shape=(shape(STEPS, SHOTS_HERE, SLAB,...  12.1 us
    all_to_all x1, blocking collectives, body(): lax.all_to_all(update.reshape(16, 8, NY), 'dom', 0, 0, tiled=True)  10.9 us
    pallas_call x1, Pallas kernels, body(): pl.pallas_call(adjoint_kernel, out_shape=shape(SLAB * NZ, NY), in_specs=[...  10.9 us
    all_to_all x1, waiting for transfers between devices, body(): lax.all_to_all(tiles.reshape(128, 8, NY), ('shot', 'dom'), 0, 0, tiled=True)  10.1 us
    all_to_all x1, starting transfers between devices, body(): lax.all_to_all(tiles.reshape(128, 8, NY), ('shot', 'dom'), 0, 0, tiled=True)  9.53 us
    all_to_all x1, starting transfers between devices, body(): lax.all_to_all(outgoing.reshape(16, 24, NY), 'dom', 0, 0, tiled=True)  7.22 us
    pallas_call x1, Pallas kernels, body(): pl.pallas_call(adjoint_start_kernel, out_shape=(shape(SHOTS_HERE, ROWS, N...  6.25 us
  transfers between devices with their start and end apart: 6, of which 3 were waited for; matrix products, arithmetic and copies ran while one was open for 0% of the time, Pallas kernels for 27%

profile of v3, /device:TPU:1, one launch (start us, length us, event | category | flops | bytes accessed | tf_op | source)
XLA Modules:
  0.0 99.4 jit_solution(18306903234724825624)
XLA Ops:
  0.0 3.0 %edges.1 = (f32[68,32,128]{2,1,0:T(8,128)}, f32[68,32,128]{2,1,0:T(8,128)}) custom-call(f32[2,32,32,128]{3,2,1,0:T(8,128)} %now.3, f32[2,32,32,128]{3,2,1,0:T(8,128)} %prev.1, f32[32,32,128]{2,1,0:T(8,128)} %vel.3), custom_call_target="tpu_custom_call" | custom-call | tf_op jit(solution)/shard_map/edges/pallas_call | solution.py:501
  3.0 4.6 %collective-permute-start = (f32[68,32,128]{2,1,0:T(8,128)}, f32[68,32,128]{2,1,0:T(8,128)S(1)}, u32[]{:S(2)}, u32[]{:S(2)}) collective-permute-start(f32[68,32,128]{2,1,0:T(8,128)} %get-tuple-element.22), channel_id=1, source_target_pairs={{0,1},{1,2},{2,3},{3,4},{4,5},{5,6},{6,7},{7,8},{8,9},{9,10},{10,1... | collective-permute-start | bytes 3342344 | tf_op jit(solution)/shard_map/ppermute | solution.py:481
  7.6 1.9 %collective-permute-start.1 = (f32[68,32,128]{2,1,0:T(8,128)}, f32[68,32,128]{2,1,0:T(8,128)S(1)}, u32[]{:S(2)}, u32[]{:S(2)}) collective-permute-start(f32[68,32,128]{2,1,0:T(8,128)} %get-tuple-element.23), channel_id=1, source_target_pairs={{1,0},{2,1},{3,2},{4,3},{5,4},{6,5},{7,6},{8,7},{9,8},{10,9},{11,1... | collective-permute-start | bytes 3342344 | tf_op jit(solution)/shard_map/ppermute | solution.py:481
  9.6 5.4 %prepare.1 = (f32[56,32,128]{2,1,0:T(8,128)}, f32[56,32,128]{2,1,0:T(8,128)}, f32[128,128]{1,0:T(8,128)}, s32[2,264]{1,0:T(2,128)}, s32[2]{0:T(128)}, /*index=5*/s32[2,16]{1,0:T(2,128)}, s32[2]{0:T(128)}) custom-call(s32[2,256]{1,0:T(2,128)} %rec.1, s32[2,8]{1,0:T(2,128)} %src.1, f32[2,32,32,128]{3,2,1,0:T(8,128)} %now.5, f32[2,32,32,128]{3,2,1,0:T(8,128)} %after.1, ...), custom_call_target="tpu_custom_call" | custom-call | tf_op jit(solution)/shard_map/prepare/pallas_call | solution.py:512
  15.0 3.6 %collective-permute-start.2 = (f32[56,32,128]{2,1,0:T(8,128)}, f32[56,32,128]{2,1,0:T(8,128)S(1)}, u32[]{:S(2)}, u32[]{:S(2)}) collective-permute-start(f32[56,32,128]{2,1,0:T(8,128)} %get-tuple-element.31), channel_id=1, source_target_pairs={{0,1},{1,2},{2,3},{3,4},{4,5},{5,6},{6,7},{7,8},{8,9},{9,10},{10,1... | collective-permute-start | bytes 2752520 | tf_op jit(solution)/shard_map/ppermute | solution.py:481
  18.7 1.9 %collective-permute-start.3 = (f32[56,32,128]{2,1,0:T(8,128)}, f32[56,32,128]{2,1,0:T(8,128)}, u32[]{:S(2)}, u32[]{:S(2)}) collective-permute-start(f32[56,32,128]{2,1,0:T(8,128)} %get-tuple-element.32), channel_id=1, source_target_pairs={{1,0},{2,1},{3,2},{4,3},{5,4},{6,5},{7,6},{8,7},{9,8},{10,9},{11,1... | collective-permute-start | bytes 2752520 | tf_op jit(solution)/shard_map/ppermute | solution.py:481
  20.6 0.0 collective-permute-done.low
  20.6 4.1 %collective-permute-done.1.high = f32[68,32,128]{2,1,0:T(8,128)S(1)} collective-permute-done((f32[68,32,128]{2,1,0:T(8,128)}, f32[68,32,128]{2,1,0:T(8,128)S(1)}, u32[]{:S(2)}, u32[]{:S(2)}) %collective-permute-start.1) | collective-permute-done | bytes 1114144 | tf_op jit(solution)/shard_map/ppermute | solution.py:481
  24.7 12.1 %forward_steps.1 = (f32[4,2,32,32,128]{4,3,2,1,0:T(8,128)}, f32[384,128]{1,0:T(8,128)}, f32[64,32,128]{2,1,0:T(8,128)}) custom-call(s32[2,264]{1,0:T(2,128)} %get-tuple-element.25.entries, s32[2]{0:T(128)} %get-tuple-element.26.counts, s32[2,16]{1,0:T(2,128)} %get-tuple-element.27.src, s32[2]{0:T(128)} %get-tuple-element.28.src_counts, s32[2,8]{1,0:T(2,128)} %signs.1, ...), custom_call_target="tpu_custom_call" | custom-call | tf_op jit(solution)/shard_map/forward_steps/pallas_call | solution.py:535
  36.8 7.2 %all-to-all-start = ((f32[16,24,128]{2,1,0:T(8,128)}), f32[16,24,128]{2,1,0:T(8,128)S(1)}, u32[]{:S(2)}, u32[]{:S(2)}) async-start(f32[16,24,128]{2,1,0:T(8,128)} %bitcast.17), calls=%async_computation | async-start | bytes 393216 | tf_op jit(solution)/shard_map/all_to_all | solution.py:558
  44.0 0.0 collective-permute-done.2.low
  44.0 0.0 collective-permute-done.3.high
  44.0 6.2 %adjoint_start.1 = (f32[2,64,32,128]{3,2,1,0:T(8,128)}, f32[4,8,32,128]{3,2,1,0:T(8,128)}) custom-call(f32[2,32,32,128]{3,2,1,0:T(8,128)} %now.5, f32[2,32,32,128]{3,2,1,0:T(8,128)} %after.1, f32[64,32,128]{2,1,0:T(8,128)} %get-tuple-element.30.speed_in, f32[56,32,128]{2,1,0:T(8,128)S(1)} %collective-permute-done.2.low, ...), custom_call_target="tpu_custom_call" | custom-call | tf_op jit(solution)/shard_map/adjoint_start/pallas_call | solution.py:561
  50.2 0.4 all-to-all-done
  50.6 10.9 %adjoint_steps.1 = f32[1024,128]{1,0:T(8,128)} custom-call(s32[2,264]{1,0:T(2,128)} %get-tuple-element.25.entries, s32[2]{0:T(128)} %get-tuple-element.26.counts, f32[2,64,32,128]{3,2,1,0:T(8,128)} %get-tuple-element.33.earlier, f32[2,32,32,128]{3,2,1,0:T(8,128)} %now.5, f32[4,8,32,128]{3,2,1,0:T(8,128)} %get-tuple-element.34.halo, ...), custom_call_target="tpu_custom_call" | custom-call | tf_op jit(solution)/shard_map/adjoint_steps/pallas_call | solution.py:570
  61.5 9.5 %all-to-all-start.1 = ((f32[128,8,128]{2,1,0:T(8,128)}), f32[128,8,128]{2,1,0:T(8,128)S(1)}, u32[]{:S(2)}, u32[]{:S(2)}) async-start(f32[128,8,128]{2,1,0:T(8,128)} %bitcast.13), calls=%async_computation.1 | async-start | bytes 1048576 | tf_op jit(solution)/shard_map/all_to_all | solution.py:601
  71.1 0.0 copy-start
  71.8 2.7 %noise_prior.1 = (f32[128,128]{1,0:T(8,128)}, f32[128,128]{1,0:T(8,128)}) custom-call(f32[1]{0:T(128)S(6)} %copy.16.step_size, f32[384,128]{1,0:T(8,128)S(1)} %bitcast.11, bf16[2,512,512]{2,1,0:T(8,128)(2,1)} %constant.8.clone.operators, f32[1024,128]{1,0:T(8,128)} %bitcast.12), custom_call_target="tpu_custom_call" | custom-call | tf_op jit(solution)/shard_map/noise_prior/pallas_call | solution.py:592
  74.5 10.1 %all-to-all-done.1 = f32[128,8,128]{2,1,0:T(8,128)S(1)} async-done(((f32[128,8,128]{2,1,0:T(8,128)}), f32[128,8,128]{2,1,0:T(8,128)S(1)}, u32[]{:S(2)}, u32[]{:S(2)}) %all-to-all-start.1) | async-done | bytes 524320 | tf_op jit(solution)/shard_map/all_to_all | solution.py:601
  84.6 0.0 copy-done
  84.6 2.2 %prior.1 = f32[128,128]{1,0:T(8,128)} custom-call(f32[1]{0:T(128)S(6)} %copy.16.step_size, f32[1024,128]{1,0:T(8,128)S(1)} %bitcast.9, f32[128,128]{1,0:T(8,128)} %get-tuple-element.37.noise, bf16[2,512,512]{2,1,0:T(8,128)(2,1)S(1)} %copy-done), custom_call_target="tpu_custom_call" | custom-call | tf_op jit(solution)/shard_map/prior/pallas_call | solution.py:602
  86.8 10.9 %all_to_all.15 = f32[16,8,128]{2,1,0:T(8,128)} all-to-all(f32[16,8,128]{2,1,0:T(8,128)} %bitcast.15), channel_id=1, replica_groups=mesh['shot'=8,'dom'=16] {'dom'}, dimensions={0} | all-to-all | bytes 131072 | tf_op jit(solution)/shard_map/all_to_all | solution.py:609
  97.7 1.7 %finish.1 = f32[32,16,32]{2,1,0:T(8,128)} custom-call(f32[128,128]{1,0:T(8,128)} %bitcast.16, f32[128,128]{1,0:T(8,128)} %get-tuple-element.38.velocity), custom_call_target="tpu_custom_call" | custom-call | tf_op jit(solution)/shard_map/finish/pallas_call | solution.py:610
Async XLA Ops:
  3.0 17.6 %collective-permute-start = (f32[68,32,128]{2,1,0:T(8,128)}, f32[68,32,128]{2,1,0:T(8,128)S(1)}, u32[]{:S(2)}, u32[]{:S(2)}) collective-permute-start(f32[68,32,128]{2,1,0:T(8,128)} %get-tuple-element.22), channel_id=1, source_target_pairs={{0,1},{1,2},{2,3},{3,4},{4,5},{5,6},{6,7},{7,8},{8,9},{9,10},{10,1... | collective-permute-start | bytes 3342344 | tf_op jit(solution)/shard_map/ppermute | solution.py:481
  7.6 17.0 %collective-permute-start.1 = (f32[68,32,128]{2,1,0:T(8,128)}, f32[68,32,128]{2,1,0:T(8,128)S(1)}, u32[]{:S(2)}, u32[]{:S(2)}) collective-permute-start(f32[68,32,128]{2,1,0:T(8,128)} %get-tuple-element.23), channel_id=1, source_target_pairs={{1,0},{2,1},{3,2},{4,3},{5,4},{6,5},{7,6},{8,7},{9,8},{10,9},{11,1... | collective-permute-start | bytes 3342344 | tf_op jit(solution)/shard_map/ppermute | solution.py:481
  15.0 29.0 %collective-permute-start.2 = (f32[56,32,128]{2,1,0:T(8,128)}, f32[56,32,128]{2,1,0:T(8,128)S(1)}, u32[]{:S(2)}, u32[]{:S(2)}) collective-permute-start(f32[56,32,128]{2,1,0:T(8,128)} %get-tuple-element.31), channel_id=1, source_target_pairs={{0,1},{1,2},{2,3},{3,4},{4,5},{5,6},{6,7},{7,8},{8,9},{9,10},{10,1... | collective-permute-start | bytes 2752520 | tf_op jit(solution)/shard_map/ppermute | solution.py:481
  18.7 25.3 %collective-permute-start.3 = (f32[56,32,128]{2,1,0:T(8,128)}, f32[56,32,128]{2,1,0:T(8,128)}, u32[]{:S(2)}, u32[]{:S(2)}) collective-permute-start(f32[56,32,128]{2,1,0:T(8,128)} %get-tuple-element.32), channel_id=1, source_target_pairs={{1,0},{2,1},{3,2},{4,3},{5,4},{6,5},{7,6},{8,7},{9,8},{10,9},{11,1... | collective-permute-start | bytes 2752520 | tf_op jit(solution)/shard_map/ppermute | solution.py:481
  36.8 13.9 %all-to-all-start = ((f32[16,24,128]{2,1,0:T(8,128)}), f32[16,24,128]{2,1,0:T(8,128)S(1)}, u32[]{:S(2)}, u32[]{:S(2)}) async-start(f32[16,24,128]{2,1,0:T(8,128)} %bitcast.17), calls=%async_computation | async-start | bytes 393216 | tf_op jit(solution)/shard_map/all_to_all | solution.py:558
  61.5 23.1 %all-to-all-start.1 = ((f32[128,8,128]{2,1,0:T(8,128)}), f32[128,8,128]{2,1,0:T(8,128)S(1)}, u32[]{:S(2)}, u32[]{:S(2)}) async-start(f32[128,8,128]{2,1,0:T(8,128)} %bitcast.13), calls=%async_computation.1 | async-start | bytes 1048576 | tf_op jit(solution)/shard_map/all_to_all | solution.py:601
  71.1 13.5 %copy-start = (bf16[2,512,512]{2,1,0:T(8,128)(2,1)S(1)}, bf16[2,512,512]{2,1,0:T(8,128)(2,1)}, u32[]{:S(2)}) copy-start(bf16[2,512,512]{2,1,0:T(8,128)(2,1)} %constant.7.clone.operators) | copy-start | bytes 3145732

commit v4 on v3

--- a/solution.py
+++ b/solution.py
@@ -24,8 +24,8 @@
 SHOTS_HERE = 2
 NREC = 256
 LIST = NREC + 8
-CHUNK = 4
-HALVES = 2
+CHUNK = 8
+HALVES = 1
 VMEM_LIMIT = 56 * 1024 * 1024
 
 ANY = pl.BlockSpec(memory_space=pl.ANY)
@@ -93,17 +93,30 @@
     return copies
 
 
-def edge_kernel(deep, shallow, velocity, up, down, sems):
-    for copy in started(edge_pairs(deep, shallow, velocity, up, down), sems):
+def stage_edges(deep, shallow, velocity, up, down, staged, sems):
+    inward = started(edge_pairs(deep, shallow, velocity, *staged), sems.at[0])
+    targets = edge_pairs(deep, shallow, velocity, up, down)
+    sources = edge_pairs(deep, shallow, velocity, *staged)
+    outward = []
+    for number, copy in enumerate(inward):
+        copy.wait()
+        out = pltpu.make_async_copy(sources[number][1], targets[number][1], sems.at[1, number])
+        out.start()
+        outward.append(out)
+    return outward
+
+
+def edge_kernel(deep, shallow, velocity, up, down, high, low, sems):
+    for copy in stage_edges(deep, shallow, velocity, up, down, (high, low), sems):
         copy.wait()
 
 
 def prepare_kernel(
     rec, src, deep, shallow, noise,
     up, down, noise_out, entries, counts, src_entries, src_counts,
-    turned, sems,
+    turned, high, low, sems,
 ):
-    copies = started(edge_pairs(deep, shallow, None, up, down), sems)
+    copies = stage_edges(deep, shallow, None, up, down, (high, low), sems)
     list_cells(rec, entries, counts)
     list_cells(src, src_entries, src_counts)
     column_slices(noise, noise_out, turned)
@@ -132,12 +145,10 @@
 
 
 def unpack_entry(entry):
-    filler = entry < 0
-    cell = jnp.where(filler, 0, entry >> 8)
-    plane = (cell >> 12) + (DEEP - SHALLOW)
-    depth = PAD + ((cell >> 7) & (NZ - 1))
-    lane = jnp.where(filler, -1, cell & (NY - 1))
-    return plane, depth, lane, jnp.where(filler, 0, entry & (NREC - 1))
+    plane = (entry >> 20) + (DEEP - SHALLOW)
+    depth = PAD + ((entry >> 15) & (NZ - 1))
+    lane = ((entry >> 8) & (NY - 1)) | (entry >> 31)
+    return plane, depth, lane, entry & (NREC - 1)
 
 
 def clear_pads(fields):
@@ -502,8 +513,11 @@
         edge_kernel,
         out_shape=(shape(planes + SHALLOW, NZ, NY),) * 2,
         in_specs=[ANY] * 3,
-        out_specs=(VMEM,) * 2,
-        scratch_shapes=[pltpu.SemaphoreType.DMA((10,))],
+        out_specs=(ANY,) * 2,
+        scratch_shapes=[
+            *[pltpu.VMEM((planes + SHALLOW, NZ, NY), jnp.float32)] * 2,
+            pltpu.SemaphoreType.DMA((2, 10)),
+        ],
         name="edges",
     )(field_now, field_prev, velocity)
     low, high = exchange("dom", up, down)
@@ -520,8 +534,12 @@
             shape(SHOTS_HERE, dtype=jnp.int32),
         ),
         in_specs=[SMEM] * 2 + [ANY] * 2 + [VMEM],
-        out_specs=(VMEM,) * 3 + (SMEM,) * 4,
-        scratch_shapes=[pltpu.VMEM((NY, NY), jnp.float32), pltpu.SemaphoreType.DMA((8,))],
+        out_specs=(ANY,) * 2 + (VMEM,) + (SMEM,) * 4,
+        scratch_shapes=[
+            pltpu.VMEM((NY, NY), jnp.float32),
+            *[pltpu.VMEM((planes, NZ, NY), jnp.float32)] * 2,
+            pltpu.SemaphoreType.DMA((2, 8)),
+        ],
         name="prepare",
     )(
         record_cells, source_cells, adjoint_edge, adjoint_next,

time: 100 us -> 98.9 us (0.989)
  starting transfers between devices: 28.8 us -> 27.8 us
  transfers between devices with their start and end apart: 6 -> 6, of which waited for: 3 -> 3; matrix products, arithmetic and copies ran while one was open for 0% -> 0% of each run, Pallas kernels for 27% -> 28%
where the time goes in v4:
time: 98.9 us; the launch traced here: 98.1 us
  Pallas kernels  44.5 us (45%)
  starting transfers between devices  27.8 us (28%)
  waiting for transfers between devices  14.1 us (14%)
  blocking collectives  10.9 us (11%)
    pallas_call x1, Pallas kernels, body(): pl.pallas_call(forward_kernel, out_shape=(shape(STEPS, SHOTS_HERE, SLAB,...  12.2 us
    ppermute x4, starting transfers between devices, exchange(): return (lax.ppermute(to_high, axis, up), lax.ppermute(to_low, axis, down))  12.1 us
    pallas_call x1, Pallas kernels, body(): pl.pallas_call(adjoint_kernel, out_shape=shape(SLAB * NZ, NY), in_specs=[...  11 us
    all_to_all x1, blocking collectives, body(): lax.all_to_all(update.reshape(16, 8, NY), 'dom', 0, 0, tiled=True)  10.9 us
    all_to_all x1, waiting for transfers between devices, body(): lax.all_to_all(tiles.reshape(128, 8, NY), ('shot', 'dom'), 0, 0, tiled=True)  10.1 us
    all_to_all x1, starting transfers between devices, body(): lax.all_to_all(tiles.reshape(128, 8, NY), ('shot', 'dom'), 0, 0, tiled=True)  9.32 us
    all_to_all x1, starting transfers between devices, body(): lax.all_to_all(outgoing.reshape(16, 24, NY), 'dom', 0, 0, tiled=True)  6.4 us
    pallas_call x1, Pallas kernels, body(): pl.pallas_call(adjoint_start_kernel, out_shape=(shape(SHOTS_HERE, ROWS, N...  6.19 us
  transfers between devices with their start and end apart: 6, of which 3 were waited for; matrix products, arithmetic and copies ran while one was open for 0% of the time, Pallas kernels for 28%

profile of v4, /device:TPU:1, one launch (start us, length us, event | category | flops | bytes accessed | tf_op | source)
XLA Modules:
  0.0 98.1 jit_solution(2167386944619566436)
XLA Ops:
  0.0 2.5 %edges.1 = (f32[68,32,128]{2,1,0:T(8,128)}, f32[68,32,128]{2,1,0:T(8,128)}) custom-call(f32[2,32,32,128]{3,2,1,0:T(8,128)} %now.3, f32[2,32,32,128]{3,2,1,0:T(8,128)} %prev.1, f32[32,32,128]{2,1,0:T(8,128)} %vel.3), custom_call_target="tpu_custom_call" | custom-call | tf_op jit(solution)/shard_map/edges/pallas_call | solution.py:512
  2.5 4.6 %collective-permute-start = (f32[68,32,128]{2,1,0:T(8,128)}, f32[68,32,128]{2,1,0:T(8,128)S(1)}, u32[]{:S(2)}, u32[]{:S(2)}) collective-permute-start(f32[68,32,128]{2,1,0:T(8,128)} %get-tuple-element.22), channel_id=1, source_target_pairs={{0,1},{1,2},{2,3},{3,4},{4,5},{5,6},{6,7},{7,8},{8,9},{9,10},{10,1... | collective-permute-start | bytes 3342344 | tf_op jit(solution)/shard_map/ppermute | solution.py:492
  7.1 1.9 %collective-permute-start.1 = (f32[68,32,128]{2,1,0:T(8,128)}, f32[68,32,128]{2,1,0:T(8,128)S(1)}, u32[]{:S(2)}, u32[]{:S(2)}) collective-permute-start(f32[68,32,128]{2,1,0:T(8,128)} %get-tuple-element.23), channel_id=1, source_target_pairs={{1,0},{2,1},{3,2},{4,3},{5,4},{6,5},{7,6},{8,7},{9,8},{10,9},{11,1... | collective-permute-start | bytes 3342344 | tf_op jit(solution)/shard_map/ppermute | solution.py:492
  9.1 6.0 %prepare.1 = (f32[56,32,128]{2,1,0:T(8,128)}, f32[56,32,128]{2,1,0:T(8,128)}, f32[128,128]{1,0:T(8,128)}, s32[2,264]{1,0:T(2,128)}, s32[2]{0:T(128)}, /*index=5*/s32[2,16]{1,0:T(2,128)}, s32[2]{0:T(128)}) custom-call(s32[2,256]{1,0:T(2,128)} %rec.1, s32[2,8]{1,0:T(2,128)} %src.1, f32[2,32,32,128]{3,2,1,0:T(8,128)} %now.5, f32[2,32,32,128]{3,2,1,0:T(8,128)} %after.1, ...), custom_call_target="tpu_custom_call" | custom-call | tf_op jit(solution)/shard_map/prepare/pallas_call | solution.py:526
  15.0 3.6 %collective-permute-start.2 = (f32[56,32,128]{2,1,0:T(8,128)}, f32[56,32,128]{2,1,0:T(8,128)S(1)}, u32[]{:S(2)}, u32[]{:S(2)}) collective-permute-start(f32[56,32,128]{2,1,0:T(8,128)} %get-tuple-element.31), channel_id=1, source_target_pairs={{0,1},{1,2},{2,3},{3,4},{4,5},{5,6},{6,7},{7,8},{8,9},{9,10},{10,1... | collective-permute-start | bytes 2752520 | tf_op jit(solution)/shard_map/ppermute | solution.py:492
  18.7 1.9 %collective-permute-start.3 = (f32[56,32,128]{2,1,0:T(8,128)}, f32[56,32,128]{2,1,0:T(8,128)}, u32[]{:S(2)}, u32[]{:S(2)}) collective-permute-start(f32[56,32,128]{2,1,0:T(8,128)} %get-tuple-element.32), channel_id=1, source_target_pairs={{1,0},{2,1},{3,2},{4,3},{5,4},{6,5},{7,6},{8,7},{9,8},{10,9},{11,1... | collective-permute-start | bytes 2752520 | tf_op jit(solution)/shard_map/ppermute | solution.py:492
  20.6 0.0 collective-permute-done.low
  20.6 3.5 %collective-permute-done.1.high = f32[68,32,128]{2,1,0:T(8,128)S(1)} collective-permute-done((f32[68,32,128]{2,1,0:T(8,128)}, f32[68,32,128]{2,1,0:T(8,128)S(1)}, u32[]{:S(2)}, u32[]{:S(2)}) %collective-permute-start.1) | collective-permute-done | bytes 1114144 | tf_op jit(solution)/shard_map/ppermute | solution.py:492
  24.2 12.2 %forward_steps.1 = (f32[4,2,32,32,128]{4,3,2,1,0:T(8,128)}, f32[384,128]{1,0:T(8,128)}, f32[64,32,128]{2,1,0:T(8,128)}) custom-call(s32[2,264]{1,0:T(2,128)} %get-tuple-element.25.entries, s32[2]{0:T(128)} %get-tuple-element.26.counts, s32[2,16]{1,0:T(2,128)} %get-tuple-element.27.src, s32[2]{0:T(128)} %get-tuple-element.28.src_counts, s32[2,8]{1,0:T(2,128)} %signs.1, ...), custom_call_target="tpu_custom_call" | custom-call | tf_op jit(solution)/shard_map/forward_steps/pallas_call | solution.py:553
  36.4 6.4 %all-to-all-start = ((f32[16,24,128]{2,1,0:T(8,128)}), f32[16,24,128]{2,1,0:T(8,128)S(1)}, u32[]{:S(2)}, u32[]{:S(2)}) async-start(f32[16,24,128]{2,1,0:T(8,128)} %bitcast.17), calls=%async_computation | async-start | bytes 393216 | tf_op jit(solution)/shard_map/all_to_all | solution.py:576
  42.8 0.0 collective-permute-done.2.low
  42.8 0.0 collective-permute-done.3.high
  42.8 6.2 %adjoint_start.1 = (f32[2,64,32,128]{3,2,1,0:T(8,128)}, f32[4,8,32,128]{3,2,1,0:T(8,128)}) custom-call(f32[2,32,32,128]{3,2,1,0:T(8,128)} %now.5, f32[2,32,32,128]{3,2,1,0:T(8,128)} %after.1, f32[64,32,128]{2,1,0:T(8,128)} %get-tuple-element.30.speed_in, f32[56,32,128]{2,1,0:T(8,128)S(1)} %collective-permute-done.2.low, ...), custom_call_target="tpu_custom_call" | custom-call | tf_op jit(solution)/shard_map/adjoint_start/pallas_call | solution.py:579
  49.0 0.4 all-to-all-done
  49.4 11.0 %adjoint_steps.1 = f32[1024,128]{1,0:T(8,128)} custom-call(s32[2,264]{1,0:T(2,128)} %get-tuple-element.25.entries, s32[2]{0:T(128)} %get-tuple-element.26.counts, f32[2,64,32,128]{3,2,1,0:T(8,128)} %get-tuple-element.33.earlier, f32[2,32,32,128]{3,2,1,0:T(8,128)} %now.5, f32[4,8,32,128]{3,2,1,0:T(8,128)} %get-tuple-element.34.halo, ...), custom_call_target="tpu_custom_call" | custom-call | tf_op jit(solution)/shard_map/adjoint_steps/pallas_call | solution.py:588
  60.5 9.3 %all-to-all-start.1 = ((f32[128,8,128]{2,1,0:T(8,128)}), f32[128,8,128]{2,1,0:T(8,128)S(1)}, u32[]{:S(2)}, u32[]{:S(2)}) async-start(f32[128,8,128]{2,1,0:T(8,128)} %bitcast.13), calls=%async_computation.1 | async-start | bytes 1048576 | tf_op jit(solution)/shard_map/all_to_all | solution.py:619
  69.8 0.0 copy-start
  70.5 2.7 %noise_prior.1 = (f32[128,128]{1,0:T(8,128)}, f32[128,128]{1,0:T(8,128)}) custom-call(f32[1]{0:T(128)S(6)} %copy.16.step_size, f32[384,128]{1,0:T(8,128)S(1)} %bitcast.11, bf16[2,512,512]{2,1,0:T(8,128)(2,1)} %constant.8.clone.operators, f32[1024,128]{1,0:T(8,128)} %bitcast.12), custom_call_target="tpu_custom_call" | custom-call | tf_op jit(solution)/shard_map/noise_prior/pallas_call | solution.py:610
  73.2 10.1 %all-to-all-done.1 = f32[128,8,128]{2,1,0:T(8,128)S(1)} async-done(((f32[128,8,128]{2,1,0:T(8,128)}), f32[128,8,128]{2,1,0:T(8,128)S(1)}, u32[]{:S(2)}, u32[]{:S(2)}) %all-to-all-start.1) | async-done | bytes 524320 | tf_op jit(solution)/shard_map/all_to_all | solution.py:619
  83.3 0.0 copy-done
  83.3 2.2 %prior.1 = f32[128,128]{1,0:T(8,128)} custom-call(f32[1]{0:T(128)S(6)} %copy.16.step_size, f32[1024,128]{1,0:T(8,128)S(1)} %bitcast.9, f32[128,128]{1,0:T(8,128)} %get-tuple-element.37.noise, bf16[2,512,512]{2,1,0:T(8,128)(2,1)S(1)} %copy-done), custom_call_target="tpu_custom_call" | custom-call | tf_op jit(solution)/shard_map/prior/pallas_call | solution.py:620
  85.5 10.9 %all_to_all.15 = f32[16,8,128]{2,1,0:T(8,128)} all-to-all(f32[16,8,128]{2,1,0:T(8,128)} %bitcast.15), channel_id=1, replica_groups=mesh['shot'=8,'dom'=16] {'dom'}, dimensions={0} | all-to-all | bytes 131072 | tf_op jit(solution)/shard_map/all_to_all | solution.py:627
  96.5 1.7 %finish.1 = f32[32,16,32]{2,1,0:T(8,128)} custom-call(f32[128,128]{1,0:T(8,128)} %bitcast.16, f32[128,128]{1,0:T(8,128)} %get-tuple-element.38.velocity), custom_call_target="tpu_custom_call" | custom-call | tf_op jit(solution)/shard_map/finish/pallas_call | solution.py:628
Async XLA Ops:
  2.5 18.1 %collective-permute-start = (f32[68,32,128]{2,1,0:T(8,128)}, f32[68,32,128]{2,1,0:T(8,128)S(1)}, u32[]{:S(2)}, u32[]{:S(2)}) collective-permute-start(f32[68,32,128]{2,1,0:T(8,128)} %get-tuple-element.22), channel_id=1, source_target_pairs={{0,1},{1,2},{2,3},{3,4},{4,5},{5,6},{6,7},{7,8},{8,9},{9,10},{10,1... | collective-permute-start | bytes 3342344 | tf_op jit(solution)/shard_map/ppermute | solution.py:492
  7.1 17.0 %collective-permute-start.1 = (f32[68,32,128]{2,1,0:T(8,128)}, f32[68,32,128]{2,1,0:T(8,128)S(1)}, u32[]{:S(2)}, u32[]{:S(2)}) collective-permute-start(f32[68,32,128]{2,1,0:T(8,128)} %get-tuple-element.23), channel_id=1, source_target_pairs={{1,0},{2,1},{3,2},{4,3},{5,4},{6,5},{7,6},{8,7},{9,8},{10,9},{11,1... | collective-permute-start | bytes 3342344 | tf_op jit(solution)/shard_map/ppermute | solution.py:492
  15.0 27.8 %collective-permute-start.2 = (f32[56,32,128]{2,1,0:T(8,128)}, f32[56,32,128]{2,1,0:T(8,128)S(1)}, u32[]{:S(2)}, u32[]{:S(2)}) collective-permute-start(f32[56,32,128]{2,1,0:T(8,128)} %get-tuple-element.31), channel_id=1, source_target_pairs={{0,1},{1,2},{2,3},{3,4},{4,5},{5,6},{6,7},{7,8},{8,9},{9,10},{10,1... | collective-permute-start | bytes 2752520 | tf_op jit(solution)/shard_map/ppermute | solution.py:492
  18.7 24.1 %collective-permute-start.3 = (f32[56,32,128]{2,1,0:T(8,128)}, f32[56,32,128]{2,1,0:T(8,128)}, u32[]{:S(2)}, u32[]{:S(2)}) collective-permute-start(f32[56,32,128]{2,1,0:T(8,128)} %get-tuple-element.32), channel_id=1, source_target_pairs={{1,0},{2,1},{3,2},{4,3},{5,4},{6,5},{7,6},{8,7},{9,8},{10,9},{11,1... | collective-permute-start | bytes 2752520 | tf_op jit(solution)/shard_map/ppermute | solution.py:492
  36.4 13.1 %all-to-all-start = ((f32[16,24,128]{2,1,0:T(8,128)}), f32[16,24,128]{2,1,0:T(8,128)S(1)}, u32[]{:S(2)}, u32[]{:S(2)}) async-start(f32[16,24,128]{2,1,0:T(8,128)} %bitcast.17), calls=%async_computation | async-start | bytes 393216 | tf_op jit(solution)/shard_map/all_to_all | solution.py:576
  60.5 22.8 %all-to-all-start.1 = ((f32[128,8,128]{2,1,0:T(8,128)}), f32[128,8,128]{2,1,0:T(8,128)S(1)}, u32[]{:S(2)}, u32[]{:S(2)}) async-start(f32[128,8,128]{2,1,0:T(8,128)} %bitcast.13), calls=%async_computation.1 | async-start | bytes 1048576 | tf_op jit(solution)/shard_map/all_to_all | solution.py:619
  69.8 13.5 %copy-start = (bf16[2,512,512]{2,1,0:T(8,128)(2,1)S(1)}, bf16[2,512,512]{2,1,0:T(8,128)(2,1)}, u32[]{:S(2)}) copy-start(bf16[2,512,512]{2,1,0:T(8,128)(2,1)} %constant.7.clone.operators) | copy-start | bytes 3145732

commit v5 on v4

--- a/solution.py
+++ b/solution.py
@@ -113,11 +113,11 @@
 
 def prepare_kernel(
     rec, src, deep, shallow, noise,
-    up, down, noise_out, entries, counts, src_entries, src_counts,
+    up, down, noise_out, own, own_count, halo, halo_count, src_entries, src_counts,
     turned, high, low, sems,
 ):
     copies = stage_edges(deep, shallow, None, up, down, (high, low), sems)
-    list_cells(rec, entries, counts)
+    list_receivers(rec, own, own_count, halo, halo_count)
     list_cells(src, src_entries, src_counts)
     column_slices(noise, noise_out, turned)
     for copy in copies:
@@ -142,6 +142,33 @@
         for extra in range(4):
             entries[shot, counts[shot] + extra] = -1
         count_out[shot] = counts[shot]
+
+
+def list_receivers(cells, own, own_count, halo, halo_count):
+    base = (lax.axis_index("dom") * SLAB - SHALLOW) * (NZ * NY)
+    begin, end = SHALLOW * NZ * NY, (SHALLOW + SLAB) * NZ * NY
+    span = (SLAB + 2 * SHALLOW) * NZ * NY
+
+    def gather(item, counts):
+        following = []
+        for shot in range(SHOTS_HERE):
+            first, second = counts[2 * shot], counts[2 * shot + 1]
+            cell = cells[shot, item] - base
+            entry = (cell << 8) | item
+            own[shot, first] = entry
+            halo[shot, second] = entry
+            mine = ((cell >= begin) & (cell < end)).astype(jnp.int32)
+            inside = ((cell >= 0) & (cell < span)).astype(jnp.int32)
+            following += [first + mine, second + (inside - mine)]
+        return tuple(following)
+
+    counts = lax.fori_loop(0, cells.shape[1], gather, (jnp.int32(0),) * (2 * SHOTS_HERE), unroll=8)
+    for shot in range(SHOTS_HERE):
+        for number, (entries, count_out) in enumerate(((own, own_count), (halo, halo_count))):
+            count = counts[2 * shot + number]
+            for extra in range(4):
+                entries[shot, count + extra] = -1
+            count_out[shot] = count
 
 
 def unpack_entry(entry):
@@ -282,9 +309,8 @@
             state = list(state)
             for member in range(4):
                 plane, depth, lane, which = unpack_entry(entries[shot, group * 4 + member])
-                own = (lane >= 0) & (plane >= DEEP) & (plane < DEEP + SLAB)
                 shift = (which - lane) & (NY - 1)
-                hits = [ids == jnp.where(own, which - half * NY, -1) for half in range(2)]
+                hits = [ids == jnp.where(lane >= 0, which - half * NY, -1) for half in range(2)]
                 for moment in range(STEPS):
                     line = fields[moment + 2][shot, plane, pl.ds(depth, 1), :]
                     line = pltpu.roll(line, shift, 1)
@@ -345,7 +371,7 @@
 
 
 def adjoint_kernel(
-    entries, counts,
+    own, own_count, beyond, beyond_count,
     earlier, now, halo, speed_in, vel, laps_in, lanes, incoming, observed,
     tiles,
     *scratch,
@@ -389,15 +415,16 @@
                 for copy in copies[1:8]:
                     copy.wait()
             leap(fields[step + 1], fields[step], fields[step + 2], speed, along, margin)
-        for shot in range(SHOTS_HERE):
-
-            @pl.loop(0, (counts[shot] + 3) >> 2)
-            def _(group, shot=shot):
-                for member in range(4):
-                    plane, depth, lane, which = unpack_entry(entries[shot, group * 4 + member])
-                    value = misfit[shot * STEPS + moment - 1, which]
-                    view = fields[step + 2].at[shot, plane, pl.ds(depth, 1), :]
-                    view[...] = view[...] + jnp.where(ids == lane, value, 0.0)
+        for entries, counts in ((own, own_count), (beyond, beyond_count))[: 2 if step < STEPS - 1 else 1]:
+            for shot in range(SHOTS_HERE):
+
+                @pl.loop(0, (counts[shot] + 3) >> 2)
+                def _(group, entries=entries, shot=shot):
+                    for member in range(4):
+                        plane, depth, lane, which = unpack_entry(entries[shot, group * 4 + member])
+                        value = misfit[shot * STEPS + moment - 1, which]
+                        view = fields[step + 2].at[shot, plane, pl.ds(depth, 1), :]
+                        view[...] = view[...] + jnp.where(ids == lane, value, 0.0)
 
     for copy in copies[8:]:
         copy.wait()
@@ -528,13 +555,12 @@
         out_shape=(
             *(shape(planes, NZ, NY),) * 2,
             shape(NY, NY),
-            shape(SHOTS_HERE, LIST, dtype=jnp.int32),
-            shape(SHOTS_HERE, dtype=jnp.int32),
+            *(shape(SHOTS_HERE, LIST, dtype=jnp.int32), shape(SHOTS_HERE, dtype=jnp.int32)) * 2,
             shape(SHOTS_HERE, 16, dtype=jnp.int32),
             shape(SHOTS_HERE, dtype=jnp.int32),
         ),
         in_specs=[SMEM] * 2 + [ANY] * 2 + [VMEM],
-        out_specs=(ANY,) * 2 + (VMEM,) + (SMEM,) * 4,
+        out_specs=(ANY,) * 2 + (VMEM,) + (SMEM,) * 6,
         scratch_shapes=[
             pltpu.VMEM((NY, NY), jnp.float32),
             *[pltpu.VMEM((planes, NZ, NY), jnp.float32)] * 2,
@@ -569,7 +595,7 @@
         compiler_params=params(),
         name="forward_steps",
     )(
-        *leave(*lists, source_signs, wavelet, field_now, field_prev, velocity),
+        *leave(*lists[:2], *lists[4:], source_signs, wavelet, field_now, field_prev, velocity),
         pin(low), pin(high), *leave(lanes, noise_tiles),
     )
 
@@ -588,7 +614,7 @@
     tiles = pl.pallas_call(
         adjoint_kernel,
         out_shape=shape(SLAB * NZ, NY),
-        in_specs=[SMEM] * 2 + [ANY] * 6 + [VMEM] * 3,
+        in_specs=[SMEM] * 4 + [ANY] * 6 + [VMEM] * 3,
         out_specs=VMEM,
         scratch_shapes=[
             *[field] * (STEPS + 1),
@@ -603,7 +629,7 @@
         compiler_params=params(),
         name="adjoint_steps",
     )(
-        *leave(*lists[:2], earlier, adjoint_now, halo, speed_sq, velocity, laplacians, lanes),
+        *leave(*lists[:4], earlier, adjoint_now, halo, speed_sq, velocity, laplacians, lanes),
         pin(incoming), *leave(observed),
     )
 

time: 98.9 us -> 98.6 us (level)
  waiting for transfers between devices: 14.1 us -> 12.2 us
    pallas_call x1, Pallas kernels: 5.96 us -> 7.81 us  [body(): pl.pallas_call(prepare_kernel, out_shape=(*(shape(planes, NZ, NY),) * 2,...]
    ppermute x4, waiting for transfers between devices: 3.55 us -> 1.71 us  [exchange(): return (lax.ppermute(to_high, axis, up), lax.ppermute(to_low, axis, down))]
  transfers between devices with their start and end apart: 6 -> 6, of which waited for: 3 -> 3; matrix products, arithmetic and copies ran while one was open for 0% -> 0% of each run, Pallas kernels for 28% -> 29%
where the time goes in v5:
time: 98.6 us; the launch traced here: 97.8 us
  Pallas kernels  45.4 us (46%)
  starting transfers between devices  28.4 us (29%)
  waiting for transfers between devices  12.2 us (12%)
  blocking collectives  10.9 us (11%)
    ppermute x4, starting transfers between devices, exchange(): return (lax.ppermute(to_high, axis, up), lax.ppermute(to_low, axis, down))  12.1 us
    pallas_call x1, Pallas kernels, body(): pl.pallas_call(forward_kernel, out_shape=(shape(STEPS, SHOTS_HERE, SLAB,...  11.6 us
    all_to_all x1, blocking collectives, body(): lax.all_to_all(update.reshape(16, 8, NY), 'dom', 0, 0, tiled=True)  10.9 us
    pallas_call x1, Pallas kernels, body(): pl.pallas_call(adjoint_kernel, out_shape=shape(SLAB * NZ, NY), in_specs=[...  10.7 us
    all_to_all x1, waiting for transfers between devices, body(): lax.all_to_all(tiles.reshape(128, 8, NY), ('shot', 'dom'), 0, 0, tiled=True)  10.1 us
    all_to_all x1, starting transfers between devices, body(): lax.all_to_all(tiles.reshape(128, 8, NY), ('shot', 'dom'), 0, 0, tiled=True)  9.69 us
    pallas_call x1, Pallas kernels, body(): pl.pallas_call(prepare_kernel, out_shape=(*(shape(planes, NZ, NY),) * 2,...  7.81 us
    all_to_all x1, starting transfers between devices, body(): lax.all_to_all(outgoing.reshape(16, 24, NY), 'dom', 0, 0, tiled=True)  6.6 us
  transfers between devices with their start and end apart: 6, of which 3 were waited for; matrix products, arithmetic and copies ran while one was open for 0% of the time, Pallas kernels for 29%

profile of v5, /device:TPU:1, one launch (start us, length us, event | category | flops | bytes accessed | tf_op | source)
XLA Modules:
  0.0 97.8 jit_solution(4138178689499116826)
XLA Ops:
  0.0 2.5 %edges.1 = (f32[68,32,128]{2,1,0:T(8,128)}, f32[68,32,128]{2,1,0:T(8,128)}) custom-call(f32[2,32,32,128]{3,2,1,0:T(8,128)} %now.3, f32[2,32,32,128]{3,2,1,0:T(8,128)} %prev.1, f32[32,32,128]{2,1,0:T(8,128)} %vel.3), custom_call_target="tpu_custom_call" | custom-call | tf_op jit(solution)/shard_map/edges/pallas_call | solution.py:539
  2.5 4.6 %collective-permute-start = (f32[68,32,128]{2,1,0:T(8,128)}, f32[68,32,128]{2,1,0:T(8,128)S(1)}, u32[]{:S(2)}, u32[]{:S(2)}) collective-permute-start(f32[68,32,128]{2,1,0:T(8,128)} %get-tuple-element.24), channel_id=1, source_target_pairs={{0,1},{1,2},{2,3},{3,4},{4,5},{5,6},{6,7},{7,8},{8,9},{9,10},{10,1... | collective-permute-start | bytes 3342344 | tf_op jit(solution)/shard_map/ppermute | solution.py:519
  7.1 1.9 %collective-permute-start.1 = (f32[68,32,128]{2,1,0:T(8,128)}, f32[68,32,128]{2,1,0:T(8,128)S(1)}, u32[]{:S(2)}, u32[]{:S(2)}) collective-permute-start(f32[68,32,128]{2,1,0:T(8,128)} %get-tuple-element.25), channel_id=1, source_target_pairs={{1,0},{2,1},{3,2},{4,3},{5,4},{6,5},{7,6},{8,7},{9,8},{10,9},{11,1... | collective-permute-start | bytes 3342344 | tf_op jit(solution)/shard_map/ppermute | solution.py:519
  9.1 7.8 %prepare.1 = (f32[56,32,128]{2,1,0:T(8,128)}, f32[56,32,128]{2,1,0:T(8,128)}, f32[128,128]{1,0:T(8,128)}, s32[2,264]{1,0:T(2,128)}, s32[2]{0:T(128)}, /*index=5*...) custom-call(s32[2,256]{1,0:T(2,128)} %rec.1, s32[2,8]{1,0:T(2,128)} %src.1, f32[2,32,32,128]{3,2,1,0:T(8,128)} %now.5, ...), custom_call_target="tpu_custom_call" | custom-call | tf_op jit(solution)/shard_map/prepare/pallas_call | solution.py:553
  16.9 3.6 %collective-permute-start.2 = (f32[56,32,128]{2,1,0:T(8,128)}, f32[56,32,128]{2,1,0:T(8,128)S(1)}, u32[]{:S(2)}, u32[]{:S(2)}) collective-permute-start(f32[56,32,128]{2,1,0:T(8,128)} %get-tuple-element.35), channel_id=1, source_target_pairs={{0,1},{1,2},{2,3},{3,4},{4,5},{5,6},{6,7},{7,8},{8,9},{9,10},{10,1... | collective-permute-start | bytes 2752520 | tf_op jit(solution)/shard_map/ppermute | solution.py:519
  20.5 1.9 %collective-permute-start.3 = (f32[56,32,128]{2,1,0:T(8,128)}, f32[56,32,128]{2,1,0:T(8,128)}, u32[]{:S(2)}, u32[]{:S(2)}) collective-permute-start(f32[56,32,128]{2,1,0:T(8,128)} %get-tuple-element.36), channel_id=1, source_target_pairs={{1,0},{2,1},{3,2},{4,3},{5,4},{6,5},{7,6},{8,7},{9,8},{10,9},{11,1... | collective-permute-start | bytes 2752520 | tf_op jit(solution)/shard_map/ppermute | solution.py:519
  22.5 0.0 collective-permute-done.low
  22.5 1.7 %collective-permute-done.1.high = f32[68,32,128]{2,1,0:T(8,128)S(1)} collective-permute-done((f32[68,32,128]{2,1,0:T(8,128)}, f32[68,32,128]{2,1,0:T(8,128)S(1)}, u32[]{:S(2)}, u32[]{:S(2)}) %collective-permute-start.1) | collective-permute-done | bytes 1114144 | tf_op jit(solution)/shard_map/ppermute | solution.py:519
  24.2 11.6 %forward_steps.1 = (f32[4,2,32,32,128]{4,3,2,1,0:T(8,128)}, f32[384,128]{1,0:T(8,128)}, f32[64,32,128]{2,1,0:T(8,128)}) custom-call(s32[2,264]{1,0:T(2,128)} %get-tuple-element.27.entries.own, s32[2]{0:T(128)} %get-tuple-element.28.counts.own_count, s32[2,16]{1,0:T(2,128)} %get-tuple-element.31.src, s32[2]{0:T(128)} %get-tuple-element.32.src_counts, ...), custom_call_target="tpu_custom_call" | custom-call | tf_op jit(solution)/shard_map/forward_steps/pallas_call | solution.py:579
  35.8 6.6 %all-to-all-start = ((f32[16,24,128]{2,1,0:T(8,128)}), f32[16,24,128]{2,1,0:T(8,128)S(1)}, u32[]{:S(2)}, u32[]{:S(2)}) async-start(f32[16,24,128]{2,1,0:T(8,128)} %bitcast.17), calls=%async_computation | async-start | bytes 393216 | tf_op jit(solution)/shard_map/all_to_all | solution.py:602
  42.4 0.0 collective-permute-done.2.low
  42.4 0.0 collective-permute-done.3.high
  42.4 6.2 %adjoint_start.1 = (f32[2,64,32,128]{3,2,1,0:T(8,128)}, f32[4,8,32,128]{3,2,1,0:T(8,128)}) custom-call(f32[2,32,32,128]{3,2,1,0:T(8,128)} %now.5, f32[2,32,32,128]{3,2,1,0:T(8,128)} %after.1, f32[64,32,128]{2,1,0:T(8,128)} %get-tuple-element.34.speed_in, f32[56,32,128]{2,1,0:T(8,128)S(1)} %collective-permute-done.2.low, ...), custom_call_target="tpu_custom_call" | custom-call | tf_op jit(solution)/shard_map/adjoint_start/pallas_call | solution.py:605
  48.6 0.4 all-to-all-done
  49.0 10.7 %adjoint_steps.1 = f32[1024,128]{1,0:T(8,128)} custom-call(s32[2,264]{1,0:T(2,128)} %get-tuple-element.27.entries.own, s32[2]{0:T(128)} %get-tuple-element.28.counts.own_count, s32[2,264]{1,0:T(2,128)} %get-tuple-element.29.beyond, s32[2]{0:T(128)} %get-tuple-element.30.beyond_count, f32[2,64,32,128]{3,2,1,0:T(8,128)} %get-tuple-element.37.earlier, ...), custom_call_target="tpu_custom_call" | custom-call | tf_op jit(solution)/shard_map/adjoint_steps/pallas_call | solution.py:614
  59.8 9.7 %all-to-all-start.1 = ((f32[128,8,128]{2,1,0:T(8,128)}), f32[128,8,128]{2,1,0:T(8,128)S(1)}, u32[]{:S(2)}, u32[]{:S(2)}) async-start(f32[128,8,128]{2,1,0:T(8,128)} %bitcast.13), calls=%async_computation.1 | async-start | bytes 1048576 | tf_op jit(solution)/shard_map/all_to_all | solution.py:645
  69.5 0.0 copy-start
  70.2 2.7 %noise_prior.1 = (f32[128,128]{1,0:T(8,128)}, f32[128,128]{1,0:T(8,128)}) custom-call(f32[1]{0:T(128)S(6)} %copy.16.step_size, f32[384,128]{1,0:T(8,128)S(1)} %bitcast.11, bf16[2,512,512]{2,1,0:T(8,128)(2,1)} %constant.8.clone.operators, f32[1024,128]{1,0:T(8,128)} %bitcast.12), custom_call_target="tpu_custom_call" | custom-call | tf_op jit(solution)/shard_map/noise_prior/pallas_call | solution.py:636
  72.9 10.1 %all-to-all-done.1 = f32[128,8,128]{2,1,0:T(8,128)S(1)} async-done(((f32[128,8,128]{2,1,0:T(8,128)}), f32[128,8,128]{2,1,0:T(8,128)S(1)}, u32[]{:S(2)}, u32[]{:S(2)}) %all-to-all-start.1) | async-done | bytes 524320 | tf_op jit(solution)/shard_map/all_to_all | solution.py:645
  83.0 0.0 copy-done
  83.0 2.2 %prior.1 = f32[128,128]{1,0:T(8,128)} custom-call(f32[1]{0:T(128)S(6)} %copy.16.step_size, f32[1024,128]{1,0:T(8,128)S(1)} %bitcast.9, f32[128,128]{1,0:T(8,128)} %get-tuple-element.41.noise, bf16[2,512,512]{2,1,0:T(8,128)(2,1)S(1)} %copy-done), custom_call_target="tpu_custom_call" | custom-call | tf_op jit(solution)/shard_map/prior/pallas_call | solution.py:646
  85.2 10.9 %all_to_all.15 = f32[16,8,128]{2,1,0:T(8,128)} all-to-all(f32[16,8,128]{2,1,0:T(8,128)} %bitcast.15), channel_id=1, replica_groups=mesh['shot'=8,'dom'=16] {'dom'}, dimensions={0} | all-to-all | bytes 131072 | tf_op jit(solution)/shard_map/all_to_all | solution.py:653
  96.1 1.7 %finish.1 = f32[32,16,32]{2,1,0:T(8,128)} custom-call(f32[128,128]{1,0:T(8,128)} %bitcast.16, f32[128,128]{1,0:T(8,128)} %get-tuple-element.42.velocity), custom_call_target="tpu_custom_call" | custom-call | tf_op jit(solution)/shard_map/finish/pallas_call | solution.py:654
Async XLA Ops:
  2.5 19.9 %collective-permute-start = (f32[68,32,128]{2,1,0:T(8,128)}, f32[68,32,128]{2,1,0:T(8,128)S(1)}, u32[]{:S(2)}, u32[]{:S(2)}) collective-permute-start(f32[68,32,128]{2,1,0:T(8,128)} %get-tuple-element.24), channel_id=1, source_target_pairs={{0,1},{1,2},{2,3},{3,4},{4,5},{5,6},{6,7},{7,8},{8,9},{9,10},{10,1... | collective-permute-start | bytes 3342344 | tf_op jit(solution)/shard_map/ppermute | solution.py:519
  7.1 17.0 %collective-permute-start.1 = (f32[68,32,128]{2,1,0:T(8,128)}, f32[68,32,128]{2,1,0:T(8,128)S(1)}, u32[]{:S(2)}, u32[]{:S(2)}) collective-permute-start(f32[68,32,128]{2,1,0:T(8,128)} %get-tuple-element.25), channel_id=1, source_target_pairs={{1,0},{2,1},{3,2},{4,3},{5,4},{6,5},{7,6},{8,7},{9,8},{10,9},{11,1... | collective-permute-start | bytes 3342344 | tf_op jit(solution)/shard_map/ppermute | solution.py:519
  16.9 25.5 %collective-permute-start.2 = (f32[56,32,128]{2,1,0:T(8,128)}, f32[56,32,128]{2,1,0:T(8,128)S(1)}, u32[]{:S(2)}, u32[]{:S(2)}) collective-permute-start(f32[56,32,128]{2,1,0:T(8,128)} %get-tuple-element.35), channel_id=1, source_target_pairs={{0,1},{1,2},{2,3},{3,4},{4,5},{5,6},{6,7},{7,8},{8,9},{9,10},{10,1... | collective-permute-start | bytes 2752520 | tf_op jit(solution)/shard_map/ppermute | solution.py:519
  20.5 21.9 %collective-permute-start.3 = (f32[56,32,128]{2,1,0:T(8,128)}, f32[56,32,128]{2,1,0:T(8,128)}, u32[]{:S(2)}, u32[]{:S(2)}) collective-permute-start(f32[56,32,128]{2,1,0:T(8,128)} %get-tuple-element.36), channel_id=1, source_target_pairs={{1,0},{2,1},{3,2},{4,3},{5,4},{6,5},{7,6},{8,7},{9,8},{10,9},{11,1... | collective-permute-start | bytes 2752520 | tf_op jit(solution)/shard_map/ppermute | solution.py:519
  35.8 13.3 %all-to-all-start = ((f32[16,24,128]{2,1,0:T(8,128)}), f32[16,24,128]{2,1,0:T(8,128)S(1)}, u32[]{:S(2)}, u32[]{:S(2)}) async-start(f32[16,24,128]{2,1,0:T(8,128)} %bitcast.17), calls=%async_computation | async-start | bytes 393216 | tf_op jit(solution)/shard_map/all_to_all | solution.py:602
  59.8 23.2 %all-to-all-start.1 = ((f32[128,8,128]{2,1,0:T(8,128)}), f32[128,8,128]{2,1,0:T(8,128)S(1)}, u32[]{:S(2)}, u32[]{:S(2)}) async-start(f32[128,8,128]{2,1,0:T(8,128)} %bitcast.13), calls=%async_computation.1 | async-start | bytes 1048576 | tf_op jit(solution)/shard_map/all_to_all | solution.py:645
  69.5 13.5 %copy-start = (bf16[2,512,512]{2,1,0:T(8,128)(2,1)S(1)}, bf16[2,512,512]{2,1,0:T(8,128)(2,1)}, u32[]{:S(2)}) copy-start(bf16[2,512,512]{2,1,0:T(8,128)(2,1)} %constant.7.clone.operators) | copy-start | bytes 3145732

commit v6 on v5

--- a/solution.py
+++ b/solution.py
@@ -225,10 +225,10 @@
             along[shot, begin : begin + part] = (both[:, :NY] + both[:, NY:]).reshape(part, NZ, NY)
 
 
-def leap(field, before, after, speed, along, margin, laplacians=None, slot=None):
+def leap(field, before, after, speed, along, margin, laplacians=None, slot=None, chunks=None):
     first = DEEP - margin
 
-    @pl.loop(0, (SLAB + 2 * margin) // CHUNK)
+    @pl.loop(*(chunks or (0, (SLAB + 2 * margin) // CHUNK)))
     def _(chunk):
         for plane in range(CHUNK):
             here = first + chunk * CHUNK + plane
@@ -362,12 +362,15 @@
     for copy in copies[6:]:
         copy.wait()
     outs = started([(rows, halo_out.at[place]) for place, rows in enumerate(halo_rows(field))], sems)
-    leap(field, later, earlier, speed, along, margin)
-    out = pltpu.make_async_copy(earlier.at[:, :, pl.ds(PAD, NZ), :], earlier_out, sems.at[4])
-    out.start()
+    for number, chunks in enumerate(((0, 3), (3, 5), (5, 7))):
+        leap(field, later, earlier, speed, along, margin, chunks=chunks)
+        rows = pl.ds(DEEP - margin + chunks[0] * CHUNK, (chunks[1] - chunks[0]) * CHUNK)
+        source = earlier.at[:, rows, pl.ds(PAD, NZ), :]
+        out = pltpu.make_async_copy(source, earlier_out.at[:, rows], sems.at[4 + number])
+        out.start()
+        outs.append(out)
     for copy in outs:
         copy.wait()
-    out.wait()
 
 
 def adjoint_kernel(
@@ -380,7 +383,10 @@
     laps, speed, along, plain, differences, misfit, sems = scratch[STEPS + 1 :]
     copies = started(
         [
-            (earlier, fields[2].at[:, :, pl.ds(PAD, NZ), :]),
+            (
+                earlier.at[:, pl.ds(DEEP - SHALLOW, SLAB + 2 * SHALLOW)],
+                fields[2].at[:, pl.ds(DEEP - SHALLOW, SLAB + 2 * SHALLOW), pl.ds(PAD, NZ), :],
+            ),
             *own_pairs(fields[1], now),
             *[(halo.at[place], rows) for place, rows in enumerate(halo_rows(fields[1]))],
             (speed_in, speed),

time: 98.6 us -> 97.9 us (level)
  no operation moved by 1% of the time
where the time goes in v6:
time: 97.9 us; the launch traced here: 97.2 us
  Pallas kernels  44.9 us (46%)
  starting transfers between devices  27.7 us (28%)
  waiting for transfers between devices  12.8 us (13%)
  blocking collectives  10.9 us (11%)
    ppermute x4, starting transfers between devices, exchange(): return (lax.ppermute(to_high, axis, up), lax.ppermute(to_low, axis, down))  12.1 us
    pallas_call x1, Pallas kernels, body(): pl.pallas_call(forward_kernel, out_shape=(shape(STEPS, SHOTS_HERE, SLAB,...  11.6 us
    all_to_all x1, blocking collectives, body(): lax.all_to_all(update.reshape(16, 8, NY), 'dom', 0, 0, tiled=True)  10.9 us
    pallas_call x1, Pallas kernels, body(): pl.pallas_call(adjoint_kernel, out_shape=shape(SLAB * NZ, NY), in_specs=[...  10.8 us
    all_to_all x1, waiting for transfers between devices, body(): lax.all_to_all(tiles.reshape(128, 8, NY), ('shot', 'dom'), 0, 0, tiled=True)  10.1 us
    all_to_all x1, starting transfers between devices, body(): lax.all_to_all(tiles.reshape(128, 8, NY), ('shot', 'dom'), 0, 0, tiled=True)  9.15 us
    pallas_call x1, Pallas kernels, body(): pl.pallas_call(prepare_kernel, out_shape=(*(shape(planes, NZ, NY),) * 2,...  7.81 us
    all_to_all x1, starting transfers between devices, body(): lax.all_to_all(outgoing.reshape(16, 24, NY), 'dom', 0, 0, tiled=True)  6.46 us
  transfers between devices with their start and end apart: 6, of which 3 were waited for; matrix products, arithmetic and copies ran while one was open for 0% of the time, Pallas kernels for 29%

profile of v6, /device:TPU:1, one launch (start us, length us, event | category | flops | bytes accessed | tf_op | source)
XLA Modules:
  0.0 97.2 jit_solution(10301373560146788014)
XLA Ops:
  0.0 2.5 %edges.1 = (f32[68,32,128]{2,1,0:T(8,128)}, f32[68,32,128]{2,1,0:T(8,128)}) custom-call(f32[2,32,32,128]{3,2,1,0:T(8,128)} %now.3, f32[2,32,32,128]{3,2,1,0:T(8,128)} %prev.1, f32[32,32,128]{2,1,0:T(8,128)} %vel.3), custom_call_target="tpu_custom_call" | custom-call | tf_op jit(solution)/shard_map/edges/pallas_call | solution.py:545
  2.5 4.6 %collective-permute-start = (f32[68,32,128]{2,1,0:T(8,128)}, f32[68,32,128]{2,1,0:T(8,128)S(1)}, u32[]{:S(2)}, u32[]{:S(2)}) collective-permute-start(f32[68,32,128]{2,1,0:T(8,128)} %get-tuple-element.24), channel_id=1, source_target_pairs={{0,1},{1,2},{2,3},{3,4},{4,5},{5,6},{6,7},{7,8},{8,9},{9,10},{10,1... | collective-permute-start | bytes 3342344 | tf_op jit(solution)/shard_map/ppermute | solution.py:525
  7.1 1.9 %collective-permute-start.1 = (f32[68,32,128]{2,1,0:T(8,128)}, f32[68,32,128]{2,1,0:T(8,128)S(1)}, u32[]{:S(2)}, u32[]{:S(2)}) collective-permute-start(f32[68,32,128]{2,1,0:T(8,128)} %get-tuple-element.25), channel_id=1, source_target_pairs={{1,0},{2,1},{3,2},{4,3},{5,4},{6,5},{7,6},{8,7},{9,8},{10,9},{11,1... | collective-permute-start | bytes 3342344 | tf_op jit(solution)/shard_map/ppermute | solution.py:525
  9.1 7.8 %prepare.1 = (f32[56,32,128]{2,1,0:T(8,128)}, f32[56,32,128]{2,1,0:T(8,128)}, f32[128,128]{1,0:T(8,128)}, s32[2,264]{1,0:T(2,128)}, s32[2]{0:T(128)}, /*index=5*...) custom-call(s32[2,256]{1,0:T(2,128)} %rec.1, s32[2,8]{1,0:T(2,128)} %src.1, f32[2,32,32,128]{3,2,1,0:T(8,128)} %now.5, ...), custom_call_target="tpu_custom_call" | custom-call | tf_op jit(solution)/shard_map/prepare/pallas_call | solution.py:559
  16.9 3.6 %collective-permute-start.2 = (f32[56,32,128]{2,1,0:T(8,128)}, f32[56,32,128]{2,1,0:T(8,128)S(1)}, u32[]{:S(2)}, u32[]{:S(2)}) collective-permute-start(f32[56,32,128]{2,1,0:T(8,128)} %get-tuple-element.35), channel_id=1, source_target_pairs={{0,1},{1,2},{2,3},{3,4},{4,5},{5,6},{6,7},{7,8},{8,9},{9,10},{10,1... | collective-permute-start | bytes 2752520 | tf_op jit(solution)/shard_map/ppermute | solution.py:525
  20.5 1.9 %collective-permute-start.3 = (f32[56,32,128]{2,1,0:T(8,128)}, f32[56,32,128]{2,1,0:T(8,128)}, u32[]{:S(2)}, u32[]{:S(2)}) collective-permute-start(f32[56,32,128]{2,1,0:T(8,128)} %get-tuple-element.36), channel_id=1, source_target_pairs={{1,0},{2,1},{3,2},{4,3},{5,4},{6,5},{7,6},{8,7},{9,8},{10,9},{11,1... | collective-permute-start | bytes 2752520 | tf_op jit(solution)/shard_map/ppermute | solution.py:525
  22.5 0.0 collective-permute-done.low
  22.5 1.7 %collective-permute-done.1.high = f32[68,32,128]{2,1,0:T(8,128)S(1)} collective-permute-done((f32[68,32,128]{2,1,0:T(8,128)}, f32[68,32,128]{2,1,0:T(8,128)S(1)}, u32[]{:S(2)}, u32[]{:S(2)}) %collective-permute-start.1) | collective-permute-done | bytes 1114144 | tf_op jit(solution)/shard_map/ppermute | solution.py:525
  24.2 11.6 %forward_steps.1 = (f32[4,2,32,32,128]{4,3,2,1,0:T(8,128)}, f32[384,128]{1,0:T(8,128)}, f32[64,32,128]{2,1,0:T(8,128)}) custom-call(s32[2,264]{1,0:T(2,128)} %get-tuple-element.27.entries.own, s32[2]{0:T(128)} %get-tuple-element.28.counts.own_count, s32[2,16]{1,0:T(2,128)} %get-tuple-element.31.src, s32[2]{0:T(128)} %get-tuple-element.32.src_counts, ...), custom_call_target="tpu_custom_call" | custom-call | tf_op jit(solution)/shard_map/forward_steps/pallas_call | solution.py:585
  35.7 6.5 %all-to-all-start = ((f32[16,24,128]{2,1,0:T(8,128)}), f32[16,24,128]{2,1,0:T(8,128)S(1)}, u32[]{:S(2)}, u32[]{:S(2)}) async-start(f32[16,24,128]{2,1,0:T(8,128)} %bitcast.17), calls=%async_computation | async-start | bytes 393216 | tf_op jit(solution)/shard_map/all_to_all | solution.py:608
  42.2 0.0 collective-permute-done.2.low
  42.2 0.0 collective-permute-done.3.high
  42.2 5.6 %adjoint_start.1 = (f32[2,64,32,128]{3,2,1,0:T(8,128)}, f32[4,8,32,128]{3,2,1,0:T(8,128)}) custom-call(f32[2,32,32,128]{3,2,1,0:T(8,128)} %now.5, f32[2,32,32,128]{3,2,1,0:T(8,128)} %after.1, f32[64,32,128]{2,1,0:T(8,128)} %get-tuple-element.34.speed_in, f32[56,32,128]{2,1,0:T(8,128)S(1)} %collective-permute-done.2.low, ...), custom_call_target="tpu_custom_call" | custom-call | tf_op jit(solution)/shard_map/adjoint_start/pallas_call | solution.py:611
  47.9 1.0 %all-to-all-done = f32[16,24,128]{2,1,0:T(8,128)S(1)} async-done(((f32[16,24,128]{2,1,0:T(8,128)}), f32[16,24,128]{2,1,0:T(8,128)S(1)}, u32[]{:S(2)}, u32[]{:S(2)}) %all-to-all-start) | async-done | bytes 196640 | tf_op jit(solution)/shard_map/all_to_all | solution.py:608
  48.9 10.8 %adjoint_steps.1 = f32[1024,128]{1,0:T(8,128)} custom-call(s32[2,264]{1,0:T(2,128)} %get-tuple-element.27.entries.own, s32[2]{0:T(128)} %get-tuple-element.28.counts.own_count, s32[2,264]{1,0:T(2,128)} %get-tuple-element.29.beyond, s32[2]{0:T(128)} %get-tuple-element.30.beyond_count, f32[2,64,32,128]{3,2,1,0:T(8,128)} %get-tuple-element.37.earlier, ...), custom_call_target="tpu_custom_call" | custom-call | tf_op jit(solution)/shard_map/adjoint_steps/pallas_call | solution.py:620
  59.7 9.1 %all-to-all-start.1 = ((f32[128,8,128]{2,1,0:T(8,128)}), f32[128,8,128]{2,1,0:T(8,128)S(1)}, u32[]{:S(2)}, u32[]{:S(2)}) async-start(f32[128,8,128]{2,1,0:T(8,128)} %bitcast.13), calls=%async_computation.1 | async-start | bytes 1048576 | tf_op jit(solution)/shard_map/all_to_all | solution.py:651
  68.9 0.0 copy-start
  69.6 2.7 %noise_prior.1 = (f32[128,128]{1,0:T(8,128)}, f32[128,128]{1,0:T(8,128)}) custom-call(f32[1]{0:T(128)S(6)} %copy.16.step_size, f32[384,128]{1,0:T(8,128)S(1)} %bitcast.11, bf16[2,512,512]{2,1,0:T(8,128)(2,1)} %constant.8.clone.operators, f32[1024,128]{1,0:T(8,128)} %bitcast.12), custom_call_target="tpu_custom_call" | custom-call | tf_op jit(solution)/shard_map/noise_prior/pallas_call | solution.py:642
  72.3 10.1 %all-to-all-done.1 = f32[128,8,128]{2,1,0:T(8,128)S(1)} async-done(((f32[128,8,128]{2,1,0:T(8,128)}), f32[128,8,128]{2,1,0:T(8,128)S(1)}, u32[]{:S(2)}, u32[]{:S(2)}) %all-to-all-start.1) | async-done | bytes 524320 | tf_op jit(solution)/shard_map/all_to_all | solution.py:651
  82.4 0.0 copy-done
  82.4 2.2 %prior.1 = f32[128,128]{1,0:T(8,128)} custom-call(f32[1]{0:T(128)S(6)} %copy.16.step_size, f32[1024,128]{1,0:T(8,128)S(1)} %bitcast.9, f32[128,128]{1,0:T(8,128)} %get-tuple-element.41.noise, bf16[2,512,512]{2,1,0:T(8,128)(2,1)S(1)} %copy-done), custom_call_target="tpu_custom_call" | custom-call | tf_op jit(solution)/shard_map/prior/pallas_call | solution.py:652
  84.6 10.9 %all_to_all.15 = f32[16,8,128]{2,1,0:T(8,128)} all-to-all(f32[16,8,128]{2,1,0:T(8,128)} %bitcast.15), channel_id=1, replica_groups=mesh['shot'=8,'dom'=16] {'dom'}, dimensions={0} | all-to-all | bytes 131072 | tf_op jit(solution)/shard_map/all_to_all | solution.py:659
  95.5 1.7 %finish.1 = f32[32,16,32]{2,1,0:T(8,128)} custom-call(f32[128,128]{1,0:T(8,128)} %bitcast.16, f32[128,128]{1,0:T(8,128)} %get-tuple-element.42.velocity), custom_call_target="tpu_custom_call" | custom-call | tf_op jit(solution)/shard_map/finish/pallas_call | solution.py:660
Async XLA Ops:
  2.5 19.9 %collective-permute-start = (f32[68,32,128]{2,1,0:T(8,128)}, f32[68,32,128]{2,1,0:T(8,128)S(1)}, u32[]{:S(2)}, u32[]{:S(2)}) collective-permute-start(f32[68,32,128]{2,1,0:T(8,128)} %get-tuple-element.24), channel_id=1, source_target_pairs={{0,1},{1,2},{2,3},{3,4},{4,5},{5,6},{6,7},{7,8},{8,9},{9,10},{10,1... | collective-permute-start | bytes 3342344 | tf_op jit(solution)/shard_map/ppermute | solution.py:525
  7.1 17.0 %collective-permute-start.1 = (f32[68,32,128]{2,1,0:T(8,128)}, f32[68,32,128]{2,1,0:T(8,128)S(1)}, u32[]{:S(2)}, u32[]{:S(2)}) collective-permute-start(f32[68,32,128]{2,1,0:T(8,128)} %get-tuple-element.25), channel_id=1, source_target_pairs={{1,0},{2,1},{3,2},{4,3},{5,4},{6,5},{7,6},{8,7},{9,8},{10,9},{11,1... | collective-permute-start | bytes 3342344 | tf_op jit(solution)/shard_map/ppermute | solution.py:525
  16.9 25.3 %collective-permute-start.2 = (f32[56,32,128]{2,1,0:T(8,128)}, f32[56,32,128]{2,1,0:T(8,128)S(1)}, u32[]{:S(2)}, u32[]{:S(2)}) collective-permute-start(f32[56,32,128]{2,1,0:T(8,128)} %get-tuple-element.35), channel_id=1, source_target_pairs={{0,1},{1,2},{2,3},{3,4},{4,5},{5,6},{6,7},{7,8},{8,9},{9,10},{10,1... | collective-permute-start | bytes 2752520 | tf_op jit(solution)/shard_map/ppermute | solution.py:525
  20.5 21.7 %collective-permute-start.3 = (f32[56,32,128]{2,1,0:T(8,128)}, f32[56,32,128]{2,1,0:T(8,128)}, u32[]{:S(2)}, u32[]{:S(2)}) collective-permute-start(f32[56,32,128]{2,1,0:T(8,128)} %get-tuple-element.36), channel_id=1, source_target_pairs={{1,0},{2,1},{3,2},{4,3},{5,4},{6,5},{7,6},{8,7},{9,8},{10,9},{11,1... | collective-permute-start | bytes 2752520 | tf_op jit(solution)/shard_map/ppermute | solution.py:525
  35.7 13.1 %all-to-all-start = ((f32[16,24,128]{2,1,0:T(8,128)}), f32[16,24,128]{2,1,0:T(8,128)S(1)}, u32[]{:S(2)}, u32[]{:S(2)}) async-start(f32[16,24,128]{2,1,0:T(8,128)} %bitcast.17), calls=%async_computation | async-start | bytes 393216 | tf_op jit(solution)/shard_map/all_to_all | solution.py:608
  59.7 22.7 %all-to-all-start.1 = ((f32[128,8,128]{2,1,0:T(8,128)}), f32[128,8,128]{2,1,0:T(8,128)S(1)}, u32[]{:S(2)}, u32[]{:S(2)}) async-start(f32[128,8,128]{2,1,0:T(8,128)} %bitcast.13), calls=%async_computation.1 | async-start | bytes 1048576 | tf_op jit(solution)/shard_map/all_to_all | solution.py:651
  68.9 13.5 %copy-start = (bf16[2,512,512]{2,1,0:T(8,128)(2,1)S(1)}, bf16[2,512,512]{2,1,0:T(8,128)(2,1)}, u32[]{:S(2)}) copy-start(bf16[2,512,512]{2,1,0:T(8,128)(2,1)} %constant.7.clone.operators) | copy-start | bytes 3145732

commit v7 on v6

--- a/solution.py
+++ b/solution.py
@@ -276,7 +276,7 @@
     begin = SHOTS_HERE * (DEEP + SHALLOW)
     square_rows(low, begin, speed, DEEP - SHALLOW, SHALLOW)
     square_rows(high, begin, speed, DEEP + SLAB, SHALLOW)
-    clear_pads(fields[1 : STEPS + 1])
+    clear_pads(fields[1:2])
     for copy in copies[:2]:
         copy.wait()
     ids = lane_ids()
@@ -285,6 +285,7 @@
         margin = 4 * (STEPS - 1 - moment)
         along_lanes(fields[moment + 1], lanes, along, margin)
         if moment == 0:
+            clear_pads(fields[2 : STEPS + 1])
             for copy in copies[2:]:
                 copy.wait()
             square_rows(speed, DEEP, speed, DEEP, SLAB)

time: 97.9 us -> 98 us (level)
  no operation moved by 1% of the time
where the time goes in v7:
time: 98 us; the launch traced here: 97.2 us
  Pallas kernels  44.9 us (46%)
  starting transfers between devices  27.7 us (28%)
  waiting for transfers between devices  12.8 us (13%)
  blocking collectives  10.9 us (11%)
    ppermute x4, starting transfers between devices, exchange(): return (lax.ppermute(to_high, axis, up), lax.ppermute(to_low, axis, down))  12.1 us
    pallas_call x1, Pallas kernels, body(): pl.pallas_call(forward_kernel, out_shape=(shape(STEPS, SHOTS_HERE, SLAB,...  11.9 us
    all_to_all x1, blocking collectives, body(): lax.all_to_all(update.reshape(16, 8, NY), 'dom', 0, 0, tiled=True)  10.9 us
    pallas_call x1, Pallas kernels, body(): pl.pallas_call(adjoint_kernel, out_shape=shape(SLAB * NZ, NY), in_specs=[...  10.5 us
    all_to_all x1, waiting for transfers between devices, body(): lax.all_to_all(tiles.reshape(128, 8, NY), ('shot', 'dom'), 0, 0, tiled=True)  10.1 us
    all_to_all x1, starting transfers between devices, body(): lax.all_to_all(tiles.reshape(128, 8, NY), ('shot', 'dom'), 0, 0, tiled=True)  9.22 us
    pallas_call x1, Pallas kernels, body(): pl.pallas_call(prepare_kernel, out_shape=(*(shape(planes, NZ, NY),) * 2,...  7.81 us
    all_to_all x1, starting transfers between devices, body(): lax.all_to_all(outgoing.reshape(16, 24, NY), 'dom', 0, 0, tiled=True)  6.35 us
  transfers between devices with their start and end apart: 6, of which 3 were waited for; matrix products, arithmetic and copies ran while one was open for 0% of the time, Pallas kernels for 29%

profile of v7, /device:TPU:1, one launch (start us, length us, event | category | flops | bytes accessed | tf_op | source)
XLA Modules:
  0.0 97.2 jit_solution(1694834768563124907)
XLA Ops:
  0.0 2.5 %edges.1 = (f32[68,32,128]{2,1,0:T(8,128)}, f32[68,32,128]{2,1,0:T(8,128)}) custom-call(f32[2,32,32,128]{3,2,1,0:T(8,128)} %now.3, f32[2,32,32,128]{3,2,1,0:T(8,128)} %prev.1, f32[32,32,128]{2,1,0:T(8,128)} %vel.3), custom_call_target="tpu_custom_call" | custom-call | tf_op jit(solution)/shard_map/edges/pallas_call | solution.py:546
  2.5 4.6 %collective-permute-start = (f32[68,32,128]{2,1,0:T(8,128)}, f32[68,32,128]{2,1,0:T(8,128)S(1)}, u32[]{:S(2)}, u32[]{:S(2)}) collective-permute-start(f32[68,32,128]{2,1,0:T(8,128)} %get-tuple-element.24), channel_id=1, source_target_pairs={{0,1},{1,2},{2,3},{3,4},{4,5},{5,6},{6,7},{7,8},{8,9},{9,10},{10,1... | collective-permute-start | bytes 3342344 | tf_op jit(solution)/shard_map/ppermute | solution.py:526
  7.1 1.9 %collective-permute-start.1 = (f32[68,32,128]{2,1,0:T(8,128)}, f32[68,32,128]{2,1,0:T(8,128)S(1)}, u32[]{:S(2)}, u32[]{:S(2)}) collective-permute-start(f32[68,32,128]{2,1,0:T(8,128)} %get-tuple-element.25), channel_id=1, source_target_pairs={{1,0},{2,1},{3,2},{4,3},{5,4},{6,5},{7,6},{8,7},{9,8},{10,9},{11,1... | collective-permute-start | bytes 3342344 | tf_op jit(solution)/shard_map/ppermute | solution.py:526
  9.1 7.8 %prepare.1 = (f32[56,32,128]{2,1,0:T(8,128)}, f32[56,32,128]{2,1,0:T(8,128)}, f32[128,128]{1,0:T(8,128)}, s32[2,264]{1,0:T(2,128)}, s32[2]{0:T(128)}, /*index=5*...) custom-call(s32[2,256]{1,0:T(2,128)} %rec.1, s32[2,8]{1,0:T(2,128)} %src.1, f32[2,32,32,128]{3,2,1,0:T(8,128)} %now.5, ...), custom_call_target="tpu_custom_call" | custom-call | tf_op jit(solution)/shard_map/prepare/pallas_call | solution.py:560
  16.9 3.6 %collective-permute-start.2 = (f32[56,32,128]{2,1,0:T(8,128)}, f32[56,32,128]{2,1,0:T(8,128)S(1)}, u32[]{:S(2)}, u32[]{:S(2)}) collective-permute-start(f32[56,32,128]{2,1,0:T(8,128)} %get-tuple-element.35), channel_id=1, source_target_pairs={{0,1},{1,2},{2,3},{3,4},{4,5},{5,6},{6,7},{7,8},{8,9},{9,10},{10,1... | collective-permute-start | bytes 2752520 | tf_op jit(solution)/shard_map/ppermute | solution.py:526
  20.5 1.9 %collective-permute-start.3 = (f32[56,32,128]{2,1,0:T(8,128)}, f32[56,32,128]{2,1,0:T(8,128)}, u32[]{:S(2)}, u32[]{:S(2)}) collective-permute-start(f32[56,32,128]{2,1,0:T(8,128)} %get-tuple-element.36), channel_id=1, source_target_pairs={{1,0},{2,1},{3,2},{4,3},{5,4},{6,5},{7,6},{8,7},{9,8},{10,9},{11,1... | collective-permute-start | bytes 2752520 | tf_op jit(solution)/shard_map/ppermute | solution.py:526
  22.5 0.0 collective-permute-done.low
  22.5 1.7 %collective-permute-done.1.high = f32[68,32,128]{2,1,0:T(8,128)S(1)} collective-permute-done((f32[68,32,128]{2,1,0:T(8,128)}, f32[68,32,128]{2,1,0:T(8,128)S(1)}, u32[]{:S(2)}, u32[]{:S(2)}) %collective-permute-start.1) | collective-permute-done | bytes 1114144 | tf_op jit(solution)/shard_map/ppermute | solution.py:526
  24.2 11.9 %forward_steps.1 = (f32[4,2,32,32,128]{4,3,2,1,0:T(8,128)}, f32[384,128]{1,0:T(8,128)}, f32[64,32,128]{2,1,0:T(8,128)}) custom-call(s32[2,264]{1,0:T(2,128)} %get-tuple-element.27.entries.own, s32[2]{0:T(128)} %get-tuple-element.28.counts.own_count, s32[2,16]{1,0:T(2,128)} %get-tuple-element.31.src, s32[2]{0:T(128)} %get-tuple-element.32.src_counts, ...), custom_call_target="tpu_custom_call" | custom-call | tf_op jit(solution)/shard_map/forward_steps/pallas_call | solution.py:586
  36.0 6.4 %all-to-all-start = ((f32[16,24,128]{2,1,0:T(8,128)}), f32[16,24,128]{2,1,0:T(8,128)S(1)}, u32[]{:S(2)}, u32[]{:S(2)}) async-start(f32[16,24,128]{2,1,0:T(8,128)} %bitcast.17), calls=%async_computation | async-start | bytes 393216 | tf_op jit(solution)/shard_map/all_to_all | solution.py:609
  42.4 0.0 collective-permute-done.2.low
  42.4 0.0 collective-permute-done.3.high
  42.4 5.6 %adjoint_start.1 = (f32[2,64,32,128]{3,2,1,0:T(8,128)}, f32[4,8,32,128]{3,2,1,0:T(8,128)}) custom-call(f32[2,32,32,128]{3,2,1,0:T(8,128)} %now.5, f32[2,32,32,128]{3,2,1,0:T(8,128)} %after.1, f32[64,32,128]{2,1,0:T(8,128)} %get-tuple-element.34.speed_in, f32[56,32,128]{2,1,0:T(8,128)S(1)} %collective-permute-done.2.low, ...), custom_call_target="tpu_custom_call" | custom-call | tf_op jit(solution)/shard_map/adjoint_start/pallas_call | solution.py:612
  48.0 1.0 %all-to-all-done = f32[16,24,128]{2,1,0:T(8,128)S(1)} async-done(((f32[16,24,128]{2,1,0:T(8,128)}), f32[16,24,128]{2,1,0:T(8,128)S(1)}, u32[]{:S(2)}, u32[]{:S(2)}) %all-to-all-start) | async-done | bytes 196640 | tf_op jit(solution)/shard_map/all_to_all | solution.py:609
  49.0 10.5 %adjoint_steps.1 = f32[1024,128]{1,0:T(8,128)} custom-call(s32[2,264]{1,0:T(2,128)} %get-tuple-element.27.entries.own, s32[2]{0:T(128)} %get-tuple-element.28.counts.own_count, s32[2,264]{1,0:T(2,128)} %get-tuple-element.29.beyond, s32[2]{0:T(128)} %get-tuple-element.30.beyond_count, f32[2,64,32,128]{3,2,1,0:T(8,128)} %get-tuple-element.37.earlier, ...), custom_call_target="tpu_custom_call" | custom-call | tf_op jit(solution)/shard_map/adjoint_steps/pallas_call | solution.py:621
  59.6 9.2 %all-to-all-start.1 = ((f32[128,8,128]{2,1,0:T(8,128)}), f32[128,8,128]{2,1,0:T(8,128)S(1)}, u32[]{:S(2)}, u32[]{:S(2)}) async-start(f32[128,8,128]{2,1,0:T(8,128)} %bitcast.13), calls=%async_computation.1 | async-start | bytes 1048576 | tf_op jit(solution)/shard_map/all_to_all | solution.py:652
  68.8 0.0 copy-start
  69.6 2.7 %noise_prior.1 = (f32[128,128]{1,0:T(8,128)}, f32[128,128]{1,0:T(8,128)}) custom-call(f32[1]{0:T(128)S(6)} %copy.16.step_size, f32[384,128]{1,0:T(8,128)S(1)} %bitcast.11, bf16[2,512,512]{2,1,0:T(8,128)(2,1)} %constant.8.clone.operators, f32[1024,128]{1,0:T(8,128)} %bitcast.12), custom_call_target="tpu_custom_call" | custom-call | tf_op jit(solution)/shard_map/noise_prior/pallas_call | solution.py:643
  72.3 10.1 %all-to-all-done.1 = f32[128,8,128]{2,1,0:T(8,128)S(1)} async-done(((f32[128,8,128]{2,1,0:T(8,128)}), f32[128,8,128]{2,1,0:T(8,128)S(1)}, u32[]{:S(2)}, u32[]{:S(2)}) %all-to-all-start.1) | async-done | bytes 524320 | tf_op jit(solution)/shard_map/all_to_all | solution.py:652
  82.3 0.0 copy-done
  82.3 2.2 %prior.1 = f32[128,128]{1,0:T(8,128)} custom-call(f32[1]{0:T(128)S(6)} %copy.16.step_size, f32[1024,128]{1,0:T(8,128)S(1)} %bitcast.9, f32[128,128]{1,0:T(8,128)} %get-tuple-element.41.noise, bf16[2,512,512]{2,1,0:T(8,128)(2,1)S(1)} %copy-done), custom_call_target="tpu_custom_call" | custom-call | tf_op jit(solution)/shard_map/prior/pallas_call | solution.py:653
  84.5 10.9 %all_to_all.15 = f32[16,8,128]{2,1,0:T(8,128)} all-to-all(f32[16,8,128]{2,1,0:T(8,128)} %bitcast.15), channel_id=1, replica_groups=mesh['shot'=8,'dom'=16] {'dom'}, dimensions={0} | all-to-all | bytes 131072 | tf_op jit(solution)/shard_map/all_to_all | solution.py:660
  95.5 1.7 %finish.1 = f32[32,16,32]{2,1,0:T(8,128)} custom-call(f32[128,128]{1,0:T(8,128)} %bitcast.16, f32[128,128]{1,0:T(8,128)} %get-tuple-element.42.velocity), custom_call_target="tpu_custom_call" | custom-call | tf_op jit(solution)/shard_map/finish/pallas_call | solution.py:661
Async XLA Ops:
  2.5 19.9 %collective-permute-start = (f32[68,32,128]{2,1,0:T(8,128)}, f32[68,32,128]{2,1,0:T(8,128)S(1)}, u32[]{:S(2)}, u32[]{:S(2)}) collective-permute-start(f32[68,32,128]{2,1,0:T(8,128)} %get-tuple-element.24), channel_id=1, source_target_pairs={{0,1},{1,2},{2,3},{3,4},{4,5},{5,6},{6,7},{7,8},{8,9},{9,10},{10,1... | collective-permute-start | bytes 3342344 | tf_op jit(solution)/shard_map/ppermute | solution.py:526
  7.1 17.0 %collective-permute-start.1 = (f32[68,32,128]{2,1,0:T(8,128)}, f32[68,32,128]{2,1,0:T(8,128)S(1)}, u32[]{:S(2)}, u32[]{:S(2)}) collective-permute-start(f32[68,32,128]{2,1,0:T(8,128)} %get-tuple-element.25), channel_id=1, source_target_pairs={{1,0},{2,1},{3,2},{4,3},{5,4},{6,5},{7,6},{8,7},{9,8},{10,9},{11,1... | collective-permute-start | bytes 3342344 | tf_op jit(solution)/shard_map/ppermute | solution.py:526
  16.9 25.5 %collective-permute-start.2 = (f32[56,32,128]{2,1,0:T(8,128)}, f32[56,32,128]{2,1,0:T(8,128)S(1)}, u32[]{:S(2)}, u32[]{:S(2)}) collective-permute-start(f32[56,32,128]{2,1,0:T(8,128)} %get-tuple-element.35), channel_id=1, source_target_pairs={{0,1},{1,2},{2,3},{3,4},{4,5},{5,6},{6,7},{7,8},{8,9},{9,10},{10,1... | collective-permute-start | bytes 2752520 | tf_op jit(solution)/shard_map/ppermute | solution.py:526
  20.5 21.9 %collective-permute-start.3 = (f32[56,32,128]{2,1,0:T(8,128)}, f32[56,32,128]{2,1,0:T(8,128)}, u32[]{:S(2)}, u32[]{:S(2)}) collective-permute-start(f32[56,32,128]{2,1,0:T(8,128)} %get-tuple-element.36), channel_id=1, source_target_pairs={{1,0},{2,1},{3,2},{4,3},{5,4},{6,5},{7,6},{8,7},{9,8},{10,9},{11,1... | collective-permute-start | bytes 2752520 | tf_op jit(solution)/shard_map/ppermute | solution.py:526
  36.0 13.0 %all-to-all-start = ((f32[16,24,128]{2,1,0:T(8,128)}), f32[16,24,128]{2,1,0:T(8,128)S(1)}, u32[]{:S(2)}, u32[]{:S(2)}) async-start(f32[16,24,128]{2,1,0:T(8,128)} %bitcast.17), calls=%async_computation | async-start | bytes 393216 | tf_op jit(solution)/shard_map/all_to_all | solution.py:609
  59.6 22.8 %all-to-all-start.1 = ((f32[128,8,128]{2,1,0:T(8,128)}), f32[128,8,128]{2,1,0:T(8,128)S(1)}, u32[]{:S(2)}, u32[]{:S(2)}) async-start(f32[128,8,128]{2,1,0:T(8,128)} %bitcast.13), calls=%async_computation.1 | async-start | bytes 1048576 | tf_op jit(solution)/shard_map/all_to_all | solution.py:652
  68.8 13.5 %copy-start = (bf16[2,512,512]{2,1,0:T(8,128)(2,1)S(1)}, bf16[2,512,512]{2,1,0:T(8,128)(2,1)}, u32[]{:S(2)}) copy-start(bf16[2,512,512]{2,1,0:T(8,128)(2,1)} %constant.7.clone.operators) | copy-start | bytes 3145732
